TPU v7x, 32 devices: a whole 2x2x4 slice. The times are simulated.
32 devices in a mesh: dp: 4 (over y, x), expert: 8 (over z, core).
Axes of the slice: x: 2, y: 2, z: 4, core: 2. Of those that a mesh axis runs over, the one named last changes fastest.
Arguments:
- tokens: bfloat16 [32768, 768], P(('dp', 'expert')), may hold values from -6 to 6
- gain_one: float32 [768], replicated, may hold values from 0.25 to 1.75
- query_w: bfloat16 [768, 768], replicated, may hold values from -0.109375 to 0.109375
- key_w: bfloat16 [768, 768], replicated, may hold values from -0.109375 to 0.109375
- value_w: bfloat16 [768, 768], replicated, may hold values from -0.21875 to 0.21875
- out_w: bfloat16 [768, 768], replicated, may hold values from -0.625 to 0.625
- rel_table: float32 [32, 12], replicated, may hold values from -4 to 4
- gain_two: float32 [768], replicated, may hold values from 0.25 to 1.75
- router_w: bfloat16 [768, 8], replicated, may hold values from -0.15625 to 0.15625
- expert_in: bfloat16 [8, 768, 3072], P('expert'), may hold values from -0.21875 to 0.21875
- expert_out: bfloat16 [8, 3072, 768], P('expert'), may hold values from -0.875 to 0.875
- routes: int32 [32768, 1], P(('dp', 'expert')), may hold values from 0 to 7
- buckets: int32 [2047], replicated, may hold values from 0 to 31, as said below
- cotangent: bfloat16 [32768, 768], P(('dp', 'expert')), may hold values from -6 to 6
Outputs:
- output: bfloat16 [32768, 768], P(('dp', 'expert'))
- input_grad: float32 [32768, 768], P(('dp', 'expert'))
- query_grad: float32 [768, 768], replicated
- key_grad: float32 [768, 768], replicated
- value_grad: float32 [768, 768], replicated
- out_grad: float32 [768, 768], replicated
- rel_grad: float32 [32, 12], replicated
- gain_one_grad: float32 [768], replicated
- gain_two_grad: float32 [768], replicated
- router_grad: float32 [768, 8], replicated
- expert_in_grad: float32 [8, 768, 3072], P('expert', 'dp')
- expert_out_grad: float32 [8, 3072, 768], P('expert', None, 'dp')
Inputs may be any that keep to these rules, and one draw needn't show every extreme that they name: buckets depends only on the distance |j - i| and on the sign of j - i, never falls as the distance grows on either side, is below 16 for j - i <= 0 and 16 or more for j - i > 0.
All inputs are finite; a program needn't handle non-finite values.
Results may differ from a plain program's by a relative error of at most 0.015.
The roundings to bfloat16 on the way count: a program that leaves them out, or rounds other values in their place, can miss the bound.
Values may be sent and summed in bfloat16 or wider, within the bound.
A program may use at most 448 MiB of HBM per device.

v0:
```python
import jax
import jax.numpy as jnp
from jax import lax
from jax.sharding import PartitionSpec as P

epsilon = 1e-06
highest = lax.Precision.HIGHEST


def rms_forward(values, gain_vec):
    row_scale = lax.rsqrt(jnp.mean(values * values, axis=-1, keepdims=True) + epsilon)
    return (values * row_scale * gain_vec, row_scale)


def rms_backward(grad_norm, values, row_scale, gain_vec):
    weighted = grad_norm * gain_vec
    gain_grad = jnp.sum(grad_norm * values * row_scale, axis=0)
    grad_in = row_scale * weighted - values * row_scale**3 * jnp.mean(
        weighted * values, axis=-1, keepdims=True
    )
    return (grad_in, gain_grad)


def gelu_tanh(values):
    return jax.nn.gelu(values, approximate=True)


def window_start(row_start, block_rows, seq_len):
    return seq_len - row_start - block_rows


def bias_block(bias_heads, row_start, block_rows, seq_len):
    head_count = bias_heads.shape[0]
    width = seq_len + block_rows - 1
    first = window_start(row_start, block_rows, seq_len)
    window = bias_heads[:, first : first + width]
    flat = jnp.tile(window, (1, block_rows))
    flat = flat[:, block_rows - 1 : block_rows - 1 + block_rows * (width - 1)]
    return flat.reshape(head_count, block_rows, width - 1)[:, :, :seq_len]


def diagonal_sums(score_grad, block_rows, seq_len):
    head_count = score_grad.shape[0]
    width = seq_len + block_rows - 1
    padded = jnp.pad(score_grad, ((0, 0), (0, 0), (0, width - 1 - seq_len)))
    flat = padded.reshape(head_count, block_rows * (width - 1))
    flat = jnp.pad(flat, ((0, 0), (block_rows - 1, 1)))
    return jnp.sum(flat.reshape(head_count, block_rows, width), axis=1)


def project(left, right):
    return jnp.dot(left, right, preferred_element_type=jnp.float32)


def project_left(left, right):
    return jnp.einsum("td,te->de", left, right, preferred_element_type=jnp.float32)


def project_right(left, right):
    return jnp.einsum("te,de->td", left, right, preferred_element_type=jnp.float32)


def on_device(
    tokens,
    gain_one,
    query_w,
    key_w,
    value_w,
    out_w,
    rel_table,
    gain_two,
    router_w,
    expert_in,
    expert_out,
    routes,
    buckets,
    cotangent,
):
    seq_len, model_width = tokens.shape
    head_count = rel_table.shape[1]
    head_dim = model_width // head_count
    experts = lax.axis_size("expert")
    capacity = (5 * seq_len + 4 * experts - 1) // (4 * experts)
    block_rows = min(512, seq_len)
    block_count = seq_len // block_rows
    trash_slot = experts * capacity
    width = seq_len + block_rows - 1
    tokens_f = tokens.astype(jnp.float32)
    normed, scale_one = rms_forward(tokens_f, gain_one)
    normed_low = normed.astype(jnp.bfloat16)
    queries = project(normed_low, query_w).astype(jnp.bfloat16)
    key_rows = project(normed_low, key_w).astype(jnp.bfloat16)
    value_rows = project(normed_low, value_w).astype(jnp.bfloat16)
    query_heads = queries.reshape(seq_len, head_count, head_dim)
    key_heads = key_rows.reshape(seq_len, head_count, head_dim)
    value_heads = value_rows.reshape(seq_len, head_count, head_dim)
    bucket_hot = (
        buckets[:, None] == jnp.arange(rel_table.shape[0], dtype=jnp.int32)[None, :]
    ).astype(jnp.float32)
    bias_heads = jnp.einsum("lb,bh->hl", bucket_hot, rel_table, precision=highest)
    context_parts = []
    logsum_parts = []
    for block_idx in range(block_count):
        row_start = block_idx * block_rows
        bias_now = bias_block(bias_heads, row_start, block_rows, seq_len)
        query_blk = query_heads[row_start : row_start + block_rows]
        scores = (
            jnp.einsum("qhd,khd->hqk", query_blk, key_heads, preferred_element_type=jnp.float32)
            + bias_now
        )
        row_max = jnp.max(scores, axis=-1, keepdims=True)
        exp_scores = jnp.exp(scores - row_max)
        row_total = jnp.sum(exp_scores, axis=-1, keepdims=True)
        att_weights = (exp_scores / row_total).astype(jnp.bfloat16)
        context_parts.append(
            jnp.einsum(
                "hqk,khd->qhd", att_weights, value_heads, preferred_element_type=jnp.float32
            ).astype(jnp.bfloat16)
        )
        logsum_parts.append(row_max + jnp.log(row_total))
    context = jnp.concatenate(context_parts, axis=0).reshape(seq_len, model_width)
    hidden = tokens_f + project(context, out_w)
    normed_two, scale_two = rms_forward(hidden, gain_two)
    normed_two_low = normed_two.astype(jnp.bfloat16)
    router_probs = jax.nn.softmax(project(normed_two_low, router_w), axis=-1)
    route_ids = routes[:, 0]
    route_hot = (route_ids[:, None] == jnp.arange(experts, dtype=jnp.int32)[None, :]).astype(
        jnp.int32
    )
    route_float = route_hot.astype(jnp.float32)
    position = jnp.sum((jnp.cumsum(route_hot, axis=0) - 1) * route_hot, axis=1)
    slot_index = jnp.where(position < capacity, route_ids * capacity + position, trash_slot)
    gate_value = jnp.sum(router_probs * route_float, axis=-1)
    send_rows = (
        jnp.zeros((trash_slot + 1, model_width), jnp.bfloat16).at[slot_index].set(normed_two_low)
    )
    send_rows = send_rows[:trash_slot].reshape(experts, capacity, model_width)
    weight_in = expert_in[0]
    weight_out = expert_out[0]
    received = lax.all_to_all(send_rows, "expert", split_axis=0, concat_axis=0, tiled=True)
    preact = jnp.einsum("scd,df->scf", received, weight_in, preferred_element_type=jnp.float32)
    active = gelu_tanh(preact).astype(jnp.bfloat16)
    produced = jnp.einsum(
        "scf,fd->scd", active, weight_out, preferred_element_type=jnp.float32
    ).astype(jnp.bfloat16)
    results = (received, preact, produced)
    received = results[0]
    produced = results[-1]
    returned = lax.all_to_all(produced, "expert", split_axis=0, concat_axis=0, tiled=True)
    padded = jnp.concatenate(
        [returned.reshape(trash_slot, model_width), jnp.zeros((1, model_width), jnp.bfloat16)],
        axis=0,
    )
    gathered = padded[slot_index].astype(jnp.float32)
    output = (hidden + gate_value[:, None] * gathered).astype(jnp.bfloat16)
    grad_out = cotangent.astype(jnp.float32)
    grad_gather = (grad_out * gate_value[:, None]).astype(jnp.bfloat16)
    gate_grad = jnp.sum(grad_out * gathered, axis=-1)
    grad_send = (
        jnp.zeros((trash_slot + 1, model_width), jnp.bfloat16).at[slot_index].set(grad_gather)
    )
    grad_send = grad_send[:trash_slot].reshape(experts, capacity, model_width)
    grad_produced = lax.all_to_all(grad_send, "expert", split_axis=0, concat_axis=0, tiled=True)
    preact_kept = results[1]
    gelu_values, gelu_pullback = jax.vjp(gelu_tanh, preact_kept)
    active = gelu_values.astype(jnp.bfloat16)
    grad_active = jnp.einsum(
        "scd,fd->scf", grad_produced, weight_out, preferred_element_type=jnp.float32
    )
    grad_preact = gelu_pullback(grad_active)[0].astype(jnp.bfloat16)
    grad_received = jnp.einsum(
        "scf,df->scd", grad_preact, weight_in, preferred_element_type=jnp.float32
    ).astype(jnp.bfloat16)
    grad_rows = lax.all_to_all(grad_received, "expert", split_axis=0, concat_axis=0, tiled=True)
    in_grad = jnp.einsum("scd,scf->df", received, grad_preact, preferred_element_type=jnp.float32)
    out_grad_local = jnp.einsum(
        "scf,scd->fd", active, grad_produced, preferred_element_type=jnp.float32
    )
    in_share, out_share = (
        lax.psum_scatter(
            in_grad.astype(jnp.bfloat16), "dp", scatter_dimension=0, tiled=True
        ).astype(jnp.float32),
        lax.psum_scatter(
            out_grad_local.astype(jnp.bfloat16), "dp", scatter_dimension=1, tiled=True
        ).astype(jnp.float32),
    )
    grad_padded = jnp.concatenate(
        [grad_rows.reshape(trash_slot, model_width), jnp.zeros((1, model_width), jnp.bfloat16)],
        axis=0,
    )
    grad_dispatched = grad_padded[slot_index].astype(jnp.float32)
    logit_low = ((gate_grad * gate_value)[:, None] * (route_float - router_probs)).astype(
        jnp.bfloat16
    )
    router_grad = project_left(normed_two_low, logit_low)
    grad_normed_two = project_right(logit_low, router_w) + grad_dispatched
    grad_hidden_norm, gain_two_grad = rms_backward(grad_normed_two, hidden, scale_two, gain_two)
    grad_hidden = grad_out + grad_hidden_norm
    branch_low = grad_hidden.astype(jnp.bfloat16)
    out_w_grad = project_left(context, branch_low)
    grad_context = (
        project_right(branch_low, out_w).astype(jnp.bfloat16).reshape(seq_len, head_count, head_dim)
    )
    key_grad_sum = jnp.zeros((seq_len, head_count, head_dim), jnp.float32)
    value_grad_sum = jnp.zeros((seq_len, head_count, head_dim), jnp.float32)
    offset_grad = jnp.zeros((head_count, 2 * seq_len - 1), jnp.float32)
    query_parts = []
    for block_idx in range(block_count):
        row_start = block_idx * block_rows
        bias_now = bias_block(bias_heads, row_start, block_rows, seq_len)
        query_blk = query_heads[row_start : row_start + block_rows]
        grad_ctx_blk = grad_context[row_start : row_start + block_rows]
        scores = (
            jnp.einsum("qhd,khd->hqk", query_blk, key_heads, preferred_element_type=jnp.float32)
            + bias_now
        )
        att_probs = jnp.exp(scores - logsum_parts[block_idx])
        att_low = att_probs.astype(jnp.bfloat16)
        value_grad_sum = value_grad_sum + jnp.einsum(
            "hqk,qhd->khd", att_low, grad_ctx_blk, preferred_element_type=jnp.float32
        )
        prob_grad = jnp.einsum(
            "qhd,khd->hqk", grad_ctx_blk, value_heads, preferred_element_type=jnp.float32
        )
        score_grad = att_probs * (
            prob_grad - jnp.sum(att_probs * prob_grad, axis=-1, keepdims=True)
        )
        first = window_start(row_start, block_rows, seq_len)
        offset_grad = offset_grad.at[:, first : first + width].add(
            diagonal_sums(score_grad, block_rows, seq_len)
        )
        score_low = score_grad.astype(jnp.bfloat16)
        query_parts.append(
            jnp.einsum(
                "hqk,khd->qhd", score_low, key_heads, preferred_element_type=jnp.float32
            ).astype(jnp.bfloat16)
        )
        key_grad_sum = key_grad_sum + jnp.einsum(
            "hqk,qhd->khd", score_low, query_blk, preferred_element_type=jnp.float32
        )
    query_grad_low = jnp.concatenate(query_parts, axis=0).reshape(seq_len, model_width)
    key_grad_low = key_grad_sum.astype(jnp.bfloat16).reshape(seq_len, model_width)
    value_grad_low = value_grad_sum.astype(jnp.bfloat16).reshape(seq_len, model_width)
    query_w_grad = project_left(normed_low, query_grad_low)
    key_w_grad = project_left(normed_low, key_grad_low)
    value_w_grad = project_left(normed_low, value_grad_low)
    grad_normed = (
        project_right(query_grad_low, query_w)
        + project_right(key_grad_low, key_w)
        + project_right(value_grad_low, value_w)
    )
    grad_tokens_norm, gain_one_grad = rms_backward(grad_normed, tokens_f, scale_one, gain_one)
    input_grad = grad_hidden + grad_tokens_norm
    rel_grad = jnp.einsum("lb,hl->bh", bucket_hot, offset_grad, precision=highest)
    (
        query_w_grad,
        key_w_grad,
        value_w_grad,
        out_w_grad,
        rel_grad,
        gain_one_grad,
        gain_two_grad,
        router_grad,
    ) = lax.psum(
        (
            query_w_grad,
            key_w_grad,
            value_w_grad,
            out_w_grad,
            rel_grad,
            gain_one_grad,
            gain_two_grad,
            router_grad,
        ),
        ("dp", "expert"),
    )
    return (
        output,
        input_grad,
        query_w_grad,
        key_w_grad,
        value_w_grad,
        out_w_grad,
        rel_grad,
        gain_one_grad,
        gain_two_grad,
        router_grad,
        in_share[None],
        out_share[None],
    )


def solution(mesh):
    return jax.shard_map(
        on_device,
        mesh=mesh,
        in_specs=(
            P(("dp", "expert"), None),
            P(),
            P(),
            P(),
            P(),
            P(),
            P(),
            P(),
            P(),
            P("expert", None, None),
            P("expert", None, None),
            P(("dp", "expert"), None),
            P(),
            P(("dp", "expert"), None),
        ),
        out_specs=(
            P(("dp", "expert"), None),
            P(("dp", "expert"), None),
            P(),
            P(),
            P(),
            P(),
            P(),
            P(),
            P(),
            P(),
            P("expert", "dp", None),
            P("expert", None, "dp"),
        ),
        check_vma=False,
    )
```

profile of v0, /device:TPU:1, one launch (start us, length us, event | category | flops | bytes accessed | tf_op | source)
XLA Modules:
  0.0 1548.7 jit_solution(11302961146978953554)
XLA Ops:
  28.0 12.7 tile.8
  40.7 61.7 %tile.9 = f32[12,785920]{1,0:T(8,128)} reshape(f32[12,512,1535]{2,1,0:T(8,128)} %tile.8) | data formatting | bytes 75448320 | tf_op jit(solution)/shard_map/tile | solution.py:37
  102.5 38.2 %slice.122 = f32[12,785408]{1,0:T(8,128)} slice(f32[12,785920]{1,0:T(8,128)} %tile.9), slice={[0:12], [511:785919]} | slice | bytes 75399168 | tf_op jit(solution)/shard_map/slice | solution.py:38
  140.7 90.3 %reshape.233 = f32[12,512,1534]{2,1,0:T(8,128)} reshape(f32[12,785408]{1,0:T(8,128)} %slice.122) | data formatting | bytes 75399168 | tf_op jit(solution)/shard_map/reshape | solution.py:39
  231.1 12.8 tile.10
  243.8 61.5 %tile.11 = f32[12,785920]{1,0:T(8,128)} reshape(f32[12,512,1535]{2,1,0:T(8,128)} %tile.10) | data formatting | bytes 75448320 | tf_op jit(solution)/shard_map/tile | solution.py:37
  305.3 38.2 %slice.126 = f32[12,785408]{1,0:T(8,128)} slice(f32[12,785920]{1,0:T(8,128)} %tile.11), slice={[0:12], [511:785919]} | slice | bytes 75399168 | tf_op jit(solution)/shard_map/slice | solution.py:38
  343.6 86.1 %reshape.234 = f32[12,512,1534]{2,1,0:T(8,128)} reshape(f32[12,785408]{1,0:T(8,128)} %slice.126) | data formatting | bytes 75399168 | tf_op jit(solution)/shard_map/reshape | solution.py:39
  429.7 16.8 %fusion.105 = (f32[12,512]{1,0:T(8,128)}, f32[12,512,1024]{2,1,0:T(8,128)}) fusion(f32[12,512,1534]{2,1,0:T(8,128)} %reshape.233, bf16[512,12,64]{0,2,1:T(8,128)(2,1)S(1)} %bitcast.134, bf16[1024,12,64]{0,2,1:T(8,128)(2,1)S(1)} %bitcast.121), kind=kOutput, calls=%fused_computation.149 | convolution fusion | flops 817883136 | bytes 52715520 | tf_op jit(solution)/shard_map/qhd,khd->hqk/dot_general | solution.py:108
  446.5 11.1 fusion
  457.6 11.4 fusion.74
  469.0 16.9 %fusion.104 = (f32[12,512]{1,0:T(8,128)}, f32[12,512,1024]{2,1,0:T(8,128)}) fusion(f32[12,512,1534]{2,1,0:T(8,128)} %reshape.234, bf16[512,12,64]{0,2,1:T(8,128)(2,1)S(1)} %bitcast.128, bf16[1024,12,64]{0,2,1:T(8,128)(2,1)S(1)} %bitcast.122), kind=kOutput, calls=%fused_computation.148 | convolution fusion | flops 817883136 | bytes 52715520 | tf_op jit(solution)/shard_map/qhd,khd->hqk/dot_general | solution.py:108
  485.9 11.1 fusion.1
  497.0 10.5 fusion.75
  515.2 7.7 scatter_custom_fusion
  524.4 51.7 %all_to_all.20 = bf16[8,160,768]{2,1,0:T(8,128)(2,1)S(1)} all-to-all(bf16[8,160,768]{2,1,0:T(8,128)(2,1)S(1)} %bitcast.125), channel_id=1, replica_groups=mesh['dp'=4,'expert'=8] {'expert'}, dimensions={0} | all-to-all | bytes 3932160 | tf_op jit(solution)/shard_map/all_to_all | solution.py:140
  577.3 8.3 fusion.33
  585.6 5.5 copy-done.68
  591.1 10.4 fusion.53
  601.5 5.2 all-to-all-start.1
  609.7 42.5 %all-to-all-done.1 = bf16[8,160,768]{2,1,0:T(8,128)(2,1)} async-done(((bf16[8,160,768]{2,1,0:T(8,128)(2,1)}), bf16[8,160,768]{2,1,0:T(8,128)(2,1)}, u32[]{:S(2)}, u32[]{:S(2)}) %all-to-all-start.1) | async-done | bytes 1966112 | tf_op jit(solution)/shard_map/all_to_all | solution.py:149
  653.9 5.2 gather_fusion
  661.8 3.3 fusion.39
  667.7 6.3 scatter_custom_fusion.1
  674.2 48.9 %all_to_all.21 = bf16[8,160,768]{2,1,0:T(8,128)(2,1)S(1)} all-to-all(bf16[8,160,768]{2,1,0:T(8,128)(2,1)S(1)} %bitcast.127), channel_id=1, replica_groups=mesh['dp'=4,'expert'=8] {'expert'}, dimensions={0} | all-to-all | bytes 3932160 | tf_op jit(solution)/shard_map/all_to_all | solution.py:163
  723.1 12.0 bitcast_convert_fusion
  735.1 17.6 %fusion.10 = bf16[8,160,3072]{2,1,0:T(8,128)(2,1)S(1)} fusion(f32[8,160,3072]{2,1,0:T(8,128)} %copy-done.68, bf16[8,160,768]{2,1,0:T(8,128)(2,1)S(1)} %all_to_all.21, bf16[1,3072,768]{2,1,0:T(8,128)(2,1)} %param.28), kind=kOutput, calls=%fused_computation.28 | convolution fusion | flops 6118440960 | bytes 30277632 | tf_op jit(solution)/shard_map/scd,fd->scf/dot_general | solution.py:167
  752.6 3.0 copy-done.69
  755.7 10.1 fusion.50
  765.8 4.5 all-to-all-start.3
  771.6 10.7 bitcast_convert_fusion.1
  782.3 33.4 %all-to-all-done.3 = bf16[8,160,768]{2,1,0:T(8,128)(2,1)S(1)} async-done(((bf16[8,160,768]{2,1,0:T(8,128)(2,1)}), bf16[8,160,768]{2,1,0:T(8,128)(2,1)S(1)}, u32[]{:S(2)}, u32[]{:S(2)}) %all-to-all-start.3) | async-done | bytes 1966112 | tf_op jit(solution)/shard_map/all_to_all | solution.py:174
  818.8 5.4 gather_fusion.1
  826.0 3.9 multiply_reduce_fusion.2
  836.0 20.4 %multiply_reduce_fusion.1 = (f32[12,512]{1,0:T(8,128)}, f32[12,512,1024]{2,1,0:T(8,128)}) fusion(f32[12,512,1024]{2,1,0:T(8,128)} %get-tuple-element.89, f32[12,512]{1,0:T(8,128)} %log_add_fusion.1, bf16[512,12,64]{0,2,1:T(8,128)(2,1)S(1)} %bitcast.130, bf16[1024,12,64]{0,2,1:T(8,128)(2,1)S(1)} %bitcast.139), kind=kOutput, calls=%fused_computation.10 | convolution fusion | flops 824174592 | bytes 52740096 | tf_op jit(solution)/shard_map/qhd,khd->hqk/dot_general | solution.py:222
  856.4 25.9 %subtract_multiply_fusion.1 = f32[12,512,1024]{2,1,0:T(8,128)} fusion(f32[12,512,1024]{2,1,0:T(8,128)} %get-tuple-element.98, f32[12,512,1024]{2,1,0:T(8,128)} %get-tuple-element.89, f32[12,512]{1,0:T(8,128)} %get-tuple-element.97, f32[12,512]{1,0:T(8,128)} %log_add_fusion.1), kind=kLoop, calls=%fused_computation.9 | loop fusion | flops 18874368 | bytes 75546624 | tf_op jit(solution)/shard_map/mul | solution.py:225
  882.3 13.0 fusion.71
  895.3 17.5 %multiply_reduce_fusion = (f32[12,512]{1,0:T(8,128)}, f32[12,512,1024]{2,1,0:T(8,128)}) fusion(f32[12,512,1024]{2,1,0:T(8,128)} %get-tuple-element.87, f32[12,512]{1,0:T(8,128)} %log_add_fusion, bf16[512,12,64]{0,2,1:T(8,128)(2,1)} %bitcast.132, bf16[1024,12,64]{0,2,1:T(8,128)(2,1)} %bitcast.136), kind=kOutput, calls=%fused_computation.7 | convolution fusion | flops 824174592 | bytes 52740096 | tf_op jit(solution)/shard_map/qhd,khd->hqk/dot_general | solution.py:222
  912.7 25.8 %subtract_multiply_fusion = f32[12,512,1024]{2,1,0:T(8,128)} fusion(f32[12,512,1024]{2,1,0:T(8,128)} %get-tuple-element.96, f32[12,512,1024]{2,1,0:T(8,128)} %get-tuple-element.87, f32[12,512]{1,0:T(8,128)} %get-tuple-element.95, f32[12,512]{1,0:T(8,128)} %log_add_fusion), kind=kLoop, calls=%fused_computation.6 | loop fusion | flops 18874368 | bytes 75546624 | tf_op jit(solution)/shard_map/mul | solution.py:225
  938.6 13.0 fusion.68
  953.2 10.8 fusion.11
  964.1 10.9 add_convert_fusion
  975.1 2.9 fusion.92
  977.9 2.9 fusion.96
  980.8 10.5 fusion.19
  991.3 10.7 add_convert_fusion.1
  1002.1 2.9 fusion.94
  1005.8 2.8 fusion.81
  1011.2 22.7 %pad.21 = f32[12,512,1534]{2,1,0:T(8,128)} pad(f32[12,512,1024]{2,1,0:T(8,128)} %subtract_multiply_fusion.1, f32[]{:T(128)} %constant.82.clone.1), padding=0_0x0_0x0_510 | pad | bytes 62865412 | tf_op jit(solution)/shard_map/jit(_pad)/pad | solution.py:45
  1033.9 23.0 %pad.23 = f32[12,512,1534]{2,1,0:T(8,128)} pad(f32[12,512,1024]{2,1,0:T(8,128)} %subtract_multiply_fusion, f32[]{:T(128)} %constant.82.clone.1), padding=0_0x0_0x0_510 | pad | bytes 62865412 | tf_op jit(solution)/shard_map/jit(_pad)/pad | solution.py:45
  1058.5 3.3 fusion.107
  1068.9 3.5 copy.47
  1072.5 70.1 %reshape.244 = f32[12,785408]{1,0:T(8,128)} reshape(f32[12,512,1534]{2,1,0:T(8,128)} %pad.21) | data formatting | bytes 75399168 | tf_op jit(solution)/shard_map/reshape | solution.py:46
  1142.6 38.4 %pad.22 = f32[12,785920]{1,0:T(8,128)} pad(f32[12,785408]{1,0:T(8,128)} %reshape.244, f32[]{:T(128)} %constant.82.clone.1), padding=0_0x511_1 | pad | bytes 75423744 | tf_op jit(solution)/shard_map/jit(_pad)/pad | solution.py:47
  1181.0 91.8 %reshape.245 = f32[12,512,1535]{2,1,0:T(8,128)} reshape(f32[12,785920]{1,0:T(8,128)} %pad.22) | data formatting | bytes 75448320 | tf_op jit(solution)/shard_map/reshape | solution.py:48
  1272.9 13.8 reduce_sum.159
  1286.7 69.0 %reshape.246 = f32[12,785408]{1,0:T(8,128)} reshape(f32[12,512,1534]{2,1,0:T(8,128)} %pad.23) | data formatting | bytes 75399168 | tf_op jit(solution)/shard_map/reshape | solution.py:46
  1355.7 37.7 %pad.24 = f32[12,785920]{1,0:T(8,128)} pad(f32[12,785408]{1,0:T(8,128)} %reshape.246, f32[]{:T(128)} %constant.82.clone.1), padding=0_0x511_1 | pad | bytes 75423744 | tf_op jit(solution)/shard_map/jit(_pad)/pad | solution.py:47
  1393.4 77.0 %reshape.247 = f32[12,512,1535]{2,1,0:T(8,128)} reshape(f32[12,785920]{1,0:T(8,128)} %pad.24) | data formatting | bytes 75448320 | tf_op jit(solution)/shard_map/reshape | solution.py:48
  1470.4 13.8 reduce_sum.160
  1486.2 38.9 %all-reduce.7 = (f32[32,12]{0,1:T(8,128)}, f32[768]{0:T(1024)}, f32[768]{0:T(1024)}, f32[768,8]{0,1:T(8,128)}) all-reduce(f32[32,12]{0,1:T(8,128)S(1)} %fusion.76, f32[768]{0:T(1024)S(1)} %copy-done.61, f32[768]{0:T(1024)S(1)} %copy-done.60, f32[768,8]{0,1:T(8,128)S(1)} %copy-done.49), channel_id=1, replica_groups=mesh['dp'=4,'expert'=8] {'dp','expert'}, use_global_device_ids=true, to_apply=%region_26.27 | all-reduce | flops 8064 | bytes 64512 | tf_op jit(solution)/shard_map/psum | solution.py:264
  1525.2 2.9 bitcast_convert_fusion.2
  1528.1 2.9 bitcast_convert_fusion.3
  1531.1 3.4 copy.59
  (208 shorter events, 75.0 us)
Async XLA Ops:
  8.0 17.4 %copy-start = (bf16[768,768]{1,0:T(8,128)(2,1)S(1)}, bf16[768,768]{1,0:T(8,128)(2,1)}, u32[]{:S(2)}) copy-start(bf16[768,768]{1,0:T(8,128)(2,1)} %param.22) | copy-start | bytes 3538948
  8.0 10.1 copy-start.56
  17.0 8.4 copy-start.7
  18.1 7.3 copy-start.52
  343.6 86.1 %copy-start.3 = (bf16[1024,768]{0,1:T(8,128)(2,1)S(1)}, bf16[1024,768]{0,1:T(8,128)(2,1)}, u32[]{:S(2)}) copy-start(bf16[1024,768]{0,1:T(8,128)(2,1)} %convolution_convert_fusion.1) | copy-start | bytes 4718596
  343.6 86.1 %copy-start.21 = (bf16[512,768]{0,1:T(8,128)(2,1)S(1)}, bf16[512,768]{0,1:T(8,128)(2,1)}, u32[]{:S(2)}) copy-start(bf16[512,768]{0,1:T(8,128)(2,1)} %get-tuple-element.78) | copy-start | bytes 2359300
  446.5 11.1 copy-start.23
  446.5 11.1 copy-start.43
  457.6 11.4 copy-start.47
  457.6 11.4 copy-start.18
  485.9 11.1 copy-start.24
  485.9 11.1 copy-start.45
  497.0 10.5 copy-start.40
  507.5 2.0 copy-start.8
  507.5 2.3 copy-start.63
  507.7 3.8 copy-start.33
  509.8 3.4 copy-start.51
  513.2 2.0 copy-start.62
  513.5 95.8 %copy-start.5 = (bf16[1024,768]{0,1:T(8,128)(2,1)}, bf16[1024,768]{0,1:T(8,128)(2,1)S(1)}, u32[]{:S(2)}) copy-start(bf16[1024,768]{0,1:T(8,128)(2,1)S(1)} %multiply_convert_fusion.1) | copy-start | bytes 4718596
  522.8 68.3 %slice-start.1 = ((s8[4718592]{0:T(1024)(128)(4,1)}), s8[4194304]{0:T(1024)(128)(4,1)S(1)}, s32[]{:S(2)}) async-start(s8[4718592]{0:T(1024)(128)(4,1)} %bitcast.158), calls=%async_computation.10 | async-start | bytes 8388608
  577.3 13.8 slice-start.2
  585.6 5.5 copy-start.68
  601.5 7.8 copy-start.50
  601.5 50.7 %all-to-all-start.1 = ((bf16[8,160,768]{2,1,0:T(8,128)(2,1)}), bf16[8,160,768]{2,1,0:T(8,128)(2,1)}, u32[]{:S(2)}, u32[]{:S(2)}) async-start(bf16[8,160,768]{2,1,0:T(8,128)(2,1)} %fusion.53), calls=%async_computation.1 | async-start | bytes 3932160 | tf_op jit(solution)/shard_map/all_to_all | solution.py:149
  606.7 3.0 copy-start.46
  606.7 918.5 %reduce-scatter.5.cloned.1.call-start = ((), (), s32[]{:S(2)}) async-start(), calls=%async_computation.7 | async-start | bytes 5898240 | tf_op jit(solution)/shard_map/reduce_scatter | solution.py:183
  609.6 216.4 %copy-start.38 = (f32[1024,8]{0,1:T(8,128)}, f32[1024,8]{0,1:T(8,128)S(1)}, u32[]{:S(2)}) copy-start(f32[1024,8]{0,1:T(8,128)S(1)} %get-tuple-element.93) | copy-start | bytes 98308
  659.1 2.7 copy-start.11
  752.6 3.1 copy-start.69
  765.8 4.5 copy-start.44
  765.8 4.5 copy-start.48
  765.8 49.9 %all-to-all-start.3 = ((bf16[8,160,768]{2,1,0:T(8,128)(2,1)}), bf16[8,160,768]{2,1,0:T(8,128)(2,1)S(1)}, u32[]{:S(2)}, u32[]{:S(2)}) async-start(bf16[8,160,768]{2,1,0:T(8,128)(2,1)} %fusion.50), calls=%async_computation.3 | async-start | bytes 3932160 | tf_op jit(solution)/shard_map/all_to_all | solution.py:174
  770.3 757.8 %reduce-scatter.3.cloned.1.call-start = ((), (), s32[]{:S(2)}) async-start(), calls=%async_computation.6 | async-start | bytes 5898240 | tf_op jit(solution)/shard_map/reduce_scatter | solution.py:180
  771.6 54.4 %copy-start.54 = (f32[1024]{0:T(1024)}, f32[1024]{0:T(1024)S(1)}, u32[]{:S(2)}) copy-start(f32[1024]{0:T(1024)S(1)} %mul.240) | copy-start | bytes 12292
  782.3 748.8 %all-reduce.11.cloned.1.call-start = ((), (), s32[]{:S(2)}) async-start(), calls=%async_computation.8 | async-start | bytes 18874368 | tf_op jit(solution)/shard_map/psum | solution.py:264
  826.0 3.9 copy-start.2
  826.0 3.9 copy-start.12
  826.0 3.9 copy-start.13
  829.9 2.7 copy-start.64
  856.4 25.9 %copy-start.4 = (bf16[1024,768]{0,1:T(8,128)(2,1)S(1)}, bf16[1024,768]{0,1:T(8,128)(2,1)}, u32[]{:S(2)}) copy-start(bf16[1024,768]{0,1:T(8,128)(2,1)} %convolution_convert_fusion.1) | copy-start | bytes 4718596
  953.2 24.7 %copy-start.35 = (bf16[1024,12,64]{0,2,1:T(8,128)(2,1)}, bf16[1024,12,64]{0,2,1:T(8,128)(2,1)S(1)}, u32[]{:S(2)}) copy-start(bf16[1024,12,64]{0,2,1:T(8,128)(2,1)S(1)} %pad_maximum_fusion.1) | copy-start | bytes 4718596
  953.2 10.9 copy-start.41
  964.1 11.0 copy-start.9
  964.1 11.0 copy-start.53
  964.1 11.0 copy-start.57
  975.0 2.9 copy-start.26
  977.9 2.9 copy-start.19
  980.8 10.5 copy-start.22
  1002.0 2.9 copy-start.36
  1002.1 2.9 copy-start.15
  1002.1 3.8 copy-start.34
  1033.9 23.0 %copy-start.28 = (bf16[1024,768]{0,1:T(8,128)(2,1)S(1)}, bf16[1024,768]{0,1:T(8,128)(2,1)}, u32[]{:S(2)}) copy-start(bf16[1024,768]{0,1:T(8,128)(2,1)} %get-tuple-element.73) | copy-start | bytes 4718596
  1058.5 3.3 copy-start.37
  1058.5 3.3 copy-start.66
  1061.8 1.9 copy-start.27
  1063.7 2.8 copy-start.16
  1063.7 2.8 copy-start.59
  1470.3 15.3 copy-start.67
  1470.4 15.9 %copy-start.49 = (f32[768,8]{0,1:T(8,128)S(1)}, f32[768,8]{0,1:T(8,128)}, u32[]{:S(2)}) copy-start(f32[768,8]{0,1:T(8,128)} %fusion.91) | copy-start | bytes 73732
  1470.4 15.8 %copy-start.60 = (f32[768]{0:T(1024)S(1)}, f32[768]{0:T(1024)}, u32[]{:S(2)}) copy-start(f32[768]{0:T(1024)} %get-tuple-element.60) | copy-start | bytes 9220
  1470.4 15.8 %copy-start.61 = (f32[768]{0:T(1024)S(1)}, f32[768]{0:T(1024)}, u32[]{:S(2)}) copy-start(f32[768]{0:T(1024)} %get-tuple-element.62) | copy-start | bytes 9220
  1531.1 3.4 copy-start.31
  1534.4 2.5 copy-start.30
  1536.9 2.5 copy-start.29
  (14 other events, 21.7 us)
Sparse Core Ops, SparseCore 0:
  735.2 56.1 reduce-scatter.4
  794.7 57.0 reduce-scatter.2
Sparse Core Ops, SparseCore 1:
  1008.8 190.9 all-reduce.10
where the time goes:
time: 1560 us; the launch traced here: 1550 us
  local copies, waits for them, and re-layouts  911 us (58%)
  matrix products  269 us (17%)
  blocking collectives  139 us (9%)
  other arithmetic  127 us (8%)
  waiting for transfers between devices  75.9 us (5%)
  between operations  16.7 us (1%)
    reshape x2, local copies, waits for them, and re-layouts, bias_block(): return flat.reshape(head_count, block_rows, width - 1)[:, :, :seq_len]  176 us
    reshape x2, local copies, waits for them, and re-layouts, diagonal_sums(): return jnp.sum(flat.reshape(head_count, block_rows, width), axis=1)  169 us
    another operation x4, local copies, waits for them, and re-layouts, bias_block(): flat = jnp.tile(window, (1, block_rows))  149 us
    reshape x2, local copies, waits for them, and re-layouts, diagonal_sums(): flat = padded.reshape(head_count, block_rows * (width - 1))  139 us
    slice x2, local copies, waits for them, and re-layouts, bias_block(): flat = flat[:, block_rows - 1:block_rows - 1 + block_rows * (width - 1)]  76.5 us
    pad x2, local copies, waits for them, and re-layouts, diagonal_sums(): flat = jnp.pad(flat, ((0, 0), (block_rows - 1, 1)))  76.1 us
    mul x2, other arithmetic, on_device(): att_probs * (prob_grad - jnp.sum(att_probs * prob_grad, axis=-1, keepdims...  51.7 us
    all_to_all x1, blocking collectives, on_device(): lax.all_to_all(send_rows, 'expert', split_axis=0, concat_axis=0, tiled=True)  51.7 us
  transfers between devices with their start and end apart: 5, of which 2 were waited for; matrix products, arithmetic and copies ran while one was open for 46% of the time, Pallas kernels for 0%

commit v1 on v0

v1 whole, which is shorter than its diff:
```python
import jax
import jax.numpy as jnp
from jax import lax
from jax.experimental import pallas as pl
from jax.experimental.pallas import tpu as pltpu
from jax.sharding import PartitionSpec as P

bf16 = jnp.bfloat16
f32 = jnp.float32
epsilon = 1e-06
highest = lax.Precision.HIGHEST

def dot_f32(left, right):
    return lax.dot_general(left, right, (((1,), (0,)), ((), ())), preferred_element_type=f32)


def fill_toeplitz(base_ref, head, row):
    rows, width = base_ref.shape[1:]
    spread = jnp.broadcast_to(row, (8, width))
    eight = pltpu.roll(spread, 0, 1, stride=1, stride_axis=0)
    for group in range(rows // 8):
        base_ref[head, 8 * group : 8 * group + 8, :] = (
            eight if group == 0 else pltpu.roll(eight, 8 * group, 1)
        )


def attend_kernel(q_ref, k_ref, v_ref, u_ref, ctx_ref, ctxt_ref, lse_ref, base, qt, vt, s_scr, p_scr):
    seq = q_ref.shape[0]
    span = 256
    half = seq
    qt[...] = q_ref[...].T
    vt[...] = v_ref[...].T
    for head in range(2):
        fill_toeplitz(base, head, u_ref[0, head : head + 1, :])
    zeros = jnp.zeros((64, span), bf16)

    def step(idx, carry):
        cols = pl.ds(pl.multiple_of(idx * span, span), span)
        outs = []
        for head in range(2):
            part = qt[64 * head : 64 * head + 64, cols]
            rhs = jnp.concatenate([part, zeros] if head == 0 else [zeros, part], axis=0)
            peak = None
            for kb in range(seq // 128):
                rows = slice(128 * kb, 128 * kb + 128)
                offs = pl.multiple_of(half + span * idx - 128 * kb, 128)
                s = dot_f32(k_ref[rows, :], rhs) + base[head, :, pl.ds(offs, span)]
                s_scr[head, rows, :] = s
                now = jnp.max(s.reshape(16, 8, span), axis=0)
                peak = now if peak is None else jnp.maximum(peak, now)
            peak = jnp.max(peak, axis=0, keepdims=True)
            total = None
            for kb in range(seq // 128):
                rows = slice(128 * kb, 128 * kb + 128)
                e = jnp.exp(s_scr[head, rows, :] - peak)
                s_scr[head, rows, :] = e
                now = jnp.sum(e.reshape(16, 8, span), axis=0)
                total = now if total is None else total + now
            total = jnp.sum(total, axis=0, keepdims=True)
            inv = 1.0 / total
            for kb in range(seq // 128):
                rows = slice(128 * kb, 128 * kb + 128)
                p_scr[head, rows, :] = (s_scr[head, rows, :] * inv).astype(bf16)
            lse_ref[0, head : head + 1, cols] = peak + jnp.log(total)
            outs.append(dot_f32(vt[64 * head : 64 * head + 64, :], p_scr[head]))
        both = jnp.concatenate(outs, axis=0)
        ctxt_ref[:, cols] = both
        ctx_ref[cols, :] = both.T.astype(bf16)
        return carry

    lax.fori_loop(0, seq // span, step, 0)


def attend(q, k, v, u):
    seq, width = q.shape
    pairs = width // 128
    blk = pl.BlockSpec((seq, 128), lambda p: (0, p))
    return pl.pallas_call(
        attend_kernel,
        grid=(pairs,),
        in_specs=[blk, blk, blk, pl.BlockSpec((1, 2, 2 * seq), lambda p: (p, 0, 0))],
        out_specs=[
            blk,
            pl.BlockSpec((128, seq), lambda p: (p, 0)),
            pl.BlockSpec((1, 8, seq), lambda p: (p, 0, 0)),
        ],
        out_shape=[
            jax.ShapeDtypeStruct((seq, width), bf16),
            jax.ShapeDtypeStruct((width, seq), f32),
            jax.ShapeDtypeStruct((pairs, 8, seq), f32),
        ],
        scratch_shapes=[
            pltpu.VMEM((2, 128, 2 * seq), f32),
            pltpu.VMEM((128, seq), bf16),
            pltpu.VMEM((128, seq), bf16),
            pltpu.VMEM((2, seq, 256), f32),
            pltpu.VMEM((2, seq, 256), bf16),
        ],
        compiler_params=pltpu.CompilerParams(vmem_limit_bytes=48 << 20),
        cost_estimate=pl.CostEstimate(
            flops=16 * seq * seq * width, bytes_accessed=20 * seq * width, transcendentals=seq * seq * 12
        ),
        name="attend",
    )(q, k, v, u)


def split_rows(row):
    hi = row.astype(bf16).astype(f32)
    mid = (row - hi).astype(bf16).astype(f32)
    low = row - hi - mid
    idx = lax.broadcasted_iota(jnp.int32, (16, row.shape[1]), 0)
    return jnp.where(idx == 0, hi, jnp.where(idx == 1, mid, jnp.where(idx == 2, low, 0.0))).astype(bf16)


def attend_back_kernel(
    q_ref, k_ref, v_ref, g_ref, u_ref, ctxt_ref, lse_ref,
    dq_ref, dk_ref, dv_ref, diag_ref,
    base, acc, kaug, vaug, qaug, gaug, qz, gz, kt, dqt,
):
    seq = q_ref.shape[0]
    span = 256
    lane = lax.broadcasted_iota(jnp.int32, (seq, 128), 1)
    gt = g_ref[...].T
    qtv = q_ref[...].T
    kt[...] = k_ref[...].T
    gtf = gt.astype(f32)
    pad = jnp.zeros((48, seq), bf16)
    one = jnp.ones((seq, 128), bf16)
    nil = jnp.zeros((seq, 128), bf16)
    acc[...] = jnp.zeros_like(acc)
    for head in range(2):
        fill_toeplitz(base, head, u_ref[0, head : head + 1, :])
        own = (lane < 64) if head == 0 else (lane >= 64)
        origin = 64 if head == 0 else 0
        extra = jnp.where((lane >= origin) & (lane < origin + 3), one, nil)
        kaug[head] = jnp.where(own, k_ref[...], extra)
        vaug[head] = jnp.where(own, v_ref[...], extra)
        qz[head] = jnp.where(own, q_ref[...], nil)
        gz[head] = jnp.where(own, g_ref[...], nil)
        rows = slice(64 * head, 64 * head + 64)
        lse = split_rows(-lse_ref[0, head : head + 1, :])
        dsum = split_rows(-jnp.sum(gtf[rows] * ctxt_ref[rows, :], axis=0, keepdims=True))
        for dst, src, aug in ((qaug, qtv, lse), (gaug, gt, dsum)):
            dst[head, rows, :] = src[rows]
            dst[head, origin : origin + 16, :] = aug
            dst[head, origin + 16 : origin + 64, :] = pad

    dqt[...] = jnp.zeros_like(dqt)

    def step(idx, carry):
        rows = pl.ds(pl.multiple_of(idx * span, span), span)
        dv = None
        dk = None
        for head in range(2):
            s = dot_f32(kaug[head, rows, :], qaug[head])
            dp = dot_f32(vaug[head, rows, :], gaug[head])
            tops = []
            grads = []
            for part in range(2):
                offs = pl.ds(pl.multiple_of(seq - span * idx - 128 * part, 128), seq)
                p = jnp.exp(s[128 * part : 128 * part + 128] + base[head, :, offs])
                ds_ = p * dp[128 * part : 128 * part + 128]
                acc[head, :, offs] += ds_
                tops.append(p.astype(bf16))
                grads.append(ds_.astype(bf16))
            p = jnp.concatenate(tops, axis=0)
            ds_ = jnp.concatenate(grads, axis=0)
            now = dot_f32(p, gz[head])
            dv = now if dv is None else dv + now
            now = dot_f32(ds_, qz[head])
            dk = now if dk is None else dk + now
            dqt[64 * head : 64 * head + 64, :] += dot_f32(kt[64 * head : 64 * head + 64, rows], ds_)
        dv_ref[rows, :] = dv.astype(bf16)
        dk_ref[rows, :] = dk.astype(bf16)
        return carry

    lax.fori_loop(0, seq // span, step, 0)
    dq_ref[...] = dqt[...].T.astype(bf16)
    width = 2 * seq
    for head in range(2):
        total = acc[head, 0:8, :]
        for group in range(1, 16):
            total = total + pltpu.roll(acc[head, 8 * group : 8 * group + 8, :], width - 8 * group, 1)
        sub = lax.broadcasted_iota(jnp.int32, (8, width), 0)
        for bit in (1, 2, 4):
            total = jnp.where((sub & bit) != 0, pltpu.roll(total, width - bit, 1), total)
        diag_ref[0, head : head + 1, :] = jnp.sum(total, axis=0, keepdims=True)


def attend_back(q, k, v, g, u, ctxt, lse):
    seq, width = q.shape
    pairs = width // 128
    blk = pl.BlockSpec((seq, 128), lambda p: (0, p))
    return pl.pallas_call(
        attend_back_kernel,
        grid=(pairs,),
        in_specs=[
            blk, blk, blk, blk,
            pl.BlockSpec((1, 2, 2 * seq), lambda p: (p, 0, 0)),
            pl.BlockSpec((128, seq), lambda p: (p, 0)),
            pl.BlockSpec((1, 8, seq), lambda p: (p, 0, 0)),
        ],
        out_specs=[blk, blk, blk, pl.BlockSpec((1, 8, 2 * seq), lambda p: (p, 0, 0))],
        out_shape=[jax.ShapeDtypeStruct((seq, width), bf16)] * 3
        + [jax.ShapeDtypeStruct((pairs, 8, 2 * seq), f32)],
        scratch_shapes=[
            pltpu.VMEM((2, 128, 2 * seq), f32),
            pltpu.VMEM((2, 128, 2 * seq), f32),
            pltpu.VMEM((2, seq, 128), bf16),
            pltpu.VMEM((2, seq, 128), bf16),
            pltpu.VMEM((2, 128, seq), bf16),
            pltpu.VMEM((2, 128, seq), bf16),
            pltpu.VMEM((2, seq, 128), bf16),
            pltpu.VMEM((2, seq, 128), bf16),
            pltpu.VMEM((128, seq), bf16),
            pltpu.VMEM((128, seq), f32),
        ],
        compiler_params=pltpu.CompilerParams(vmem_limit_bytes=56 << 20),
        cost_estimate=pl.CostEstimate(
            flops=40 * seq * seq * width, bytes_accessed=20 * seq * width, transcendentals=seq * seq * 12
        ),
        name="attend_back",
    )(q, k, v, g, u, ctxt, lse)


def rms_backward(grad_norm, values, row_scale, gain_vec):
    weighted = grad_norm * gain_vec
    gain_grad = jnp.sum(grad_norm * values * row_scale, axis=0)
    grad_in = row_scale * weighted - values * row_scale**3 * jnp.mean(
        weighted * values, axis=-1, keepdims=True
    )
    return grad_in, gain_grad


def rms_forward(values, gain_vec):
    row_scale = lax.rsqrt(jnp.mean(values * values, axis=-1, keepdims=True) + epsilon)
    return values * row_scale * gain_vec, row_scale


def gelu_tanh(values):
    return jax.nn.gelu(values, approximate=True)


def contract(left, right, dims):
    return lax.dot_general(left, right, (((dims[0],), (dims[1],)), ((), ())), preferred_element_type=f32)


def on_device(
    tokens, gain_one, query_w, key_w, value_w, out_w, rel_table, gain_two, router_w,
    expert_in, expert_out, routes, buckets, cotangent,
):
    seq_len, width = tokens.shape
    heads = rel_table.shape[1]
    experts = lax.axis_size("expert")
    capacity = (5 * seq_len + 4 * experts - 1) // (4 * experts)
    slots = experts * capacity
    weight_in = expert_in[0]
    weight_out = expert_out[0]

    route_ids = routes[:, 0]
    route_hot = route_ids[:, None] == jnp.arange(experts, dtype=jnp.int32)[None, :]
    route_int = route_hot.astype(jnp.int32)
    route_float = route_hot.astype(f32)
    position = jnp.sum((jnp.cumsum(route_int, axis=0) - 1) * route_int, axis=1)
    slot_index = jnp.where(position < capacity, route_ids * capacity + position, slots)
    pick = (jnp.arange(slots, dtype=jnp.int32)[:, None] == slot_index[None, :]).astype(bf16)

    def exchange(rows):
        rows = rows.reshape(experts, capacity, width)
        return lax.all_to_all(rows, "expert", split_axis=0, concat_axis=0, tiled=True).reshape(slots, width)

    def scatter_rows(rows):
        return contract(pick, rows, (1, 0)).astype(bf16)

    def gather_rows(rows):
        return contract(pick, rows, (0, 0))

    grad_recv = exchange(scatter_rows(cotangent))

    tokens_f = tokens.astype(f32)
    normed, scale_one = rms_forward(tokens_f, gain_one)
    normed_low = normed.astype(bf16)
    queries = contract(normed_low, query_w, (1, 0)).astype(bf16)
    key_rows = contract(normed_low, key_w, (1, 0)).astype(bf16)
    value_rows = contract(normed_low, value_w, (1, 0)).astype(bf16)
    reach = jnp.concatenate([buckets, jnp.full((1,), -1, jnp.int32)])[::-1]
    bucket_hot = (jnp.arange(rel_table.shape[0], dtype=jnp.int32)[:, None] == reach[None, :]).astype(f32)
    spread = jnp.einsum("bh,bx->hx", rel_table, bucket_hot, precision=highest)
    spread = spread.reshape(heads // 2, 2, 2 * seq_len)
    context, context_t, logsum = attend(queries, key_rows, value_rows, spread)
    hidden = tokens_f + contract(context, out_w, (1, 0))
    normed_two, scale_two = rms_forward(hidden, gain_two)
    normed_two_low = normed_two.astype(bf16)

    received = exchange(scatter_rows(normed_two_low))
    own = lax.axis_index("expert")
    own_hot = (jnp.arange(experts, dtype=jnp.int32) == own).astype(f32)[None, :]
    probs_recv = jax.nn.softmax(contract(received, router_w, (1, 0)), axis=-1)
    gate_recv = jnp.sum(probs_recv * own_hot, axis=-1, keepdims=True)
    grad_recv_f = grad_recv.astype(f32)
    grad_produced = (grad_recv_f * gate_recv).astype(bf16)
    preact = contract(received, weight_in, (1, 0))
    gelu_values, gelu_pullback = jax.vjp(gelu_tanh, preact)
    active = gelu_values.astype(bf16)
    produced = contract(active, weight_out, (1, 0)).astype(bf16)
    gate_grad = jnp.sum(grad_recv_f * produced.astype(f32), axis=-1, keepdims=True)
    logit_low = (gate_grad * gate_recv * (own_hot - probs_recv)).astype(bf16)
    grad_active = contract(grad_produced, weight_out, (1, 1))
    grad_preact = gelu_pullback(grad_active)[0].astype(bf16)
    grad_received = contract(grad_preact, weight_in, (1, 1)) + contract(logit_low, router_w, (1, 1))
    grad_rows = exchange(grad_received.astype(bf16))
    returned = exchange(produced)
    in_grad = contract(received, grad_preact, (0, 0)).astype(bf16)
    out_grad_local = contract(active, grad_produced, (0, 0)).astype(bf16)
    router_grad = contract(received, logit_low, (0, 0))
    in_share = lax.psum_scatter(in_grad, "dp", scatter_dimension=0, tiled=True).astype(f32)
    out_share = lax.psum_scatter(out_grad_local, "dp", scatter_dimension=1, tiled=True).astype(f32)

    router_probs = jax.nn.softmax(contract(normed_two_low, router_w, (1, 0)), axis=-1)
    gate_value = jnp.sum(router_probs * route_float, axis=-1, keepdims=True)
    output = (hidden + gate_value * gather_rows(returned)).astype(bf16)

    grad_out = cotangent.astype(f32)
    grad_normed_two = gather_rows(grad_rows)
    grad_hidden_norm, gain_two_grad = rms_backward(grad_normed_two, hidden, scale_two, gain_two)
    grad_hidden = grad_out + grad_hidden_norm
    branch_low = grad_hidden.astype(bf16)
    out_w_grad = contract(context, branch_low, (0, 0))
    grad_context = contract(branch_low, out_w, (1, 1)).astype(bf16)
    out_w_grad = lax.psum(out_w_grad, ("dp", "expert"))
    query_grad, key_grad, value_grad, diagonals = attend_back(
        queries, key_rows, value_rows, grad_context, spread, context_t, logsum
    )
    query_w_grad = contract(normed_low, query_grad, (0, 0))
    key_w_grad = contract(normed_low, key_grad, (0, 0))
    value_w_grad = contract(normed_low, value_grad, (0, 0))
    grad_normed = (
        contract(query_grad, query_w, (1, 1))
        + contract(key_grad, key_w, (1, 1))
        + contract(value_grad, value_w, (1, 1))
    )
    grad_tokens_norm, gain_one_grad = rms_backward(grad_normed, tokens_f, scale_one, gain_one)
    input_grad = grad_hidden + grad_tokens_norm
    diagonals = diagonals[:, :2].reshape(heads, 2 * seq_len)
    rel_grad = jnp.einsum("bx,hx->bh", bucket_hot, diagonals, precision=highest)
    query_w_grad, key_w_grad, value_w_grad, rel_grad, gain_one_grad, gain_two_grad, router_grad = lax.psum(
        (query_w_grad, key_w_grad, value_w_grad, rel_grad, gain_one_grad, gain_two_grad, router_grad),
        ("dp", "expert"),
    )
    return (
        output, input_grad, query_w_grad, key_w_grad, value_w_grad, out_w_grad, rel_grad,
        gain_one_grad, gain_two_grad, router_grad, in_share[None], out_share[None],
    )


def solution(mesh):
    rows = P(("dp", "expert"), None)
    whole = P()
    split = P("expert", None, None)
    return jax.shard_map(
        on_device,
        mesh=mesh,
        in_specs=(
            rows, whole, whole, whole, whole, whole, whole, whole, whole, split, split, rows, whole, rows,
        ),
        out_specs=(
            rows, rows, whole, whole, whole, whole, whole, whole, whole, whole,
            P("expert", "dp", None), P("expert", None, "dp"),
        ),
        check_vma=False,
    )
```

time: 1560 us -> 593 us (0.38)
  local copies, waits for them, and re-layouts: 911 us -> 21.8 us
  waiting for transfers between devices: 75.9 us -> 222 us
  matrix products: 269 us -> 140 us
  other arithmetic: 127 us -> 18.1 us
  Pallas kernels: 0 us -> 99.7 us
  blocking collectives: 139 us -> 42.7 us
    reshape x6 -> x2, local copies, waits for them, and re-layouts: 484 us -> 0.13 us  [the longest x1 0.07 us: on_device(): diagonals = diagonals[:, :2].reshape(heads, 2 * seq_len)]
    another operation x5 -> x0, local copies, waits for them, and re-layouts: 149 us -> none  [the longest x4 149 us: bias_block(): flat = jnp.tile(window, (1, block_rows))]
    dot_general x35 -> x28, matrix products: 269 us -> 140 us  [the longest x26 139 us: contract(): lax.dot_general(left, right, (((dims[0],), (dims[1],)), ((), ())), prefer...]
    pad x4 -> x0, local copies, waits for them, and re-layouts: 122 us -> none  [the longest x2 76.1 us: diagonal_sums(): flat = jnp.pad(flat, ((0, 0), (block_rows - 1, 1)))]
    psum x1, waiting for transfers between devices: 0.01 us -> 120 us  [on_device(): lax.psum((query_w_grad, key_w_grad, value_w_grad, rel_grad, gain_one_grad...]
    all_to_all x2 -> x0, blocking collectives: 101 us -> none  [the longest x1 51.7 us: on_device(): lax.all_to_all(send_rows, 'expert', split_axis=0, concat_axis=0, tiled=True)]
    pallas_call x0 -> x2, Pallas kernels: none -> 99.7 us  [the longest x1 57.5 us: attend_back(): pl.pallas_call(attend_back_kernel, grid=(pairs,), in_specs=[blk, blk, blk...]
    slice x8 -> x2, local copies, waits for them, and re-layouts: 80.5 us -> 1.3 us  [the longest x1 1.02 us: on_device(): diagonals = diagonals[:, :2].reshape(heads, 2 * seq_len)]
  transfers between devices with their start and end apart: 5 -> 7, of which waited for: 2 -> 4; matrix products, arithmetic and copies ran while one was open for 46% -> 21% of each run, Pallas kernels for 0% -> 10%
where the time goes in v1:
time: 593 us; the launch traced here: 583 us
  waiting for transfers between devices  222 us (37%)
  matrix products  140 us (24%)
  Pallas kernels  99.7 us (17%)
  blocking collectives  42.7 us (7%)
  starting transfers between devices  21.9 us (4%)
  local copies, waits for them, and re-layouts  21.8 us (4%)
  other arithmetic  18.1 us (3%)
  between operations  16.4 us (3%)
    dot_general x26, matrix products, contract(): lax.dot_general(left, right, (((dims[0],), (dims[1],)), ((), ())), prefer...  139 us
    psum x1, waiting for transfers between devices, on_device(): lax.psum((query_w_grad, key_w_grad, value_w_grad, rel_grad, gain_one_grad...  120 us
    all_to_all x4, waiting for transfers between devices, exchange(): lax.all_to_all(rows, 'expert', split_axis=0, concat_axis=0, tiled=True)  102 us
    pallas_call x1, Pallas kernels, attend_back(): pl.pallas_call(attend_back_kernel, grid=(pairs,), in_specs=[blk, blk, blk...  57.5 us
    psum x1, blocking collectives, on_device(): lax.psum((query_w_grad, key_w_grad, value_w_grad, rel_grad, gain_one_grad...  42.7 us
    pallas_call x1, Pallas kernels, attend(): pl.pallas_call(attend_kernel, grid=(pairs,), in_specs=[blk, blk, blk, pl....  42.2 us
    all_to_all x4, starting transfers between devices, exchange(): lax.all_to_all(rows, 'expert', split_axis=0, concat_axis=0, tiled=True)  21.6 us
    unnamed x82, local copies, waits for them, and re-layouts  20.3 us
  transfers between devices with their start and end apart: 7, of which 4 were waited for; matrix products, arithmetic and copies ran while one was open for 21% of the time, Pallas kernels for 10%

profile of v1, /device:TPU:1, one launch (start us, length us, event | category | flops | bytes accessed | tf_op | source)
XLA Modules:
  0.0 582.9 jit_solution(9234907398915730586)
XLA Ops:
  8.0 0.9 pad_add_fusion
  9.0 0.7 fusion.50
  9.7 2.3 reduce-window.6
  11.9 0.3 slice_reduce_fusion
  12.5 0.7 fusion.49
  13.2 0.7 add_select_fusion
  13.9 0.9 convolution_bitcast_fusion
  14.9 1.8 copy.36
  16.6 0.4 fusion.27
  17.0 0.7 multiply_multiply_fusion.2
  17.7 2.8 convolution_convert_fusion.4.k_ref
  20.6 2.7 convolution_convert_fusion.3.v_ref
  23.3 1.5 convolution_convert_fusion.5.q_ref
  24.9 42.2 %attend.1 = (bf16[1024,768]{1,0:T(8,128)(2,1)S(1)}, f32[768,1024]{1,0:T(8,128)}, f32[6,8,1024]{2,1,0:T(8,128)S(1)}) custom-call(bf16[1024,768]{1,0:T(8,128)(2,1)S(1)} %convolution_convert_fusion.5.q_ref, bf16[1024,768]{1,0:T(8,128)(2,1)S(1)} %convolution_convert_fusion.4.k_ref, bf16[1024,768]{1,0:T(8,128)(2,1)} %convolution_convert_fusion.3.v_ref, ...), custom_call_target="tpu_custom_call" | custom-call | flops 12884901888 | bytes 15728640 | tf_op jit(solution)/shard_map/attend/pallas_call | solution.py:78
  67.1 1.6 multiply_reduce_fusion.2
  68.7 3.9 fusion.25
  72.6 6.4 %all-to-all-start = ((bf16[8,160,768]{2,1,0:T(8,128)(2,1)}), bf16[8,160,768]{2,1,0:T(8,128)(2,1)S(1)}, u32[]{:S(2)}, u32[]{:S(2)}) async-start(bf16[8,160,768]{2,1,0:T(8,128)(2,1)} %bitcast.93), calls=%async_computation | async-start | bytes 3932160 | tf_op jit(solution)/shard_map/all_to_all | solution.py:270
  78.9 5.1 fusion.26
  84.0 40.3 %all-to-all-done = bf16[8,160,768]{2,1,0:T(8,128)(2,1)S(1)} async-done(((bf16[8,160,768]{2,1,0:T(8,128)(2,1)}), bf16[8,160,768]{2,1,0:T(8,128)(2,1)S(1)}, u32[]{:S(2)}, u32[]{:S(2)}) %all-to-all-start) | async-done | bytes 1966112 | tf_op jit(solution)/shard_map/all_to_all | solution.py:270
  124.3 5.1 all-to-all-start.2
  129.4 0.6 fusion.63
  130.2 11.9 %fusion.16 = f32[1280,3072]{1,0:T(8,128)} fusion(bf16[1280,768]{1,0:T(8,128)(2,1)S(1)} %bitcast.87, bf16[1,768,3072]{2,1,0:T(8,128)(2,1)} %param.23), kind=kOutput, calls=%fused_computation.28 | convolution fusion | flops 6039797760 | bytes 22413312 | tf_op jit(solution)/shard_map/dot_general | solution.py:245
  142.1 32.8 %all-to-all-done.2 = bf16[8,160,768]{2,1,0:T(8,128)(2,1)} async-done(((bf16[8,160,768]{2,1,0:T(8,128)(2,1)}), bf16[8,160,768]{2,1,0:T(8,128)(2,1)}, u32[]{:S(2)}, u32[]{:S(2)}) %all-to-all-start.2) | async-done | bytes 1966112 | tf_op jit(solution)/shard_map/all_to_all | solution.py:270
  174.9 15.9 %fusion.20 = (bf16[1280,768]{1,0:T(8,128)(2,1)}, f32[1280]{0:T(1024)S(1)}, bf16[1280,768]{1,0:T(8,128)(2,1)}) fusion(bf16[8,160,768]{2,1,0:T(8,128)(2,1)} %all-to-all-done.2, f32[1280]{0:T(1024)S(1)} %multiply_reduce_fusion.3, bf16[1,3072,768]{2,1,0:T(8,128)(2,1)} %param.24, f32[1280,3072]{1,0:T(8,128)} %fusion.16), kind=kOutput, calls=%fused_computation.36 | convolution fusion | flops 6082067456 | bytes 26355712 | tf_op jit(solution)/shard_map/dot_general | solution.py:245
  190.9 11.1 %convolution_convert_fusion = bf16[3072,768]{0,1:T(8,128)(2,1)} fusion(bf16[1280,768]{1,0:T(8,128)(2,1)} %get-tuple-element.62, f32[1280,3072]{1,0:T(8,128)S(1)} %copy-done.36), kind=kOutput, calls=%fused_computation.21 | convolution fusion | flops 6077546496 | bytes 22413312 | tf_op jit(solution)/shard_map/dot_general | solution.py:245
  202.1 1.9 fusion.18
  204.0 17.6 %fusion.6 = bf16[1280,3072]{1,0:T(8,128)(2,1)S(1)} fusion(f32[1280,3072]{1,0:T(8,128)} %fusion.16, bf16[1280,768]{1,0:T(8,128)(2,1)S(1)} %bitcast.94, bf16[1,3072,768]{2,1,0:T(8,128)(2,1)} %param.24), kind=kOutput, calls=%fused_computation.8 | convolution fusion | flops 6118440960 | bytes 30277632 | tf_op jit(solution)/shard_map/dot_general | solution.py:245
  221.6 11.7 %fusion.14 = f32[1280,768]{1,0:T(8,128)S(1)} fusion(bf16[1280,3072]{1,0:T(8,128)(2,1)S(1)} %fusion.6, bf16[1,768,3072]{2,1,0:T(8,128)(2,1)} %param.23), kind=kOutput, calls=%fused_computation.26 | convolution fusion | flops 6039797760 | bytes 16515072 | tf_op jit(solution)/shard_map/dot_general | solution.py:245
  233.4 2.1 fusion.24
  235.5 5.1 all-to-all-start.3
  240.5 12.0 %convolution_convert_fusion.1 = bf16[768,3072]{1,0:T(8,128)(2,1)} fusion(bf16[1280,768]{1,0:T(8,128)(2,1)S(1)} %bitcast.88, bf16[1280,3072]{1,0:T(8,128)(2,1)} %copy-done.35), kind=kOutput, calls=%fused_computation.22 | convolution fusion | flops 6042157056 | bytes 14548992 | tf_op jit(solution)/shard_map/dot_general | solution.py:245
  252.5 1.7 copy.38
  254.3 2.4 fusion.62
  256.8 29.3 %all-to-all-done.3 = bf16[8,160,768]{2,1,0:T(8,128)(2,1)} async-done(((bf16[8,160,768]{2,1,0:T(8,128)(2,1)}), bf16[8,160,768]{2,1,0:T(8,128)(2,1)}, u32[]{:S(2)}, u32[]{:S(2)}) %all-to-all-start.3) | async-done | bytes 1966112 | tf_op jit(solution)/shard_map/all_to_all | solution.py:270
  286.0 5.1 all-to-all-start.1
  291.2 0.2 all-reduce.4.cloned.1.call-start
  291.4 5.6 multiply_reduce_fusion
  297.0 0.9 subtract_add_fusion
  297.9 0.4 copy-done.30
  298.3 2.6 convolution_convert_fusion.2.g_ref
  300.9 57.5 %attend_back.1 = (bf16[1024,768]{1,0:T(8,128)(2,1)}, bf16[1024,768]{1,0:T(8,128)(2,1)}, bf16[1024,768]{1,0:T(8,128)(2,1)}, f32[6,8,2048]{2,1,0:T(8,128)}) custom-call(bf16[1024,768]{1,0:T(8,128)(2,1)} %copy-done.5, bf16[1024,768]{1,0:T(8,128)(2,1)} %copy-done.4, bf16[1024,768]{1,0:T(8,128)(2,1)} %convolution_convert_fusion.3.v_ref, ...), custom_call_target="tpu_custom_call" | custom-call | flops 32212254720 | bytes 15728640 | tf_op jit(solution)/shard_map/attend_back/pallas_call | solution.py:194
  358.4 4.4 fusion.57
  362.8 2.8 fusion.55
  365.6 2.8 fusion.53
  368.5 2.9 fusion.40
  371.4 2.0 fusion.64
  373.4 6.0 %add_convert_fusion = bf16[1024,768]{0,1:T(8,128)(2,1)} fusion(f32[1024,768]{0,1:T(8,128)} %copy-done.10, f32[1024]{0:T(1024)S(1)} %select_reduce_fusion, bf16[1280,768]{1,0:T(8,128)(2,1)} %bitcast.9, s32[1024]{0:T(1024)S(1)} %add_select_fusion), kind=kOutput, calls=%fused_computation.54 | convolution fusion | flops 2016935936 | bytes 6692864 | tf_op jit(solution)/shard_map/dot_general | solution.py:245
  379.4 2.9 copy.44
  382.2 1.0 slice.11
  383.3 3.3 fusion.65
  386.7 1.4 fusion.66
  388.2 2.1 fusion.35
  390.2 2.6 fusion.32
  392.9 3.6 copy.45
  396.6 42.7 %all-reduce = (f32[32,12]{0,1:T(8,128)}, f32[768]{0:T(1024)}, f32[768]{0:T(1024)}, f32[768,8]{0,1:T(8,128)}) all-reduce(f32[32,12]{0,1:T(8,128)S(1)} %fusion.43, f32[768]{0:T(1024)S(1)} %get-tuple-element.52, f32[768]{0:T(1024)S(1)} %get-tuple-element.50, f32[768,8]{0,1:T(8,128)S(1)} %fusion.64), channel_id=1, replica_groups=mesh['dp'=4,'expert'=8] {'dp','expert'}, use_global_device_ids=true, to_apply=%region_18.19 | all-reduce | flops 8064 | bytes 64512 | tf_op jit(solution)/shard_map/psum | solution.py:346
  439.4 2.9 bitcast_convert_fusion
  442.3 3.0 bitcast_convert_fusion.1
  445.3 119.9 %all-reduce.4.cloned.1.call-done = (f32[768,768]{1,0:T(8,128)}, f32[768,768]{1,0:T(8,128)}, f32[768,768]{1,0:T(8,128)}, f32[768,768]{1,0:T(8,128)}) async-done(((f32[768,768]{1,0:T(8,128)}, f32[768,768]{1,0:T(8,128)}, f32[768,768]{1,0:T(8,128)}, f32[768,768]{1,0:T(8,128)}), (f32[768,768]{1,0:T(8,128)}, f32[768,768]{1,0:T(8,128)}, f32[768,768]{1,0:T(8,128)}, ...) | async-done | bytes 9437200 | tf_op jit(solution)/shard_map/psum | solution.py:346
  565.2 3.4 copy.57
  568.5 1.4 copy.58
  569.9 1.1 copy-done.17
  571.1 1.4 copy.59
  572.5 1.1 copy-done.16
  573.6 1.4 copy.60
  (95 shorter events, 1.2 us)
Async XLA Ops:
  8.0 12.5 %copy-start = (bf16[768,768]{1,0:T(8,128)(2,1)S(1)}, bf16[768,768]{1,0:T(8,128)(2,1)}, u32[]{:S(2)}) copy-start(bf16[768,768]{1,0:T(8,128)(2,1)} %param.18) | copy-start | bytes 3538948
  8.0 9.7 %copy-start.25 = (f32[768]{0:T(1024)S(1)}, f32[768]{0:T(1024)}, u32[]{:S(2)}) copy-start(f32[768]{0:T(1024)} %param.15) | copy-start | bytes 9220
  9.0 5.8 copy-start.22
  14.9 10.0 %copy-start.1 = (f32[6,2,2048]{2,1,0:T(2,128)}, f32[6,2,2048]{2,1,0:T(2,128)S(1)}, u32[]{:S(2)}) copy-start(f32[6,2,2048]{2,1,0:T(2,128)S(1)} %reshape.144.u_ref) | copy-start | bytes 294916
  16.6 50.4 %copy-start.7 = (bf16[1024,768]{0,1:T(8,128)(2,1)}, bf16[1024,768]{0,1:T(8,128)(2,1)S(1)}, u32[]{:S(2)}) copy-start(bf16[1024,768]{0,1:T(8,128)(2,1)S(1)} %copy.36) | copy-start | bytes 4718596
  17.7 5.5 copy-start.19
  20.6 4.3 copy-start.4
  20.6 2.7 copy-start.31
  24.8 42.2 %copy-start.5 = (bf16[1024,768]{1,0:T(8,128)(2,1)}, bf16[1024,768]{1,0:T(8,128)(2,1)S(1)}, u32[]{:S(2)}) copy-start(bf16[1024,768]{1,0:T(8,128)(2,1)S(1)} %convolution_convert_fusion.5.q_ref) | copy-start | bytes 4718596
  24.8 42.2 %copy-start.29 = (bf16[768,768]{1,0:T(8,128)(2,1)S(1)}, bf16[768,768]{1,0:T(8,128)(2,1)}, u32[]{:S(2)}) copy-start(bf16[768,768]{1,0:T(8,128)(2,1)} %param.19) | copy-start | bytes 3538948
  67.0 1.6 copy-start.2
  67.0 1.6 copy-start.6
  67.1 1.6 copy-start.27
  68.7 3.9 copy-start.10
  72.6 51.8 %all-to-all-start = ((bf16[8,160,768]{2,1,0:T(8,128)(2,1)}), bf16[8,160,768]{2,1,0:T(8,128)(2,1)S(1)}, u32[]{:S(2)}, u32[]{:S(2)}) async-start(bf16[8,160,768]{2,1,0:T(8,128)(2,1)} %bitcast.93), calls=%async_computation | async-start | bytes 3932160 | tf_op jit(solution)/shard_map/all_to_all | solution.py:270
  84.0 45.4 %copy-start.21 = (bf16[768,8]{0,1:T(8,128)(2,1)S(1)}, bf16[768,8]{0,1:T(8,128)(2,1)}, u32[]{:S(2)}) copy-start(bf16[768,8]{0,1:T(8,128)(2,1)} %param.22) | copy-start | bytes 36868
  124.3 116.2 %copy-start.9 = (bf16[8,160,768]{2,1,0:T(8,128)(2,1)}, bf16[8,160,768]{2,1,0:T(8,128)(2,1)S(1)}, u32[]{:S(2)}) copy-start(bf16[8,160,768]{2,1,0:T(8,128)(2,1)S(1)} %all-to-all-done) | copy-start | bytes 5898244
  124.3 50.6 %all-to-all-start.2 = ((bf16[8,160,768]{2,1,0:T(8,128)(2,1)}), bf16[8,160,768]{2,1,0:T(8,128)(2,1)}, u32[]{:S(2)}, u32[]{:S(2)}) async-start(bf16[8,160,768]{2,1,0:T(8,128)(2,1)} %bitcast.92), calls=%async_computation.2 | async-start | bytes 3932160 | tf_op jit(solution)/shard_map/all_to_all | solution.py:270
  129.4 309.9 %reduce-scatter.5.cloned.1.call-start = ((), (), s32[]{:S(2)}) async-start(), calls=%async_computation.7 | async-start | bytes 5898240 | tf_op jit(solution)/shard_map/reduce_scatter | solution.py:317
  174.9 15.9 %copy-start.36 = (f32[1280,3072]{1,0:T(8,128)S(1)}, f32[1280,3072]{1,0:T(8,128)}, u32[]{:S(2)}) copy-start(f32[1280,3072]{1,0:T(8,128)} %fusion.16) | copy-start | bytes 47185924
  221.6 11.7 %copy-start.35 = (bf16[1280,3072]{1,0:T(8,128)(2,1)}, bf16[1280,3072]{1,0:T(8,128)(2,1)S(1)}, u32[]{:S(2)}) copy-start(bf16[1280,3072]{1,0:T(8,128)(2,1)S(1)} %fusion.6) | copy-start | bytes 23592964
  235.5 50.6 %all-to-all-start.3 = ((bf16[8,160,768]{2,1,0:T(8,128)(2,1)}), bf16[8,160,768]{2,1,0:T(8,128)(2,1)}, u32[]{:S(2)}, u32[]{:S(2)}) async-start(bf16[8,160,768]{2,1,0:T(8,128)(2,1)} %bitcast.90), calls=%async_computation.3 | async-start | bytes 3932160 | tf_op jit(solution)/shard_map/all_to_all | solution.py:270
  240.5 201.8 %reduce-scatter.3.cloned.1.call-start = ((), (), s32[]{:S(2)}) async-start(), calls=%async_computation.6 | async-start | bytes 5898240 | tf_op jit(solution)/shard_map/reduce_scatter | solution.py:316
  252.5 4.2 copy-start.24
  286.0 87.3 %all-to-all-start.1 = ((bf16[8,160,768]{2,1,0:T(8,128)(2,1)}), bf16[8,160,768]{2,1,0:T(8,128)(2,1)}, u32[]{:S(2)}, u32[]{:S(2)}) async-start(bf16[8,160,768]{2,1,0:T(8,128)(2,1)} %bitcast.91), calls=%async_computation.1 | async-start | bytes 3932160 | tf_op jit(solution)/shard_map/all_to_all | solution.py:270
  291.2 274.0 %all-reduce.4.cloned.1.call-start = ((), (), s32[]{:S(2)}) async-start(), calls=%async_computation.8 | async-start | bytes 18874368 | tf_op jit(solution)/shard_map/psum | solution.py:346
  291.4 5.7 copy-start.11
  297.0 1.3 copy-start.30
  298.3 70.2 %copy-start.12 = (f32[1024,768]{0,1:T(8,128)}, f32[1024,768]{0,1:T(8,128)S(1)}, u32[]{:S(2)}) copy-start(f32[1024,768]{0,1:T(8,128)S(1)} %subtract_add_fusion) | copy-start | bytes 9437188
  300.9 57.5 %copy-start.8 = (bf16[1024,768]{0,1:T(8,128)(2,1)S(1)}, bf16[1024,768]{0,1:T(8,128)(2,1)}, u32[]{:S(2)}) copy-start(bf16[1024,768]{0,1:T(8,128)(2,1)} %copy-done.7) | copy-start | bytes 4718596
  300.9 57.5 %copy-start.20 = (f32[1024]{0:T(1024)S(1)}, f32[1024]{0:T(1024)}, u32[]{:S(2)}) copy-start(f32[1024]{0:T(1024)} %copy-done.19) | copy-start | bytes 12292
  300.9 57.5 %copy-start.26 = (f32[768]{0:T(1024)S(1)}, f32[768]{0:T(1024)}, u32[]{:S(2)}) copy-start(f32[768]{0:T(1024)} %param.15) | copy-start | bytes 9220
  358.4 4.4 copy-start.33
  362.8 2.9 copy-start.14
  365.6 2.8 copy-start.3
  383.3 3.4 copy-start.32
  383.3 3.4 copy-start.34
  386.7 1.5 copy-start.15
  388.2 2.1 copy-start.13
  388.2 2.1 copy-start.28
  392.9 3.6 copy-start.23
  565.2 3.4 copy-start.18
  568.5 2.5 copy-start.17
  571.1 2.5 copy-start.16
Sparse Core Ops, SparseCore 0:
  202.1 56.1 reduce-scatter.4
  261.6 57.0 reduce-scatter.2
Sparse Core Ops, SparseCore 1:
  371.5 193.6 all-reduce.3

commit v2 on v1

--- a/solution.py
+++ b/solution.py
@@ -1,3 +1,5 @@
+import functools
+
 import jax
 import jax.numpy as jnp
 from jax import lax
@@ -12,6 +14,10 @@
 
 def dot_f32(left, right):
     return lax.dot_general(left, right, (((1,), (0,)), ((), ())), preferred_element_type=f32)
+
+
+def dot_nt(left, right):
+    return lax.dot_general(left, right, (((1,), (1,)), ((), ())), preferred_element_type=f32)
 
 
 def fill_toeplitz(base_ref, head, row):
@@ -223,6 +229,483 @@
     )(q, k, v, g, u, ctxt, lse)
 
 
+def gelu_both(v):
+    scale = 0.7978845608028654
+    square = v * v
+    t = jnp.tanh(scale * v * (1.0 + 0.044715 * square))
+    half = 0.5 * (1.0 + t)
+    slope = half + 0.5 * v * (1.0 - t * t) * (scale * (1.0 + 3 * 0.044715 * square))
+    return v * half, slope
+
+
+def expert_kernel(
+    experts, capacity, tile,
+    xs, gr_h, win_h, wout_h, rw,
+    gback_o, prod_o, dwin_o, dwout_o, drw_o,
+    xall, gr, gp, win, wout, act, gpre, gback, gsend, prod, logit, acc_p, acc_g, xt, gpt, stage,
+    send_x, recv_x, send_g, recv_g, local, out_sem,
+):
+    me = lax.axis_index("expert")
+    place = me // 2
+    chips = experts // 2
+    span = 2 * capacity
+    width = xall.shape[1]
+    hidden = win.shape[1]
+    barrier = pltpu.get_barrier_semaphore()
+    for k in range(1, experts):
+        pl.semaphore_signal(barrier, inc=1, device_id={"expert": lax.rem(me + k, experts)})
+    loads = [
+        pltpu.make_async_copy(win_h, win, local.at[0]),
+        pltpu.make_async_copy(wout_h, wout, local.at[1]),
+        pltpu.make_async_copy(gr_h, gr, local.at[2]),
+    ]
+    rows_of = lambda who: pl.ds(pl.multiple_of(who * capacity, 16), capacity)
+    own = pltpu.make_async_copy(xs.at[rows_of(me), :], xall.at[rows_of(me), :], local.at[3])
+    own.start()
+    for copy in loads:
+        copy.start()
+    pl.semaphore_wait(barrier, experts - 1)
+
+    def partner(step):
+        flip = lax.rem(chips - step, chips)
+        high, low = place // 2, lax.rem(place, 2)
+        fhigh, flow = flip // 2, lax.rem(flip, 2)
+        return 2 * (high + fhigh - 2 * high * fhigh) + low + flow - 2 * low * flow
+
+    def send_rows(peer):
+        return pltpu.make_async_remote_copy(
+            src_ref=xs.at[rows_of(peer), :], dst_ref=xall.at[rows_of(me), :],
+            send_sem=send_x.at[peer], recv_sem=recv_x.at[me], device_id={"expert": peer},
+        )
+
+    def got_rows(peer):
+        return pltpu.make_async_remote_copy(
+            src_ref=xs.at[rows_of(peer), :], dst_ref=xall.at[rows_of(peer), :],
+            send_sem=send_x.at[peer], recv_sem=recv_x.at[peer], device_id={"expert": peer},
+        )
+
+    def send_back(peer):
+        return pltpu.make_async_remote_copy(
+            src_ref=gsend.at[rows_of(peer), :], dst_ref=gback.at[rows_of(me), :],
+            send_sem=send_g.at[peer], recv_sem=recv_g.at[me], device_id={"expert": peer},
+        )
+
+    def got_back(peer):
+        return pltpu.make_async_remote_copy(
+            src_ref=gsend.at[rows_of(peer), :], dst_ref=gback.at[rows_of(peer), :],
+            send_sem=send_g.at[peer], recv_sem=recv_g.at[peer], device_id={"expert": peer},
+        )
+
+    sibling = me + 1 - 2 * lax.rem(me, 2)
+    send_rows(sibling).start()
+    for step in range(1, chips):
+        for core in range(2):
+            send_rows(2 * partner(step) + lax.rem(me + core, 2)).start()
+    for copy in loads:
+        copy.wait()
+
+    lanes = lax.broadcasted_iota(jnp.int32, (span, rw.shape[1]), 1)
+    mine = jnp.where(lanes == me, 1.0, 0.0)
+
+    def work(step, carry):
+        where = partner(step)
+        base = pl.multiple_of(where * span, 32)
+
+        @pl.when(step == 0)
+        def _():
+            own.wait()
+            got_rows(sibling).wait_recv()
+
+        @pl.when(step > 0)
+        def _():
+            got_rows(2 * where).wait_recv()
+            got_rows(2 * where + 1).wait_recv()
+
+        rows = pl.ds(base, span)
+        x = xall[rows, :]
+        logits = jnp.where(lanes < experts, dot_f32(x, rw[...]), -1e30)
+        weights = jnp.exp(logits - jnp.max(logits, axis=-1, keepdims=True))
+        probs = weights / jnp.sum(weights, axis=-1, keepdims=True)
+        gate = jnp.sum(probs * mine, axis=-1, keepdims=True)
+        gp[rows, :] = (gr[rows, :].astype(f32) * gate).astype(bf16)
+        acc_p[...] = jnp.zeros_like(acc_p)
+        acc_g[...] = jnp.zeros_like(acc_g)
+
+        def block(idx, carry):
+            cols = pl.ds(pl.multiple_of(idx * tile, tile), tile)
+            h = dot_f32(xall[rows, :], win[:, cols])
+            grad = dot_nt(gp[rows, :], wout[cols, :])
+            value, slope = gelu_both(h)
+            value = value.astype(bf16)
+            grad = (grad * slope).astype(bf16)
+            act[rows, cols] = value
+            gpre[rows, cols] = grad
+            acc_p[...] += dot_f32(value, wout[cols, :])
+            acc_g[...] += dot_nt(grad, win[:, cols])
+            return carry
+
+        lax.fori_loop(0, hidden // tile, block, 0)
+        made = acc_p[...].astype(bf16)
+        prod[rows, :] = made
+        gate_grad = jnp.sum(gr[rows, :].astype(f32) * made.astype(f32), axis=-1, keepdims=True)
+        low = (gate_grad * gate * (mine - probs)).astype(bf16)
+        low = jnp.where(lanes < experts, low, jnp.zeros_like(low))
+        logit[rows, :] = low
+        gsend[rows, :] = (acc_g[...] + dot_nt(low, rw[...])).astype(bf16)
+
+        @pl.when(step == 0)
+        def _():
+            send_back(sibling).start()
+
+        @pl.when(step > 0)
+        def _():
+            send_back(2 * where).start()
+            send_back(2 * where + 1).start()
+
+        return carry
+
+    lax.fori_loop(0, chips, work, 0)
+    outs = [
+        pltpu.make_async_copy(prod, prod_o, local.at[0]),
+        pltpu.make_async_copy(gsend.at[rows_of(me), :], gback.at[rows_of(me), :], local.at[3]),
+    ]
+    for copy in outs:
+        copy.start()
+    xt[...] = xall[...].T
+    gpt[...] = gp[...].T
+    drw_o[...] = dot_f32(xt[...], logit[...])
+
+    def weight_block(idx, carry):
+        cols = pl.ds(pl.multiple_of(idx * tile, tile), tile)
+
+        def put(slot, out):
+            return pltpu.make_async_copy(stage.at[slot], out.at[:, cols], out_sem.at[slot])
+
+        for slot, (left, right, out) in enumerate(((gpt, act, dwout_o), (xt, gpre, dwin_o))):
+            @pl.when(idx > 0)
+            def _():
+                put(slot, out).wait()
+
+            stage[slot] = dot_f32(left[...], right[:, cols]).astype(bf16)
+            put(slot, out).start()
+        return carry
+
+    lax.fori_loop(0, hidden // tile, weight_block, 0)
+    for slot, out in enumerate((dwout_o, dwin_o)):
+        pltpu.make_async_copy(stage.at[slot], out.at[:, 0:tile], out_sem.at[slot]).wait()
+    for copy in outs:
+        copy.wait()
+    for k in range(1, experts):
+        peer = lax.rem(me + k, experts)
+        got_rows(peer).wait_send()
+        got_back(peer).wait_send()
+        got_back(peer).wait_recv()
+    back = pltpu.make_async_copy(gback, gback_o, local.at[1])
+    back.start()
+    back.wait()
+
+
+def expert_pass(xs, gr, weight_in, weight_out, router_pad, experts, capacity):
+    slots, width = xs.shape
+    hidden = weight_in.shape[1]
+    tile = 512
+    span = 2 * capacity
+    hbm = pl.BlockSpec(memory_space=pl.ANY)
+    vmem = pl.BlockSpec(memory_space=pltpu.VMEM)
+    return pl.pallas_call(
+        functools.partial(expert_kernel, experts, capacity, tile),
+        in_specs=[hbm, hbm, hbm, hbm, vmem],
+        out_specs=[hbm, hbm, hbm, hbm, vmem],
+        out_shape=[
+            jax.ShapeDtypeStruct((slots, width), bf16),
+            jax.ShapeDtypeStruct((slots, width), bf16),
+            jax.ShapeDtypeStruct((width, hidden), bf16),
+            jax.ShapeDtypeStruct((width, hidden), bf16),
+            jax.ShapeDtypeStruct((width, router_pad.shape[1]), f32),
+        ],
+        scratch_shapes=[
+            pltpu.VMEM((slots, width), bf16),
+            pltpu.VMEM((slots, width), bf16),
+            pltpu.VMEM((slots, width), bf16),
+            pltpu.VMEM((width, hidden), bf16),
+            pltpu.VMEM((hidden, width), bf16),
+            pltpu.VMEM((slots, hidden), bf16),
+            pltpu.VMEM((slots, hidden), bf16),
+            pltpu.VMEM((slots, width), bf16),
+            pltpu.VMEM((slots, width), bf16),
+            pltpu.VMEM((slots, width), bf16),
+            pltpu.VMEM((slots, router_pad.shape[1]), bf16),
+            pltpu.VMEM((span, width), f32),
+            pltpu.VMEM((span, width), f32),
+            pltpu.VMEM((width, slots), bf16),
+            pltpu.VMEM((width, slots), bf16),
+            pltpu.VMEM((2, width, tile), bf16),
+            pltpu.SemaphoreType.DMA((experts,)),
+            pltpu.SemaphoreType.DMA((experts,)),
+            pltpu.SemaphoreType.DMA((experts,)),
+            pltpu.SemaphoreType.DMA((experts,)),
+            pltpu.SemaphoreType.DMA((4,)),
+            pltpu.SemaphoreType.DMA((2,)),
+        ],
+        compiler_params=pltpu.CompilerParams(
+            vmem_limit_bytes=60 << 20, collective_id=1, has_side_effects=True
+        ),
+        cost_estimate=pl.CostEstimate(
+            flops=12 * slots * width * hidden, bytes_accessed=8 * width * hidden, transcendentals=slots * hidden
+        ),
+        name="experts",
+    )(xs, gr, weight_in, weight_out, router_pad)
+
+
+def remote(src, dst, send_sem, recv_sem, axis, peer):
+    return pltpu.make_async_remote_copy(
+        src_ref=src, dst_ref=dst, send_sem=send_sem, recv_sem=recv_sem, device_id={axis: peer}
+    )
+
+
+def tail_kernel(
+    groups, experts,
+    tok, gain, nl, dq, dk, dv, wq, wk, wv, ghid, dwo, small,
+    wout_o, ing_o, small_o,
+    part, r1, s1, r2, r3, s3, g4, full, nt, sbuf, srecv, sone, stwo,
+    send1, recv1, send2, recv2, send3, recv3, send4, recv4, send5, recv5, send6, recv6, send7, recv7,
+):
+    me = lax.axis_index("expert")
+    my_dp = lax.axis_index("dp")
+    core = lax.rem(me, 2)
+    place = me // 2
+    chips = experts // 2
+    sibling = me + 1 - 2 * core
+    width = part.shape[2]
+    half = width // 2
+    piece = half // groups
+    barrier = pltpu.get_barrier_semaphore()
+    for k in range(1, experts):
+        pl.semaphore_signal(barrier, inc=1, device_id={"expert": lax.rem(me + k, experts)})
+    for k in range(1, groups):
+        pl.semaphore_signal(barrier, inc=1, device_id={"dp": lax.rem(my_dp + k, groups)})
+
+    def half_rows(which):
+        return pl.ds(pl.multiple_of(which * half, 16), half)
+
+    def piece_rows(which):
+        return pl.ds(pl.multiple_of(which * piece, 16), piece)
+
+    def copy1(c):
+        return remote(part.at[c, half_rows(1 - core), :], r1.at[c], send1.at[c], recv1.at[c], "expert", sibling)
+
+    def copy2(c, peer, slot):
+        return remote(s1.at[c, piece_rows(peer), :], r2.at[c, slot], send2.at[c, peer], recv2.at[c, slot], "dp", peer)
+
+    def copy3(c, peer, slot):
+        return remote(
+            r3.at[c, place], r3.at[c, slot], send3.at[c, peer], recv3.at[c, slot], "expert", 2 * peer + core
+        )
+
+    def copy4(c, peer, slot):
+        return remote(
+            g4.at[c, piece_rows(my_dp), :], g4.at[c, piece_rows(slot), :],
+            send4.at[c, peer], recv4.at[c, slot], "dp", peer,
+        )
+
+    def copy5(c):
+        return remote(
+            full.at[c, half_rows(core), :], full.at[c, half_rows(core), :], send5.at[c], recv5.at[c], "expert", sibling
+        )
+
+    def got5(c):
+        return remote(
+            full.at[c, half_rows(1 - core), :], full.at[c, half_rows(1 - core), :],
+            send5.at[c], recv5.at[c], "expert", sibling,
+        )
+
+    def others(count, mine):
+        return [lax.rem(mine + k, count) for k in range(1, count)]
+
+    def stage1(c):
+        copy1(c).start()
+
+    def stage2(c):
+        copy1(c).wait_recv()
+        s1[c] = (part[c, half_rows(core), :].astype(f32) + r1[c].astype(f32)).astype(bf16)
+        for peer in others(groups, my_dp):
+            copy2(c, peer, my_dp).start()
+
+    def stage3(c):
+        total = s1[c, piece_rows(my_dp), :].astype(f32)
+        for peer in others(groups, my_dp):
+            copy2(c, peer, peer).wait_recv()
+            total = total + r2[c, peer].astype(f32)
+        r3[c, place] = total.astype(bf16)
+        for peer in others(chips, place):
+            copy3(c, peer, place).start()
+
+    def stage4(c):
+        for peer in others(chips, place):
+            copy3(c, peer, peer).wait_recv()
+        total = r3[c, 0].astype(f32)
+        for slot in range(1, chips):
+            total = total + r3[c, slot].astype(f32)
+        g4[c, piece_rows(my_dp), :] = total.astype(bf16)
+        for peer in others(groups, my_dp):
+            copy4(c, peer, my_dp).start()
+
+    def stage5(c):
+        for peer in others(groups, my_dp):
+            copy4(c, peer, peer).wait_recv()
+        full[c, half_rows(core), :] = g4[c]
+        copy5(c).start()
+
+    def stage6(c):
+        got5(c).wait_recv()
+        wout_o[c] = full[c]
+
+    def finish(c):
+        copy1(c).wait_send()
+        for peer in others(groups, my_dp):
+            copy2(c, peer, my_dp).wait_send()
+            copy4(c, peer, my_dp).wait_send()
+        for peer in others(chips, place):
+            copy3(c, peer, place).wait_send()
+        copy5(c).wait_send()
+
+    def weight_grad(c, grad):
+        def block(idx, carry):
+            rows = pl.ds(pl.multiple_of(idx * 256, 256), 256)
+            part[c, rows, :] = dot_f32(nt[rows, :], grad[...]).astype(bf16)
+            return carry
+
+        lax.fori_loop(0, width // 256, block, 0)
+
+    rows_total = tok.shape[0]
+    part[0] = dwo[...]
+    nt[...] = nl[...].T
+    pl.semaphore_wait(barrier, experts + groups - 2)
+    stage1(0)
+    weight_grad(1, dq)
+    stage1(1)
+    stage2(0)
+    weight_grad(2, dk)
+    stage1(2)
+    stage2(1)
+    stage3(0)
+    weight_grad(3, dv)
+    stage1(3)
+    stage2(2)
+    stage3(1)
+    stage4(0)
+
+    def token_block(idx, carry):
+        rows = pl.ds(pl.multiple_of(idx * 256, 256), 256)
+        grad = dot_nt(dq[rows, :], wq[...]) + dot_nt(dk[rows, :], wk[...]) + dot_nt(dv[rows, :], wv[...])
+        values = tok[rows, :].astype(f32)
+        scale = lax.rsqrt(jnp.mean(values * values, axis=-1, keepdims=True) + epsilon)
+        weighted = grad * gain[...]
+        inner = jnp.mean(weighted * values, axis=-1, keepdims=True)
+        ing_o[rows, :] = ghid[rows, :] + scale * weighted - values * (scale * scale * scale * inner)
+        return carry + jnp.sum(grad * values * scale, axis=0, keepdims=True)
+
+    gain_grad = jnp.zeros((1, width), f32)
+    gain_grad = lax.fori_loop(0, rows_total // 512, token_block, gain_grad)
+    stage2(3)
+    stage3(2)
+    stage4(1)
+    stage5(0)
+    gain_grad = lax.fori_loop(rows_total // 512, rows_total // 256, token_block, gain_grad)
+
+    sbuf[...] = small[...]
+    sbuf[0:1, :] = gain_grad
+    srecv[me] = sbuf[...]
+
+    def copy6(peer, slot):
+        return remote(sbuf, srecv.at[slot], send6.at[peer], recv6.at[slot], "expert", peer)
+
+    def copy7(peer, slot):
+        return remote(sone, stwo.at[slot], send7.at[peer], recv7.at[slot], "dp", peer)
+
+    for peer in others(experts, me):
+        copy6(peer, me).start()
+    stage3(3)
+    stage4(2)
+    stage5(1)
+    stage6(0)
+    for peer in others(experts, me):
+        copy6(peer, peer).wait_recv()
+    total = srecv[0]
+    for slot in range(1, experts):
+        total = total + srecv[slot]
+    sone[...] = total
+    stwo[my_dp] = total
+    for peer in others(groups, my_dp):
+        copy7(peer, my_dp).start()
+    stage4(3)
+    stage5(2)
+    stage6(1)
+    stage5(3)
+    stage6(2)
+    for peer in others(groups, my_dp):
+        copy7(peer, peer).wait_recv()
+    total = stwo[0]
+    for slot in range(1, groups):
+        total = total + stwo[slot]
+    small_o[...] = total
+    stage6(3)
+    for c in range(4):
+        finish(c)
+    for peer in others(experts, me):
+        copy6(peer, me).wait_send()
+    for peer in others(groups, my_dp):
+        copy7(peer, my_dp).wait_send()
+
+
+def tail(tokens, gain, normed_low, dq, dk, dv, wq, wk, wv, grad_hidden, dwo, small, groups, experts):
+    rows, width = tokens.shape
+    half = width // 2
+    piece = half // groups
+    chips = experts // 2
+    vmem = pl.BlockSpec(memory_space=pltpu.VMEM)
+    dma = pltpu.SemaphoreType.DMA
+    return pl.pallas_call(
+        functools.partial(tail_kernel, groups, experts),
+        in_specs=[vmem] * 12,
+        out_specs=[vmem] * 3,
+        out_shape=[
+            jax.ShapeDtypeStruct((4, width, width), bf16),
+            jax.ShapeDtypeStruct((rows, width), f32),
+            jax.ShapeDtypeStruct(small.shape, f32),
+        ],
+        scratch_shapes=[
+            pltpu.VMEM((4, width, width), bf16),
+            pltpu.VMEM((4, half, width), bf16),
+            pltpu.VMEM((4, half, width), bf16),
+            pltpu.VMEM((4, groups, piece, width), bf16),
+            pltpu.VMEM((4, chips, piece, width), bf16),
+            pltpu.VMEM((4, piece, width), bf16),
+            pltpu.VMEM((4, half, width), bf16),
+            pltpu.VMEM((4, width, width), bf16),
+            pltpu.VMEM((width, rows), bf16),
+            pltpu.VMEM(small.shape, f32),
+            pltpu.VMEM((experts,) + small.shape, f32),
+            pltpu.VMEM(small.shape, f32),
+            pltpu.VMEM((groups,) + small.shape, f32),
+            dma((4,)), dma((4,)),
+            dma((4, groups)), dma((4, groups)),
+            dma((4, chips)), dma((4, chips)),
+            dma((4, groups)), dma((4, groups)),
+            dma((4,)), dma((4,)),
+            dma((experts,)), dma((experts,)),
+            dma((groups,)), dma((groups,)),
+        ],
+        compiler_params=pltpu.CompilerParams(
+            vmem_limit_bytes=60 << 20, collective_id=2, has_side_effects=True
+        ),
+        cost_estimate=pl.CostEstimate(
+            flops=12 * rows * width * width, bytes_accessed=20 * rows * width, transcendentals=rows
+        ),
+        name="tail",
+    )(tokens, gain, normed_low, dq, dk, dv, wq, wk, wv, grad_hidden, dwo, small)
+
+
 def rms_backward(grad_norm, values, row_scale, gain_vec):
     weighted = grad_norm * gain_vec
     gain_grad = jnp.sum(grad_norm * values * row_scale, axis=0)
@@ -245,17 +728,60 @@
     return lax.dot_general(left, right, (((dims[0],), (dims[1],)), ((), ())), preferred_element_type=f32)
 
 
+def exchange(rows, experts):
+    slots, width = rows.shape
+    rows = rows.reshape(experts, slots // experts, width)
+    return lax.all_to_all(rows, "expert", split_axis=0, concat_axis=0, tiled=True).reshape(slots, width)
+
+
+def expert_native(send, grad_recv, weight_in, weight_out, router_w, experts):
+    received = exchange(send, experts)
+    own = lax.axis_index("expert")
+    own_hot = (jnp.arange(experts, dtype=jnp.int32) == own).astype(f32)[None, :]
+    probs = jax.nn.softmax(contract(received, router_w, (1, 0)), axis=-1)
+    gate = jnp.sum(probs * own_hot, axis=-1, keepdims=True)
+    grad_recv_f = grad_recv.astype(f32)
+    grad_produced = (grad_recv_f * gate).astype(bf16)
+    preact = contract(received, weight_in, (1, 0))
+    gelu_values, gelu_pullback = jax.vjp(gelu_tanh, preact)
+    active = gelu_values.astype(bf16)
+    produced = contract(active, weight_out, (1, 0)).astype(bf16)
+    gate_grad = jnp.sum(grad_recv_f * produced.astype(f32), axis=-1, keepdims=True)
+    logit_low = (gate_grad * gate * (own_hot - probs)).astype(bf16)
+    grad_active = contract(grad_produced, weight_out, (1, 1))
+    grad_preact = gelu_pullback(grad_active)[0].astype(bf16)
+    grad_received = contract(grad_preact, weight_in, (1, 1)) + contract(logit_low, router_w, (1, 1))
+    grad_rows = exchange(grad_received.astype(bf16), experts)
+    in_grad = contract(received, grad_preact, (0, 0)).astype(bf16)
+    out_grad_t = contract(grad_produced, active, (0, 0)).astype(bf16)
+    router_grad = contract(received, logit_low, (0, 0))
+    return grad_rows, produced, in_grad, out_grad_t, router_grad
+
+
+def tail_native(tokens, gain, normed_low, dq, dk, dv, wq, wk, wv, grad_hidden, dwo, small):
+    tokens_f = tokens.astype(f32)
+    grads = jnp.stack([dwo.astype(f32)] + [contract(normed_low, d, (0, 0)) for d in (dq, dk, dv)])
+    grad_normed = contract(dq, wq, (1, 1)) + contract(dk, wk, (1, 1)) + contract(dv, wv, (1, 1))
+    _, scale = rms_forward(tokens_f, gain)
+    grad_tokens, gain_grad = rms_backward(grad_normed, tokens_f, scale, gain)
+    small = jnp.concatenate([gain_grad[None], small[1:]])
+    grads, small = lax.psum((grads, small), ("dp", "expert"))
+    return grads, grad_hidden + grad_tokens, small
+
+
 def on_device(
     tokens, gain_one, query_w, key_w, value_w, out_w, rel_table, gain_two, router_w,
     expert_in, expert_out, routes, buckets, cotangent,
 ):
     seq_len, width = tokens.shape
     heads = rel_table.shape[1]
+    groups = lax.axis_size("dp")
     experts = lax.axis_size("expert")
     capacity = (5 * seq_len + 4 * experts - 1) // (4 * experts)
     slots = experts * capacity
     weight_in = expert_in[0]
     weight_out = expert_out[0]
+    kernels = capacity % 16 == 0 and experts == 8 and groups == 4
 
     route_ids = routes[:, 0]
     route_hot = route_ids[:, None] == jnp.arange(experts, dtype=jnp.int32)[None, :]
@@ -265,17 +791,13 @@
     slot_index = jnp.where(position < capacity, route_ids * capacity + position, slots)
     pick = (jnp.arange(slots, dtype=jnp.int32)[:, None] == slot_index[None, :]).astype(bf16)
 
-    def exchange(rows):
-        rows = rows.reshape(experts, capacity, width)
-        return lax.all_to_all(rows, "expert", split_axis=0, concat_axis=0, tiled=True).reshape(slots, width)
-
     def scatter_rows(rows):
         return contract(pick, rows, (1, 0)).astype(bf16)
 
     def gather_rows(rows):
         return contract(pick, rows, (0, 0))
 
-    grad_recv = exchange(scatter_rows(cotangent))
+    grad_recv = exchange(scatter_rows(cotangent), experts)
 
     tokens_f = tokens.astype(f32)
     normed, scale_one = rms_forward(tokens_f, gain_one)
@@ -288,33 +810,25 @@
     spread = jnp.einsum("bh,bx->hx", rel_table, bucket_hot, precision=highest)
     spread = spread.reshape(heads // 2, 2, 2 * seq_len)
     context, context_t, logsum = attend(queries, key_rows, value_rows, spread)
+    context, grad_recv = lax.optimization_barrier((context, grad_recv))
     hidden = tokens_f + contract(context, out_w, (1, 0))
     normed_two, scale_two = rms_forward(hidden, gain_two)
     normed_two_low = normed_two.astype(bf16)
 
-    received = exchange(scatter_rows(normed_two_low))
-    own = lax.axis_index("expert")
-    own_hot = (jnp.arange(experts, dtype=jnp.int32) == own).astype(f32)[None, :]
-    probs_recv = jax.nn.softmax(contract(received, router_w, (1, 0)), axis=-1)
-    gate_recv = jnp.sum(probs_recv * own_hot, axis=-1, keepdims=True)
-    grad_recv_f = grad_recv.astype(f32)
-    grad_produced = (grad_recv_f * gate_recv).astype(bf16)
-    preact = contract(received, weight_in, (1, 0))
-    gelu_values, gelu_pullback = jax.vjp(gelu_tanh, preact)
-    active = gelu_values.astype(bf16)
-    produced = contract(active, weight_out, (1, 0)).astype(bf16)
-    gate_grad = jnp.sum(grad_recv_f * produced.astype(f32), axis=-1, keepdims=True)
-    logit_low = (gate_grad * gate_recv * (own_hot - probs_recv)).astype(bf16)
-    grad_active = contract(grad_produced, weight_out, (1, 1))
-    grad_preact = gelu_pullback(grad_active)[0].astype(bf16)
-    grad_received = contract(grad_preact, weight_in, (1, 1)) + contract(logit_low, router_w, (1, 1))
-    grad_rows = exchange(grad_received.astype(bf16))
-    returned = exchange(produced)
-    in_grad = contract(received, grad_preact, (0, 0)).astype(bf16)
-    out_grad_local = contract(active, grad_produced, (0, 0)).astype(bf16)
-    router_grad = contract(received, logit_low, (0, 0))
+    send = scatter_rows(normed_two_low)
+    if kernels:
+        router_pad = jnp.pad(router_w, ((0, 0), (0, 128 - experts)))
+        grad_rows, produced, in_grad, out_grad_t, router_grad = expert_pass(
+            send, grad_recv, weight_in, weight_out, router_pad, experts, capacity
+        )
+        router_grad = router_grad[:, :experts]
+    else:
+        grad_rows, produced, in_grad, out_grad_t, router_grad = expert_native(
+            send, grad_recv, weight_in, weight_out, router_w, experts
+        )
+    returned = exchange(produced, experts)
     in_share = lax.psum_scatter(in_grad, "dp", scatter_dimension=0, tiled=True).astype(f32)
-    out_share = lax.psum_scatter(out_grad_local, "dp", scatter_dimension=1, tiled=True).astype(f32)
+    out_share = lax.psum_scatter(out_grad_t, "dp", scatter_dimension=0, tiled=True).astype(f32).T
 
     router_probs = jax.nn.softmax(contract(normed_two_low, router_w, (1, 0)), axis=-1)
     gate_value = jnp.sum(router_probs * route_float, axis=-1, keepdims=True)
@@ -325,31 +839,33 @@
     grad_hidden_norm, gain_two_grad = rms_backward(grad_normed_two, hidden, scale_two, gain_two)
     grad_hidden = grad_out + grad_hidden_norm
     branch_low = grad_hidden.astype(bf16)
-    out_w_grad = contract(context, branch_low, (0, 0))
+    out_w_grad = contract(context, branch_low, (0, 0)).astype(bf16)
     grad_context = contract(branch_low, out_w, (1, 1)).astype(bf16)
-    out_w_grad = lax.psum(out_w_grad, ("dp", "expert"))
     query_grad, key_grad, value_grad, diagonals = attend_back(
         queries, key_rows, value_rows, grad_context, spread, context_t, logsum
     )
-    query_w_grad = contract(normed_low, query_grad, (0, 0))
-    key_w_grad = contract(normed_low, key_grad, (0, 0))
-    value_w_grad = contract(normed_low, value_grad, (0, 0))
-    grad_normed = (
-        contract(query_grad, query_w, (1, 1))
-        + contract(key_grad, key_w, (1, 1))
-        + contract(value_grad, value_w, (1, 1))
-    )
-    grad_tokens_norm, gain_one_grad = rms_backward(grad_normed, tokens_f, scale_one, gain_one)
-    input_grad = grad_hidden + grad_tokens_norm
     diagonals = diagonals[:, :2].reshape(heads, 2 * seq_len)
     rel_grad = jnp.einsum("bx,hx->bh", bucket_hot, diagonals, precision=highest)
-    query_w_grad, key_w_grad, value_w_grad, rel_grad, gain_one_grad, gain_two_grad, router_grad = lax.psum(
-        (query_w_grad, key_w_grad, value_w_grad, rel_grad, gain_one_grad, gain_two_grad, router_grad),
-        ("dp", "expert"),
+    rel_flat = rel_grad.reshape(1, -1)
+    small = jnp.concatenate(
+        [
+            jnp.zeros((1, width), f32),
+            gain_two_grad[None],
+            jnp.pad(rel_flat, ((0, 5), (0, width - rel_flat.shape[1]))),
+            router_grad.T,
+        ]
     )
+    run = functools.partial(tail, groups=groups, experts=experts) if kernels else tail_native
+    grads, input_grad, small = run(
+        tokens, gain_one[None], normed_low, query_grad, key_grad, value_grad,
+        query_w, key_w, value_w, grad_hidden, out_w_grad, small,
+    )
+    grads = grads.astype(f32)
+    rel_grad = small[2, : rel_flat.shape[1]].reshape(rel_grad.shape)
+    router_grad = small[8:].T
     return (
-        output, input_grad, query_w_grad, key_w_grad, value_w_grad, out_w_grad, rel_grad,
-        gain_one_grad, gain_two_grad, router_grad, in_share[None], out_share[None],
+        output, input_grad, grads[1], grads[2], grads[3], grads[0], rel_grad,
+        small[0], small[1], router_grad, in_share[None], out_share[None],
     )
 
 

time: 593 us -> 393 us (0.66)
  waiting for transfers between devices: 222 us -> 0.72 us
  Pallas kernels: 99.7 us -> 289 us
  matrix products: 140 us -> 37.7 us
  blocking collectives: 42.7 us -> 0 us
  starting transfers between devices: 21.9 us -> 11.4 us
  local copies, waits for them, and re-layouts: 21.8 us -> 14.7 us
    pallas_call x0 -> x2, Pallas kernels: none -> 190 us  [the longest x1 96.3 us: expert_pass(): pl.pallas_call(functools.partial(expert_kernel, experts, capacity, tile),...]
    psum x1 -> x0, waiting for transfers between devices: 120 us -> none  [on_device(): lax.psum((query_w_grad, key_w_grad, value_w_grad, rel_grad, gain_one_grad...]
    all_to_all x4 -> x2, waiting for transfers between devices: 102 us -> 0.01 us  [exchange(): lax.all_to_all(rows, 'expert', split_axis=0, concat_axis=0, tiled=True)]
    dot_general x26 -> x11, matrix products: 139 us -> 37.2 us  [contract(): lax.dot_general(left, right, (((dims[0],), (dims[1],)), ((), ())), prefer...]
    psum x1 -> x0, blocking collectives: 42.7 us -> none  [on_device(): lax.psum((query_w_grad, key_w_grad, value_w_grad, rel_grad, gain_one_grad...]
    unnamed x82 -> x53, local copies, waits for them, and re-layouts: 20.3 us -> 5.66 us
    all_to_all x4 -> x2, starting transfers between devices: 21.6 us -> 11.4 us  [exchange(): lax.all_to_all(rows, 'expert', split_axis=0, concat_axis=0, tiled=True)]
  transfers between devices with their start and end apart: 7 -> 4, of which waited for: 4 -> 0; matrix products, arithmetic and copies ran while one was open for 21% -> 11% of each run, Pallas kernels for 10% -> 50%
where the time goes in v2:
time: 393 us; the launch traced here: 385 us
  Pallas kernels  289 us (74%)
  matrix products  37.7 us (10%)
  other arithmetic  16.7 us (4%)
  between operations  14.9 us (4%)
  local copies, waits for them, and re-layouts  14.7 us (4%)
  starting transfers between devices  11.4 us (3%)
    pallas_call x1, Pallas kernels, expert_pass(): pl.pallas_call(functools.partial(expert_kernel, experts, capacity, tile),...  96.3 us
    pallas_call x1, Pallas kernels, tail(): pl.pallas_call(functools.partial(tail_kernel, groups, experts), in_specs=...  93.8 us
    pallas_call x1, Pallas kernels, attend_back(): pl.pallas_call(attend_back_kernel, grid=(pairs,), in_specs=[blk, blk, blk...  57.4 us
    pallas_call x1, Pallas kernels, attend(): pl.pallas_call(attend_kernel, grid=(pairs,), in_specs=[blk, blk, blk, pl....  41.7 us
    dot_general x11, matrix products, contract(): lax.dot_general(left, right, (((dims[0],), (dims[1],)), ((), ())), prefer...  37.2 us
    all_to_all x2, starting transfers between devices, exchange(): lax.all_to_all(rows, 'expert', split_axis=0, concat_axis=0, tiled=True)  11.4 us
  transfers between devices with their start and end apart: 4, of which 0 were waited for; matrix products, arithmetic and copies ran while one was open for 11% of the time, Pallas kernels for 50%

profile of v2, /device:TPU:1, one launch (start us, length us, event | category | flops | bytes accessed | tf_op | source)
XLA Modules:
  0.0 385.4 jit_solution(3550900160656625371)
XLA Ops:
  7.2 0.0 copy-start
  7.2 0.8 fusion.22
  8.0 2.3 reduce-window.6
  10.2 0.3 slice_reduce_fusion
  10.5 0.2 reduce-window.9
  10.7 0.1 add_bitcast_fusion
  10.8 0.7 fusion.21
  11.5 0.7 add_select_fusion
  12.2 5.1 %fusion.4 = bf16[1280,768]{1,0:T(8,128)(2,1)} fusion(bf16[1024,768]{1,0:T(8,128)(2,1)} %param.27, s32[1024]{0:T(1024)S(1)} %add_select_fusion), kind=kOutput, calls=%fused_computation.8 | convolution fusion | flops 2015559680 | bytes 3543040 | tf_op jit(solution)/shard_map/dot_general | solution.py:728
  17.3 6.5 %all-to-all-start = ((bf16[8,160,768]{2,1,0:T(8,128)(2,1)}), bf16[8,160,768]{2,1,0:T(8,128)(2,1)}, u32[]{:S(2)}, u32[]{:S(2)}) async-start(bf16[8,160,768]{2,1,0:T(8,128)(2,1)} %bitcast.62), calls=%async_computation | async-start | bytes 3932160 | tf_op jit(solution)/shard_map/all_to_all | solution.py:734
  23.8 0.1 pad_add_fusion
  23.9 0.1 rev.3
  24.0 0.2 convolution_bitcast_fusion
  24.2 0.1 reshape.105.u_ref
  24.3 0.2 copy.32
  24.4 0.7 pad.8.rw
  25.2 0.4 fusion.6
  25.5 0.0 copy-start.24
  25.6 0.4 fusion.8.nl
  26.0 0.8 copy-done.24
  26.8 2.5 convolution_convert_fusion.1.v_ref
  29.4 1.4 convolution_convert_fusion.2.k_ref
  30.8 0.0 copy-start.3
  30.8 1.4 convolution_convert_fusion.3.q_ref
  32.2 41.7 %attend.1 = (bf16[1024,768]{1,0:T(8,128)(2,1)S(1)}, f32[768,1024]{1,0:T(8,128)}, f32[6,8,1024]{2,1,0:T(8,128)S(1)}) custom-call(bf16[1024,768]{1,0:T(8,128)(2,1)S(1)} %convolution_convert_fusion.3.q_ref, bf16[1024,768]{1,0:T(8,128)(2,1)S(1)} %convolution_convert_fusion.2.k_ref, bf16[1024,768]{1,0:T(8,128)(2,1)} %convolution_convert_fusion.1.v_ref, ...), custom_call_target="tpu_custom_call" | custom-call | flops 12884901888 | bytes 15728640 | tf_op jit(solution)/shard_map/attend/pallas_call | solution.py:84
  73.9 1.1 copy-done.4
  75.1 0.7 copy-done.5
  75.8 0.0 all-to-all-done
  75.8 2.9 multiply_reduce_fusion.2
  78.7 3.9 %fusion.5.xs = bf16[1280,768]{1,0:T(8,128)(2,1)} fusion(s32[1024]{0:T(1024)S(1)} %add_select_fusion, f32[1024,768]{1,0:T(8,128)S(1)} %get-tuple-element.81, f32[768]{0:T(1024)S(1)} %copy-done.18, f32[1024]{0:T(1024)S(1)} %get-tuple-element.79), kind=kOutput, calls=%fused_computation.9 | convolution fusion | flops 2017918976 | bytes 5123072 | tf_op jit(solution)/shard_map/dot_general | solution.py:728
  82.6 96.3 %experts.1 = (bf16[1280,768]{1,0:T(8,128)(2,1)}, bf16[1280,768]{1,0:T(8,128)(2,1)}, bf16[768,3072]{1,0:T(8,128)(2,1)}, bf16[768,3072]{1,0:T(8,128)(2,1)}, f32[768,128]{1,0:T(8,128)}) custom-call(bf16[1280,768]{1,0:T(8,128)(2,1)} %fusion.5.xs, bf16[1280,768]{1,0:T(8,128)(2,1)} %bitcast.5.gr_h, bf16[768,3072]{1,0:T(8,128)(2,1)} %bitcast.68, ...), custom_call_target="tpu_custom_call" | custom-call | flops 36238786560 | bytes 18874368 | tf_op jit(solution)/shard_map/experts/pallas_call | solution.py:415
  178.9 0.0 reduce-scatter.5.cloned.1.call-update
  179.0 0.0 reduce-scatter.3.cloned.1.call-start
  179.0 0.7 reduce-scatter.3.cloned.1.call-update
  179.7 0.6 broadcast_in_dim.40.gain
  180.3 4.9 %all-to-all-start.1 = ((bf16[8,160,768]{2,1,0:T(8,128)(2,1)}), bf16[8,160,768]{2,1,0:T(8,128)(2,1)}, u32[]{:S(2)}, u32[]{:S(2)}) async-start(bf16[8,160,768]{2,1,0:T(8,128)(2,1)} %bitcast.61), calls=%async_computation.1 | async-start | bytes 3932160 | tf_op jit(solution)/shard_map/all_to_all | solution.py:734
  185.2 0.0 copy-start.13
  185.2 6.2 %multiply_reduce_fusion = (f32[768]{0:T(1024)S(1)}, f32[1024]{0:T(1024)S(1)}, f32[1024,768]{1,0:T(8,128)S(1)}) fusion(f32[1024,768]{1,0:T(8,128)} %copy-done.6, f32[1024]{0:T(1024)S(1)} %get-tuple-element.79, f32[768]{0:T(1024)S(1)} %copy-done.18, bf16[1280,768]{1,0:T(8,128)(2,1)} %get-tuple-element.33, s32[1024]{0:T(1024)S(1)} %add_select_fusion), kind=kOutput, calls=%fused_computation.13 | convolution fusion | flops 2019293440 | bytes 8275968 | tf_op jit(solution)/shard_map/dot_general | solution.py:728
  191.4 1.0 subtract_add_fusion.ghid
  192.5 2.6 convolution_convert_fusion.g_ref
  195.1 57.4 %attend_back.1 = (bf16[1024,768]{1,0:T(8,128)(2,1)}, bf16[1024,768]{1,0:T(8,128)(2,1)}, bf16[1024,768]{1,0:T(8,128)(2,1)}, f32[6,8,2048]{2,1,0:T(8,128)}) custom-call(bf16[1024,768]{1,0:T(8,128)(2,1)} %copy-done.4, bf16[1024,768]{1,0:T(8,128)(2,1)} %copy-done.3, bf16[1024,768]{1,0:T(8,128)(2,1)} %convolution_convert_fusion.1.v_ref, ...), custom_call_target="tpu_custom_call" | custom-call | flops 32212254720 | bytes 15728640 | tf_op jit(solution)/shard_map/attend_back/pallas_call | solution.py:200
  252.5 0.2 copy.34
  252.7 1.0 slice.38
  253.7 0.1 reshape.111
  253.8 0.2 fusion.15
  254.0 0.2 reshape.112
  254.2 0.7 fusion.18.small
  254.9 4.6 %convolution_convert_fusion.4.dwo = bf16[768,768]{1,0:T(8,128)(2,1)} fusion(bf16[1024,768]{1,0:T(8,128)(2,1)S(1)} %get-tuple-element.30, f32[1024,768]{1,0:T(8,128)} %copy-done.11), kind=kOutput, calls=%fused_computation.33 | convolution fusion | flops 1209335808 | bytes 5898240 | tf_op jit(solution)/shard_map/dot_general | solution.py:728
  259.5 93.8 %tail.1 = (bf16[4,768,768]{2,1,0:T(8,128)(2,1)}, f32[1024,768]{1,0:T(8,128)}, f32[16,768]{1,0:T(8,128)}) custom-call(bf16[1024,768]{1,0:T(8,128)(2,1)} %tok.1, f32[1,768]{1,0:T(1,128)} %broadcast_in_dim.40.gain, bf16[1024,768]{1,0:T(8,128)(2,1)} %copy-done.12, bf16[1024,768]{1,0:T(8,128)(2,1)} %get-tuple-element.36.dq, ...), custom_call_target="tpu_custom_call" | custom-call | flops 7247757312 | bytes 15728640 | tf_op jit(solution)/shard_map/tail/pallas_call | solution.py:668
  353.3 0.7 slice_reduce_fusion.3
  354.0 0.1 reshape_squeeze.3
  354.1 0.7 copy.35
  354.8 3.3 convert_element_type.70
  358.1 0.0 copy-start.15
  358.1 0.6 slice_reduce_fusion.1
  358.8 0.6 fusion.25
  359.5 0.6 slice_bitcast_fusion.5
  360.1 3.8 slice_bitcast_fusion
  363.9 0.0 all-to-all-done.1
  363.9 6.1 %add_convert_fusion = bf16[1024,768]{1,0:T(8,128)(2,1)} fusion(f32[1024,768]{1,0:T(8,128)} %copy-done.6, f32[1024]{0:T(1024)S(1)} %select_reduce_fusion, bf16[1280,768]{1,0:T(8,128)(2,1)} %bitcast.9, s32[1024]{0:T(1024)S(1)} %add_select_fusion), kind=kOutput, calls=%fused_computation.16 | convolution fusion | flops 2016935936 | bytes 6692864 | tf_op jit(solution)/shard_map/dot_general | solution.py:728
  370.0 2.9 convert_bitcast_fusion
  372.9 3.1 bitcast_convert_fusion
  376.0 1.7 copy.41
  377.7 0.4 copy-done.1
  (52 shorter events, 0.2 us)
Async XLA Ops:
  7.2 68.6 %copy-start = (bf16[768,768]{1,0:T(8,128)(2,1)S(1)}, bf16[768,768]{1,0:T(8,128)(2,1)}, u32[]{:S(2)}) copy-start(bf16[768,768]{1,0:T(8,128)(2,1)} %param.19) | copy-start | bytes 3538948
  17.3 6.5 %copy-start.21 = (s32[2047]{0:T(1024)S(1)}, s32[2047]{0:T(1024)}, u32[]{:S(2)}) copy-start(s32[2047]{0:T(1024)} %param.26) | copy-start | bytes 24568
  17.3 6.7 %copy-start.20 = (f32[32,12]{0,1:T(8,128)S(1)}, f32[32,12]{0,1:T(8,128)}, u32[]{:S(2)}) copy-start(f32[32,12]{0,1:T(8,128)} %param.20) | copy-start | bytes 4612
  17.3 7.0 %copy-start.16 = (bf16[768,8]{0,1:T(8,128)(2,1)S(1)}, bf16[768,8]{0,1:T(8,128)(2,1)}, u32[]{:S(2)}) copy-start(bf16[768,8]{0,1:T(8,128)(2,1)} %param.22) | copy-start | bytes 36868
  17.3 7.9 %copy-start.9 = (bf16[1024,768]{1,0:T(8,128)(2,1)S(1)}, bf16[1024,768]{1,0:T(8,128)(2,1)}, u32[]{:S(2)}) copy-start(bf16[1024,768]{1,0:T(8,128)(2,1)} %tok.1) | copy-start | bytes 4718596
  17.3 58.5 %all-to-all-start = ((bf16[8,160,768]{2,1,0:T(8,128)(2,1)}), bf16[8,160,768]{2,1,0:T(8,128)(2,1)}, u32[]{:S(2)}, u32[]{:S(2)}) async-start(bf16[8,160,768]{2,1,0:T(8,128)(2,1)} %bitcast.62), calls=%async_computation | async-start | bytes 3932160 | tf_op jit(solution)/shard_map/all_to_all | solution.py:734
  23.8 1.8 copy-start.19
  23.8 346.2 %reduce-scatter.5.cloned.1.call-start = ((), (), s32[]{:S(2)}) async-start(), calls=%async_computation.5 | async-start | bytes 5898240 | tf_op jit(solution)/shard_map/reduce_scatter | solution.py:831
  24.3 7.9 %copy-start.2 = (f32[6,2,2048]{2,1,0:T(2,128)}, f32[6,2,2048]{2,1,0:T(2,128)S(1)}, u32[]{:S(2)}) copy-start(f32[6,2,2048]{2,1,0:T(2,128)S(1)} %reshape.105.u_ref) | copy-start | bytes 294916
  25.5 1.3 copy-start.24
  26.8 3.9 %copy-start.12 = (bf16[1024,768]{1,0:T(8,128)(2,1)}, bf16[1024,768]{1,0:T(8,128)(2,1)S(1)}, u32[]{:S(2)}) copy-start(bf16[1024,768]{1,0:T(8,128)(2,1)S(1)} %fusion.8.nl) | copy-start | bytes 4718596
  26.8 2.5 copy-start.23
  29.4 1.4 copy-start.22
  30.8 1.4 copy-start.3
  73.9 1.1 copy-start.4
  75.1 0.7 copy-start.5
  75.8 2.9 copy-start.18
  78.7 3.9 %copy-start.6 = (f32[1024,768]{1,0:T(8,128)}, f32[1024,768]{1,0:T(8,128)S(1)}, u32[]{:S(2)}) copy-start(f32[1024,768]{1,0:T(8,128)S(1)} %get-tuple-element.81) | copy-start | bytes 9437188
  179.0 193.9 %reduce-scatter.3.cloned.1.call-start = ((), (), s32[]{:S(2)}) async-start(), calls=%async_computation.4 | async-start | bytes 5898240 | tf_op jit(solution)/shard_map/reduce_scatter | solution.py:830
  180.3 183.6 %all-to-all-start.1 = ((bf16[8,160,768]{2,1,0:T(8,128)(2,1)}), bf16[8,160,768]{2,1,0:T(8,128)(2,1)}, u32[]{:S(2)}, u32[]{:S(2)}) async-start(bf16[8,160,768]{2,1,0:T(8,128)(2,1)} %bitcast.61), calls=%async_computation.1 | async-start | bytes 3932160 | tf_op jit(solution)/shard_map/all_to_all | solution.py:734
  185.2 6.2 %copy-start.7 = (f32[1024,768]{1,0:T(8,128)S(1)}, f32[1024,768]{1,0:T(8,128)}, u32[]{:S(2)}) copy-start(f32[1024,768]{1,0:T(8,128)} %copy-done.6) | copy-start | bytes 9437188
  185.2 6.2 %copy-start.13 = (bf16[1024,768]{1,0:T(8,128)(2,1)S(1)}, bf16[1024,768]{1,0:T(8,128)(2,1)}, u32[]{:S(2)}) copy-start(bf16[1024,768]{1,0:T(8,128)(2,1)} %param.27) | copy-start | bytes 4718596
  192.5 2.6 copy-start.11
  195.1 57.5 %copy-start.14 = (f32[768,128]{1,0:T(8,128)S(1)}, f32[768,128]{1,0:T(8,128)}, u32[]{:S(2)}) copy-start(f32[768,128]{1,0:T(8,128)} %get-tuple-element.40) | copy-start | bytes 1179652
  354.8 3.3 copy-start.17
  354.8 4.0 %copy-start.8 = (f32[1024,768]{1,0:T(8,128)S(1)}, f32[1024,768]{1,0:T(8,128)}, u32[]{:S(2)}) copy-start(f32[1024,768]{1,0:T(8,128)} %copy-done.6) | copy-start | bytes 9437188
  358.1 1.3 copy-start.15
  372.9 3.1 copy-start.10
  376.0 2.1 copy-start.1
Sparse Core Ops, SparseCore 0:
  179.1 56.8 reduce-scatter.4
  239.0 86.2 reduce-scatter.2

commit v3 on v2

--- a/solution.py
+++ b/solution.py
@@ -267,9 +267,8 @@
     pl.semaphore_wait(barrier, experts - 1)
 
     def partner(step):
-        flip = lax.rem(chips - step, chips)
         high, low = place // 2, lax.rem(place, 2)
-        fhigh, flow = flip // 2, lax.rem(flip, 2)
+        fhigh, flow = step // 2, lax.rem(step, 2)
         return 2 * (high + fhigh - 2 * high * fhigh) + low + flow - 2 * low * flow
 
     def send_rows(peer):
@@ -463,39 +462,47 @@
     )
 
 
-def tail_kernel(
-    groups, experts,
-    tok, gain, nl, dq, dk, dv, wq, wk, wv, ghid, dwo, small,
-    wout_o, ing_o, small_o,
-    part, r1, s1, r2, r3, s3, g4, full, nt, sbuf, srecv, sone, stwo,
-    send1, recv1, send2, recv2, send3, recv3, send4, recv4, send5, recv5, send6, recv6, send7, recv7,
+def others(count, mine):
+    return [lax.rem(mine + k, count) for k in range(1, count)]
+
+
+LAGS = (1, 4, 9, 13, 15)
+
+
+def back_kernel(
+    groups, experts, pairs,
+    q_ref, k_ref, v_ref, g_ref, u_ref, ctxt_ref, lse_ref, wq, wk, wv, hot, gain, nl_h, tok_h, ghid_h, dwo_h, small_h,
+    wsum_o, ing_o, small_o,
+    base, acc, kaug, vaug, qaug, gaug, qz, gz, kt, dqt, dall, nt, tok,
+    part, r1, r2, r3, full, sbuf, srecv, sone, stwo,
+    send1, recv1, send2, recv2, send3, recv3, send4, recv4, send5, recv5, send6, recv6, send7, recv7, local,
 ):
+    seq = q_ref.shape[0]
+    width = tok.shape[1]
+    span = 256
+    pair = pl.program_id(0)
     me = lax.axis_index("expert")
     my_dp = lax.axis_index("dp")
     core = lax.rem(me, 2)
     place = me // 2
     chips = experts // 2
     sibling = me + 1 - 2 * core
-    width = part.shape[2]
     half = width // 2
     piece = half // groups
-    barrier = pltpu.get_barrier_semaphore()
-    for k in range(1, experts):
-        pl.semaphore_signal(barrier, inc=1, device_id={"expert": lax.rem(me + k, experts)})
-    for k in range(1, groups):
-        pl.semaphore_signal(barrier, inc=1, device_id={"dp": lax.rem(my_dp + k, groups)})
+    thick = part.shape[2]
+    gain_rows = width // 128
 
     def half_rows(which):
         return pl.ds(pl.multiple_of(which * half, 16), half)
 
-    def piece_rows(which):
-        return pl.ds(pl.multiple_of(which * piece, 16), piece)
+    def own_piece(which):
+        return pl.ds(pl.multiple_of(core * half + which * piece, 16), piece)
 
     def copy1(c):
         return remote(part.at[c, half_rows(1 - core), :], r1.at[c], send1.at[c], recv1.at[c], "expert", sibling)
 
     def copy2(c, peer, slot):
-        return remote(s1.at[c, piece_rows(peer), :], r2.at[c, slot], send2.at[c, peer], recv2.at[c, slot], "dp", peer)
+        return remote(part.at[c, own_piece(peer), :], r2.at[c, slot], send2.at[c, peer], recv2.at[c, slot], "dp", peer)
 
     def copy3(c, peer, slot):
         return remote(
@@ -504,35 +511,27 @@
 
     def copy4(c, peer, slot):
         return remote(
-            g4.at[c, piece_rows(my_dp), :], g4.at[c, piece_rows(slot), :],
+            full.at[c, own_piece(my_dp), :], full.at[c, own_piece(slot), :],
             send4.at[c, peer], recv4.at[c, slot], "dp", peer,
         )
 
-    def copy5(c):
+    def copy5(c, which):
         return remote(
-            full.at[c, half_rows(core), :], full.at[c, half_rows(core), :], send5.at[c], recv5.at[c], "expert", sibling
-        )
-
-    def got5(c):
-        return remote(
-            full.at[c, half_rows(1 - core), :], full.at[c, half_rows(1 - core), :],
+            full.at[c, half_rows(which), :], full.at[c, half_rows(which), :],
             send5.at[c], recv5.at[c], "expert", sibling,
         )
-
-    def others(count, mine):
-        return [lax.rem(mine + k, count) for k in range(1, count)]
 
     def stage1(c):
         copy1(c).start()
 
     def stage2(c):
         copy1(c).wait_recv()
-        s1[c] = (part[c, half_rows(core), :].astype(f32) + r1[c].astype(f32)).astype(bf16)
+        part[c, half_rows(core), :] = (part[c, half_rows(core), :].astype(f32) + r1[c].astype(f32)).astype(bf16)
         for peer in others(groups, my_dp):
             copy2(c, peer, my_dp).start()
 
     def stage3(c):
-        total = s1[c, piece_rows(my_dp), :].astype(f32)
+        total = part[c, own_piece(my_dp), :].astype(f32)
         for peer in others(groups, my_dp):
             copy2(c, peer, peer).wait_recv()
             total = total + r2[c, peer].astype(f32)
@@ -546,164 +545,334 @@
         total = r3[c, 0].astype(f32)
         for slot in range(1, chips):
             total = total + r3[c, slot].astype(f32)
-        g4[c, piece_rows(my_dp), :] = total.astype(bf16)
+        full[c, own_piece(my_dp), :] = total.astype(bf16)
         for peer in others(groups, my_dp):
             copy4(c, peer, my_dp).start()
 
     def stage5(c):
         for peer in others(groups, my_dp):
             copy4(c, peer, peer).wait_recv()
-        full[c, half_rows(core), :] = g4[c]
-        copy5(c).start()
+        copy5(c, core).start()
 
     def stage6(c):
-        got5(c).wait_recv()
-        wout_o[c] = full[c]
-
-    def finish(c):
-        copy1(c).wait_send()
+        copy5(c, 1 - core).wait_recv()
+
+    early = pl.ds(8 + hot.shape[0], sbuf.shape[0] - 8 - hot.shape[0])
+    late = pl.ds(0, 8 + hot.shape[0])
+
+    def copy6(part_idx, rows, peer, slot):
+        return remote(
+            sbuf.at[rows, :], srecv.at[slot, rows, :],
+            send6.at[part_idx, peer], recv6.at[part_idx, slot], "expert", peer,
+        )
+
+    def copy7(part_idx, rows, peer, slot):
+        return remote(
+            sone.at[rows, :], stwo.at[slot, rows, :],
+            send7.at[part_idx, peer], recv7.at[part_idx, slot], "dp", peer,
+        )
+
+    def small1(part_idx, rows):
+        srecv[me, rows, :] = sbuf[rows, :]
+        for peer in others(experts, me):
+            copy6(part_idx, rows, peer, me).start()
+
+    def small2(part_idx, rows):
+        for peer in others(experts, me):
+            copy6(part_idx, rows, peer, peer).wait_recv()
+        total = srecv[0, rows, :]
+        for slot in range(1, experts):
+            total = total + srecv[slot, rows, :]
+        sone[rows, :] = total
+        stwo[my_dp, rows, :] = total
         for peer in others(groups, my_dp):
-            copy2(c, peer, my_dp).wait_send()
-            copy4(c, peer, my_dp).wait_send()
-        for peer in others(chips, place):
-            copy3(c, peer, place).wait_send()
-        copy5(c).wait_send()
-
-    def weight_grad(c, grad):
-        def block(idx, carry):
+            copy7(part_idx, rows, peer, my_dp).start()
+
+    def small3(part_idx, rows):
+        for peer in others(groups, my_dp):
+            copy7(part_idx, rows, peer, peer).wait_recv()
+        total = stwo[0, rows, :]
+        for slot in range(1, groups):
+            total = total + stwo[slot, rows, :]
+        small_o[rows, :] = total
+
+    stages = (stage2, stage3, stage4, stage5, stage6)
+
+    def advance(slot):
+        for lag, stage in reversed(list(zip(LAGS, stages))):
+            since = slot - lag
+
+            @pl.when((since >= 0) & (since <= 4 * pairs) & ((lax.rem(since, 4) == 0) | (since == 2)))
+            def _():
+                stage(since // 4 + jnp.minimum(since, 1))
+
+    loads = [
+        pltpu.make_async_copy(nl_h, tok, local.at[0]),
+        pltpu.make_async_copy(ghid_h, ing_o, local.at[2]),
+        pltpu.make_async_copy(dwo_h.at[:, 0:thick], part.at[0], local.at[3]),
+        pltpu.make_async_copy(dwo_h.at[:, thick : 2 * thick], part.at[1], local.at[4]),
+        pltpu.make_async_copy(small_h, sbuf, local.at[5]),
+    ]
+
+    @pl.when(pair == 0)
+    def _():
+        barrier = pltpu.get_barrier_semaphore()
+        for peer in others(experts, me):
+            pl.semaphore_signal(barrier, inc=1, device_id={"expert": peer})
+        for peer in others(groups, my_dp):
+            pl.semaphore_signal(barrier, inc=1, device_id={"dp": peer})
+        for copy in loads:
+            copy.start()
+        for copy in loads:
+            copy.wait()
+        nt[...] = tok[...].T
+        pl.semaphore_wait(barrier, experts + groups - 2)
+        stage1(0)
+        stage1(1)
+        small1(0, early)
+
+    mine = pl.ds(pl.multiple_of(128 * pair, 128), 128)
+    lane = lax.broadcasted_iota(jnp.int32, (seq, 128), 1)
+    gt = g_ref[...].T
+    qtv = q_ref[...].T
+    kt[...] = k_ref[...].T
+    gtf = gt.astype(f32)
+    pad = jnp.zeros((48, seq), bf16)
+    one = jnp.ones((seq, 128), bf16)
+    nil = jnp.zeros((seq, 128), bf16)
+    acc[...] = jnp.zeros_like(acc)
+    for head in range(2):
+        fill_toeplitz(base, head, u_ref[0, head : head + 1, :])
+        own = (lane < 64) if head == 0 else (lane >= 64)
+        origin = 64 if head == 0 else 0
+        extra = jnp.where((lane >= origin) & (lane < origin + 3), one, nil)
+        kaug[head] = jnp.where(own, k_ref[...], extra)
+        vaug[head] = jnp.where(own, v_ref[...], extra)
+        qz[head] = jnp.where(own, q_ref[...], nil)
+        gz[head] = jnp.where(own, g_ref[...], nil)
+        rows = slice(64 * head, 64 * head + 64)
+        lse = split_rows(-lse_ref[0, head : head + 1, :])
+        dsum = split_rows(-jnp.sum(gtf[rows] * ctxt_ref[rows, :], axis=0, keepdims=True))
+        for dst, src, aug in ((qaug, qtv, lse), (gaug, gt, dsum)):
+            dst[head, rows, :] = src[rows]
+            dst[head, origin : origin + 16, :] = aug
+            dst[head, origin + 16 : origin + 64, :] = pad
+
+    dqt[...] = jnp.zeros_like(dqt)
+
+    def step(idx, carry):
+        rows = pl.ds(pl.multiple_of(idx * span, span), span)
+        dv = None
+        dk = None
+        for head in range(2):
+            s = dot_f32(kaug[head, rows, :], qaug[head])
+            dp = dot_f32(vaug[head, rows, :], gaug[head])
+            tops = []
+            grads = []
+            for piece_idx in range(2):
+                offs = pl.ds(pl.multiple_of(seq - span * idx - 128 * piece_idx, 128), seq)
+                p = jnp.exp(s[128 * piece_idx : 128 * piece_idx + 128] + base[head, :, offs])
+                ds_ = p * dp[128 * piece_idx : 128 * piece_idx + 128]
+                acc[head, :, offs] += ds_
+                tops.append(p.astype(bf16))
+                grads.append(ds_.astype(bf16))
+            p = jnp.concatenate(tops, axis=0)
+            ds_ = jnp.concatenate(grads, axis=0)
+            now = dot_f32(p, gz[head])
+            dv = now if dv is None else dv + now
+            now = dot_f32(ds_, qz[head])
+            dk = now if dk is None else dk + now
+            dqt[64 * head : 64 * head + 64, :] += dot_f32(kt[64 * head : 64 * head + 64, rows], ds_)
+        dall[1, rows, mine] = dk.astype(bf16)
+        dall[2, rows, mine] = dv.astype(bf16)
+        advance(4 * pair + idx)
+
+        @pl.when(4 * pair + idx == 7)
+        def _():
+            small2(0, early)
+
+        @pl.when(4 * pair + idx == 11)
+        def _():
+            small3(0, early)
+
+        return carry
+
+    lax.fori_loop(0, seq // span, step, 0)
+    dall[0, :, mine] = dqt[...].T.astype(bf16)
+    twice = 2 * seq
+    sub = lax.broadcasted_iota(jnp.int32, (8, twice), 0)
+    head_lane = lax.broadcasted_iota(jnp.int32, (hot.shape[0], 128), 1)
+    rel_rows = slice(8, 8 + hot.shape[0])
+    for head in range(2):
+        total = acc[head, 0:8, :]
+        for group in range(1, 16):
+            total = total + pltpu.roll(acc[head, 8 * group : 8 * group + 8, :], twice - 8 * group, 1)
+        for bit in (1, 2, 4):
+            total = jnp.where((sub & bit) != 0, pltpu.roll(total, twice - bit, 1), total)
+        diag = jnp.sum(total, axis=0, keepdims=True)
+        sums = jnp.sum(hot[...] * diag, axis=1, keepdims=True)
+        sbuf[rel_rows, :] = jnp.where(head_lane == 2 * pair + head, sums, sbuf[rel_rows, :])
+
+    def weight_block(idx, carry):
+        rows = pl.ds(pl.multiple_of(idx * 256, 256), 256)
+        grads = jnp.concatenate([dall[which, :, mine] for which in range(3)], axis=1)
+        part[pair + 2, rows, :] = dot_f32(nt[rows, :], grads).astype(bf16)
+        return carry
+
+    lax.fori_loop(0, width // 256, weight_block, 0)
+    stage1(pair + 2)
+
+    @pl.when(pair == pairs - 1)
+    def _():
+        def token_block(idx, carry):
             rows = pl.ds(pl.multiple_of(idx * 256, 256), 256)
-            part[c, rows, :] = dot_f32(nt[rows, :], grad[...]).astype(bf16)
+            grad = (
+                dot_nt(dall[0, rows, :], wq[...])
+                + dot_nt(dall[1, rows, :], wk[...])
+                + dot_nt(dall[2, rows, :], wv[...])
+            )
+            values = tok[rows, :].astype(f32)
+            scale = lax.rsqrt(jnp.mean(values * values, axis=-1, keepdims=True) + epsilon)
+            weighted = grad * gain[...]
+            inner = jnp.mean(weighted * values, axis=-1, keepdims=True)
+            ing_o[rows, :] += scale * weighted - values * (scale * scale * scale * inner)
+            return carry + jnp.sum(grad * values * scale, axis=0, keepdims=True)
+
+        reload = pltpu.make_async_copy(tok_h, tok, local.at[1])
+        reload.start()
+        last = pairs + 1
+        first = 4 * pairs
+        older = sorted(
+            (4 * c - 4 + lag, c, stage)
+            for c in range(2, last)
+            for lag, stage in zip(LAGS, range(2, 7))
+            if 4 * c - 4 + lag >= first
+        )
+
+        def drain(until):
+            while older and older[0][0] < first + until:
+                _, c, stage = older.pop(0)
+                stages[stage - 2](c)
+
+        def tokens_done(lower, upper, gain_grad):
+            return lax.fori_loop(lower, upper, token_block, gain_grad)
+
+        drain(1)
+        reload.wait()
+        gain_grad = tokens_done(0, 1, jnp.zeros((1, width), f32))
+        stage2(last)
+        drain(2)
+        gain_grad = tokens_done(1, seq // 512, gain_grad)
+        drain(4)
+        gain_grad = tokens_done(seq // 512, seq // 256, gain_grad)
+        stage3(last)
+        for row in range(gain_rows):
+            sbuf[row : row + 1, :] = gain_grad[:, 128 * row : 128 * row + 128]
+        small1(1, late)
+        drain(8)
+        small2(1, late)
+        stage4(last)
+        drain(99)
+        small3(1, late)
+        stage5(last)
+        stage6(last)
+        for c in range(2):
+            wsum_o[0, :, thick * c : thick * c + thick] = full[c]
+        for c in range(pairs):
+            for which in range(3):
+                wsum_o[1 + which, :, 128 * c : 128 * c + 128] = full[c + 2, :, 128 * which : 128 * which + 128]
+
+        def finish(c, carry):
+            copy1(c).wait_send()
+            for peer in others(groups, my_dp):
+                copy2(c, peer, my_dp).wait_send()
+                copy4(c, peer, my_dp).wait_send()
+            for peer in others(chips, place):
+                copy3(c, peer, place).wait_send()
+            copy5(c, core).wait_send()
             return carry
 
-        lax.fori_loop(0, width // 256, block, 0)
-
-    rows_total = tok.shape[0]
-    part[0] = dwo[...]
-    nt[...] = nl[...].T
-    pl.semaphore_wait(barrier, experts + groups - 2)
-    stage1(0)
-    weight_grad(1, dq)
-    stage1(1)
-    stage2(0)
-    weight_grad(2, dk)
-    stage1(2)
-    stage2(1)
-    stage3(0)
-    weight_grad(3, dv)
-    stage1(3)
-    stage2(2)
-    stage3(1)
-    stage4(0)
-
-    def token_block(idx, carry):
-        rows = pl.ds(pl.multiple_of(idx * 256, 256), 256)
-        grad = dot_nt(dq[rows, :], wq[...]) + dot_nt(dk[rows, :], wk[...]) + dot_nt(dv[rows, :], wv[...])
-        values = tok[rows, :].astype(f32)
-        scale = lax.rsqrt(jnp.mean(values * values, axis=-1, keepdims=True) + epsilon)
-        weighted = grad * gain[...]
-        inner = jnp.mean(weighted * values, axis=-1, keepdims=True)
-        ing_o[rows, :] = ghid[rows, :] + scale * weighted - values * (scale * scale * scale * inner)
-        return carry + jnp.sum(grad * values * scale, axis=0, keepdims=True)
-
-    gain_grad = jnp.zeros((1, width), f32)
-    gain_grad = lax.fori_loop(0, rows_total // 512, token_block, gain_grad)
-    stage2(3)
-    stage3(2)
-    stage4(1)
-    stage5(0)
-    gain_grad = lax.fori_loop(rows_total // 512, rows_total // 256, token_block, gain_grad)
-
-    sbuf[...] = small[...]
-    sbuf[0:1, :] = gain_grad
-    srecv[me] = sbuf[...]
-
-    def copy6(peer, slot):
-        return remote(sbuf, srecv.at[slot], send6.at[peer], recv6.at[slot], "expert", peer)
-
-    def copy7(peer, slot):
-        return remote(sone, stwo.at[slot], send7.at[peer], recv7.at[slot], "dp", peer)
-
-    for peer in others(experts, me):
-        copy6(peer, me).start()
-    stage3(3)
-    stage4(2)
-    stage5(1)
-    stage6(0)
-    for peer in others(experts, me):
-        copy6(peer, peer).wait_recv()
-    total = srecv[0]
-    for slot in range(1, experts):
-        total = total + srecv[slot]
-    sone[...] = total
-    stwo[my_dp] = total
-    for peer in others(groups, my_dp):
-        copy7(peer, my_dp).start()
-    stage4(3)
-    stage5(2)
-    stage6(1)
-    stage5(3)
-    stage6(2)
-    for peer in others(groups, my_dp):
-        copy7(peer, peer).wait_recv()
-    total = stwo[0]
-    for slot in range(1, groups):
-        total = total + stwo[slot]
-    small_o[...] = total
-    stage6(3)
-    for c in range(4):
-        finish(c)
-    for peer in others(experts, me):
-        copy6(peer, me).wait_send()
-    for peer in others(groups, my_dp):
-        copy7(peer, my_dp).wait_send()
-
-
-def tail(tokens, gain, normed_low, dq, dk, dv, wq, wk, wv, grad_hidden, dwo, small, groups, experts):
-    rows, width = tokens.shape
+        lax.fori_loop(0, pairs + 2, finish, 0)
+        for part_idx, rows in ((0, early), (1, late)):
+            for peer in others(experts, me):
+                copy6(part_idx, rows, peer, me).wait_send()
+            for peer in others(groups, my_dp):
+                copy7(part_idx, rows, peer, my_dp).wait_send()
+
+
+def back_pass(
+    q, k, v, g, u, ctxt, lse, wq, wk, wv, hot, gain, normed_low, tokens, grad_hidden, dwo, small, groups, experts
+):
+    seq, width = q.shape
+    pairs = width // 128
+    chunks = pairs + 2
+    thick = width // 2
     half = width // 2
     piece = half // groups
     chips = experts // 2
-    vmem = pl.BlockSpec(memory_space=pltpu.VMEM)
+    blk = pl.BlockSpec((seq, 128), lambda p: (0, p))
+    hbm = pl.BlockSpec(memory_space=pl.ANY)
+    fixed = lambda shape: pl.BlockSpec(shape, lambda p: (0,) * len(shape), pipeline_mode=pl.Buffered(1))
     dma = pltpu.SemaphoreType.DMA
     return pl.pallas_call(
-        functools.partial(tail_kernel, groups, experts),
-        in_specs=[vmem] * 12,
-        out_specs=[vmem] * 3,
+        functools.partial(back_kernel, groups, experts, pairs),
+        grid=(pairs,),
+        in_specs=[
+            blk, blk, blk, blk,
+            pl.BlockSpec((1, 2, 2 * seq), lambda p: (p, 0, 0)),
+            pl.BlockSpec((128, seq), lambda p: (p, 0)),
+            pl.BlockSpec((1, 8, seq), lambda p: (p, 0, 0)),
+            fixed((width, width)), fixed((width, width)), fixed((width, width)),
+            fixed(hot.shape), fixed(gain.shape),
+            hbm, hbm, hbm, hbm, hbm,
+        ],
+        out_specs=[fixed((4, width, width)), fixed((seq, width)), fixed(small.shape)],
         out_shape=[
             jax.ShapeDtypeStruct((4, width, width), bf16),
-            jax.ShapeDtypeStruct((rows, width), f32),
+            jax.ShapeDtypeStruct((seq, width), f32),
             jax.ShapeDtypeStruct(small.shape, f32),
         ],
         scratch_shapes=[
-            pltpu.VMEM((4, width, width), bf16),
-            pltpu.VMEM((4, half, width), bf16),
-            pltpu.VMEM((4, half, width), bf16),
-            pltpu.VMEM((4, groups, piece, width), bf16),
-            pltpu.VMEM((4, chips, piece, width), bf16),
-            pltpu.VMEM((4, piece, width), bf16),
-            pltpu.VMEM((4, half, width), bf16),
-            pltpu.VMEM((4, width, width), bf16),
-            pltpu.VMEM((width, rows), bf16),
+            pltpu.VMEM((2, 128, 2 * seq), f32),
+            pltpu.VMEM((2, 128, 2 * seq), f32),
+            pltpu.VMEM((2, seq, 128), bf16),
+            pltpu.VMEM((2, seq, 128), bf16),
+            pltpu.VMEM((2, 128, seq), bf16),
+            pltpu.VMEM((2, 128, seq), bf16),
+            pltpu.VMEM((2, seq, 128), bf16),
+            pltpu.VMEM((2, seq, 128), bf16),
+            pltpu.VMEM((128, seq), bf16),
+            pltpu.VMEM((128, seq), f32),
+            pltpu.VMEM((3, seq, width), bf16),
+            pltpu.VMEM((width, seq), bf16),
+            pltpu.VMEM((seq, width), bf16),
+            pltpu.VMEM((chunks, width, thick), bf16),
+            pltpu.VMEM((chunks, half, thick), bf16),
+            pltpu.VMEM((chunks, groups, piece, thick), bf16),
+            pltpu.VMEM((chunks, chips, piece, thick), bf16),
+            pltpu.VMEM((chunks, width, thick), bf16),
             pltpu.VMEM(small.shape, f32),
             pltpu.VMEM((experts,) + small.shape, f32),
             pltpu.VMEM(small.shape, f32),
             pltpu.VMEM((groups,) + small.shape, f32),
-            dma((4,)), dma((4,)),
-            dma((4, groups)), dma((4, groups)),
-            dma((4, chips)), dma((4, chips)),
-            dma((4, groups)), dma((4, groups)),
-            dma((4,)), dma((4,)),
-            dma((experts,)), dma((experts,)),
-            dma((groups,)), dma((groups,)),
+            dma((chunks,)), dma((chunks,)),
+            dma((chunks, groups)), dma((chunks, groups)),
+            dma((chunks, chips)), dma((chunks, chips)),
+            dma((chunks, groups)), dma((chunks, groups)),
+            dma((chunks,)), dma((chunks,)),
+            dma((2, experts)), dma((2, experts)),
+            dma((2, groups)), dma((2, groups)),
+            dma((6,)),
         ],
         compiler_params=pltpu.CompilerParams(
-            vmem_limit_bytes=60 << 20, collective_id=2, has_side_effects=True
+            vmem_limit_bytes=62 << 20, collective_id=2, has_side_effects=True
         ),
         cost_estimate=pl.CostEstimate(
-            flops=12 * rows * width * width, bytes_accessed=20 * rows * width, transcendentals=rows
+            flops=40 * seq * seq * width + 12 * seq * width * width,
+            bytes_accessed=40 * seq * width, transcendentals=seq * seq * 12,
         ),
-        name="tail",
-    )(tokens, gain, normed_low, dq, dk, dv, wq, wk, wv, grad_hidden, dwo, small)
+        name="attend_back",
+    )(q, k, v, g, u, ctxt, lse, wq, wk, wv, hot, gain, normed_low, tokens, grad_hidden, dwo, small)
 
 
 def rms_backward(grad_norm, values, row_scale, gain_vec):
@@ -764,9 +933,8 @@
     grad_normed = contract(dq, wq, (1, 1)) + contract(dk, wk, (1, 1)) + contract(dv, wv, (1, 1))
     _, scale = rms_forward(tokens_f, gain)
     grad_tokens, gain_grad = rms_backward(grad_normed, tokens_f, scale, gain)
-    small = jnp.concatenate([gain_grad[None], small[1:]])
-    grads, small = lax.psum((grads, small), ("dp", "expert"))
-    return grads, grad_hidden + grad_tokens, small
+    grads, gain_grad, small = lax.psum((grads, gain_grad, small), ("dp", "expert"))
+    return grads, grad_hidden + grad_tokens, gain_grad, small
 
 
 def on_device(
@@ -841,31 +1009,39 @@
     branch_low = grad_hidden.astype(bf16)
     out_w_grad = contract(context, branch_low, (0, 0)).astype(bf16)
     grad_context = contract(branch_low, out_w, (1, 1)).astype(bf16)
-    query_grad, key_grad, value_grad, diagonals = attend_back(
-        queries, key_rows, value_rows, grad_context, spread, context_t, logsum
-    )
-    diagonals = diagonals[:, :2].reshape(heads, 2 * seq_len)
-    rel_grad = jnp.einsum("bx,hx->bh", bucket_hot, diagonals, precision=highest)
-    rel_flat = rel_grad.reshape(1, -1)
-    small = jnp.concatenate(
-        [
-            jnp.zeros((1, width), f32),
-            gain_two_grad[None],
-            jnp.pad(rel_flat, ((0, 5), (0, width - rel_flat.shape[1]))),
-            router_grad.T,
-        ]
-    )
-    run = functools.partial(tail, groups=groups, experts=experts) if kernels else tail_native
-    grads, input_grad, small = run(
-        tokens, gain_one[None], normed_low, query_grad, key_grad, value_grad,
-        query_w, key_w, value_w, grad_hidden, out_w_grad, small,
-    )
+    if kernels:
+        small = jnp.concatenate(
+            [
+                jnp.zeros((8 + rel_table.shape[0], 128), f32),
+                jnp.pad(gain_two_grad.reshape(-1, 128), ((0, 2), (0, 0))),
+                router_grad.T.reshape(-1, 128),
+            ]
+        )
+        grads, input_grad, small = back_pass(
+            queries, key_rows, value_rows, grad_context, spread, context_t, logsum, query_w, key_w, value_w,
+            bucket_hot, gain_one[None], normed_low, tokens, grad_hidden, out_w_grad, small, groups, experts,
+        )
+        tiles = width // 128
+        first = 8 + rel_table.shape[0]
+        gain_one_grad = small[:tiles].reshape(-1)
+        rel_grad = small[8:first, :heads]
+        gain_two_grad = small[first : first + tiles].reshape(-1)
+        router_grad = small[first + 8 :].reshape(experts, width).T
+    else:
+        query_grad, key_grad, value_grad, diagonals = attend_back(
+            queries, key_rows, value_rows, grad_context, spread, context_t, logsum
+        )
+        diagonals = diagonals[:, :2].reshape(heads, 2 * seq_len)
+        rel_grad = jnp.einsum("bx,hx->bh", bucket_hot, diagonals, precision=highest)
+        grads, input_grad, gain_one_grad, small = tail_native(
+            tokens, gain_one, normed_low, query_grad, key_grad, value_grad,
+            query_w, key_w, value_w, grad_hidden, out_w_grad, (rel_grad, gain_two_grad, router_grad),
+        )
+        rel_grad, gain_two_grad, router_grad = small
     grads = grads.astype(f32)
-    rel_grad = small[2, : rel_flat.shape[1]].reshape(rel_grad.shape)
-    router_grad = small[8:].T
     return (
         output, input_grad, grads[1], grads[2], grads[3], grads[0], rel_grad,
-        small[0], small[1], router_grad, in_share[None], out_share[None],
+        gain_one_grad, gain_two_grad, router_grad, in_share[None], out_share[None],
     )
 
 

time: 393 us -> 380 us (0.967)
  Pallas kernels: 289 us -> 271 us
  starting transfers between devices: 11.4 us -> 19.6 us
    pallas_call x1, Pallas kernels: 96.3 us -> 82.6 us  [expert_pass(): pl.pallas_call(functools.partial(expert_kernel, experts, capacity, tile),...]
    all_to_all x2, starting transfers between devices: 11.4 us -> 19.6 us  [exchange(): lax.all_to_all(rows, 'expert', split_axis=0, concat_axis=0, tiled=True)]
    pallas_call x2 -> x1, Pallas kernels: 151 us -> 146 us  [back_pass(): pl.pallas_call(functools.partial(back_kernel, groups, experts, pairs), gr...]
where the time goes in v3:
time: 380 us; the launch traced here: 373 us
  Pallas kernels  271 us (71%)
  matrix products  34.9 us (9%)
  starting transfers between devices  19.6 us (5%)
  other arithmetic  18.1 us (5%)
  local copies, waits for them, and re-layouts  14.9 us (4%)
  between operations  14.6 us (4%)
    pallas_call x1, Pallas kernels, back_pass(): pl.pallas_call(functools.partial(back_kernel, groups, experts, pairs), gr...  146 us
    pallas_call x1, Pallas kernels, expert_pass(): pl.pallas_call(functools.partial(expert_kernel, experts, capacity, tile),...  82.6 us
    pallas_call x1, Pallas kernels, attend(): pl.pallas_call(attend_kernel, grid=(pairs,), in_specs=[blk, blk, blk, pl....  42.1 us
    dot_general x11, matrix products, contract(): lax.dot_general(left, right, (((dims[0],), (dims[1],)), ((), ())), prefer...  34.7 us
    all_to_all x2, starting transfers between devices, exchange(): lax.all_to_all(rows, 'expert', split_axis=0, concat_axis=0, tiled=True)  19.6 us
  transfers between devices with their start and end apart: 4, of which 0 were waited for; matrix products, arithmetic and copies ran while one was open for 11% of the time, Pallas kernels for 50%

profile of v3, /device:TPU:1, one launch (start us, length us, event | category | flops | bytes accessed | tf_op | source)
XLA Modules:
  0.0 373.5 jit_solution(1714043748201302067)
XLA Ops:
  7.2 0.0 copy-start
  7.2 0.8 fusion.21
  8.0 2.3 reduce-window.6
  10.2 0.3 slice_reduce_fusion
  10.5 0.2 reduce-window.9
  10.7 0.1 add_bitcast_fusion
  10.8 0.7 fusion.20
  11.5 0.7 add_select_fusion
  12.2 5.1 %fusion.4 = bf16[1280,768]{1,0:T(8,128)(2,1)} fusion(bf16[1024,768]{1,0:T(8,128)(2,1)} %param.27, s32[1024]{0:T(1024)S(1)} %add_select_fusion), kind=kOutput, calls=%fused_computation.8 | convolution fusion | flops 2015559680 | bytes 3543040 | tf_op jit(solution)/shard_map/dot_general | solution.py:897
  17.3 0.0 copy-start.20
  17.3 6.5 %all-to-all-start = ((bf16[8,160,768]{2,1,0:T(8,128)(2,1)}), bf16[8,160,768]{2,1,0:T(8,128)(2,1)}, u32[]{:S(2)}, u32[]{:S(2)}) async-start(bf16[8,160,768]{2,1,0:T(8,128)(2,1)} %bitcast.64), calls=%async_computation | async-start | bytes 3932160 | tf_op jit(solution)/shard_map/all_to_all | solution.py:903
  23.8 0.1 pad_add_fusion
  23.9 0.1 rev.3
  24.0 0.2 convolution_bitcast_fusion
  24.2 0.1 reshape.114.u_ref
  24.3 0.2 copy.31
  24.5 0.7 pad.8.rw
  25.2 0.4 fusion.6
  25.6 0.4 fusion.8.nl_h
  26.0 0.4 copy-done.28
  26.5 2.5 convolution_convert_fusion.1.v_ref
  29.0 1.4 convolution_convert_fusion.2.k_ref
  30.4 0.0 copy-start.3
  30.4 1.4 convolution_convert_fusion.3.q_ref
  31.8 42.1 %attend.1 = (bf16[1024,768]{1,0:T(8,128)(2,1)S(1)}, f32[768,1024]{1,0:T(8,128)}, f32[6,8,1024]{2,1,0:T(8,128)S(1)}) custom-call(bf16[1024,768]{1,0:T(8,128)(2,1)S(1)} %convolution_convert_fusion.3.q_ref, bf16[1024,768]{1,0:T(8,128)(2,1)S(1)} %convolution_convert_fusion.2.k_ref, bf16[1024,768]{1,0:T(8,128)(2,1)} %convolution_convert_fusion.1.v_ref, ...), custom_call_target="tpu_custom_call" | custom-call | flops 12884901888 | bytes 15728640 | tf_op jit(solution)/shard_map/attend/pallas_call | solution.py:84
  73.9 1.1 copy-done.4
  75.1 0.7 copy-done.5
  75.7 2.9 multiply_reduce_fusion.2
  78.7 0.6 multiply_multiply_fusion
  79.3 3.9 %fusion.5.xs = bf16[1280,768]{1,0:T(8,128)(2,1)} fusion(s32[1024]{0:T(1024)S(1)} %add_select_fusion, f32[1024,768]{1,0:T(8,128)S(1)} %get-tuple-element.73, f32[768]{0:T(1024)S(1)} %copy-done.17, f32[1024]{0:T(1024)S(1)} %get-tuple-element.71), kind=kOutput, calls=%fused_computation.9 | convolution fusion | flops 2017918976 | bytes 5123072 | tf_op jit(solution)/shard_map/dot_general | solution.py:897
  83.2 82.6 %experts.1 = (bf16[1280,768]{1,0:T(8,128)(2,1)}, bf16[1280,768]{1,0:T(8,128)(2,1)}, bf16[768,3072]{1,0:T(8,128)(2,1)}, bf16[768,3072]{1,0:T(8,128)(2,1)}, f32[768,128]{1,0:T(8,128)}) custom-call(bf16[1280,768]{1,0:T(8,128)(2,1)} %fusion.5.xs, bf16[1280,768]{1,0:T(8,128)(2,1)} %bitcast.5.gr_h, bf16[768,3072]{1,0:T(8,128)(2,1)} %bitcast.72, ...), custom_call_target="tpu_custom_call" | custom-call | flops 36238786560 | bytes 18874368 | tf_op jit(solution)/shard_map/experts/pallas_call | solution.py:414
  165.8 0.0 reduce-scatter.5.cloned.1.call-update
  165.9 0.0 reduce-scatter.3.cloned.1.call-start
  165.9 0.7 reduce-scatter.3.cloned.1.call-update
  166.6 0.6 broadcast_in_dim.19.gain
  167.2 0.5 pad.10.clone
  167.7 0.7 fusion.15.hot
  168.4 13.1 %all-to-all-start.1 = ((bf16[8,160,768]{2,1,0:T(8,128)(2,1)}), bf16[8,160,768]{2,1,0:T(8,128)(2,1)}, u32[]{:S(2)}, u32[]{:S(2)}) async-start(bf16[8,160,768]{2,1,0:T(8,128)(2,1)} %bitcast.63), calls=%async_computation.1 | async-start | bytes 3932160 | tf_op jit(solution)/shard_map/all_to_all | solution.py:903
  181.6 0.1 copy.32
  181.7 0.0 copy-start.13
  181.7 0.0 copy-start.18
  181.7 0.0 copy-start.19
  181.8 5.7 %multiply_reduce_fusion = (f32[768]{0:T(1024)S(1)}, f32[1024]{0:T(1024)S(1)}, f32[1024,768]{1,0:T(8,128)S(1)}) fusion(f32[1024,768]{1,0:T(8,128)} %copy-done.6, f32[1024]{0:T(1024)S(1)} %get-tuple-element.71, f32[768]{0:T(1024)} %param.21, bf16[1280,768]{1,0:T(8,128)(2,1)} %get-tuple-element.29, s32[1024]{0:T(1024)} %copy-done.23), kind=kOutput, calls=%fused_computation.13 | convolution fusion | flops 2019293440 | bytes 8275968 | tf_op jit(solution)/shard_map/dot_general | solution.py:897
  187.5 0.7 fusion.17.small_h
  188.2 1.1 subtract_add_fusion.ghid_h
  189.3 2.6 convolution_convert_fusion.g_ref
  191.9 2.5 convolution_convert_fusion.4.dwo_h
  194.4 145.9 %attend_back.1 = (bf16[4,768,768]{2,1,0:T(8,128)(2,1)}, f32[1024,768]{1,0:T(8,128)}, f32[96,128]{1,0:T(8,128)}) custom-call(bf16[1024,768]{1,0:T(8,128)(2,1)} %copy-done.4, bf16[1024,768]{1,0:T(8,128)(2,1)} %copy-done.3, bf16[1024,768]{1,0:T(8,128)(2,1)} %convolution_convert_fusion.1.v_ref, bf16[1024,768]{1,0:T(8,128)(2,1)} %convolution_convert_fusion.g_ref, ...), custom_call_target="tpu_custom_call" | custom-call | flops 39460012032 | bytes 31457280 | tf_op jit(solution)/shard_map/attend_back/pallas_call | solution.py:817
  340.3 0.7 slice.40
  341.0 0.7 slice.43
  341.7 0.7 copy.33
  342.4 0.6 reshape.124
  343.0 3.3 convert_element_type.73
  346.3 0.0 copy-start.15
  346.3 0.6 fusion.24
  347.0 0.0 copy-done.15
  347.1 1.3 slice_bitcast_fusion.5
  348.3 3.8 %slice_bitcast_fusion = (f32[768,768]{1,0:T(8,128)}, f32[768,768]{1,0:T(8,128)}, f32[768,768]{1,0:T(8,128)}, f32[768,768]{1,0:T(8,128)}) fusion(f32[4,768,768]{2,1,0:T(8,128)S(1)} %convert_element_type.73), kind=kLoop, calls=%fused_computation.23 | loop fusion | bytes 18874368 | tf_op jit(solution)/shard_map/squeeze | solution.py:1043
  352.2 0.0 all-to-all-done.1
  352.2 6.1 %add_convert_fusion = bf16[1024,768]{1,0:T(8,128)(2,1)} fusion(f32[1024,768]{1,0:T(8,128)} %copy-done.6, f32[1024]{0:T(1024)S(1)} %select_reduce_fusion, bf16[1280,768]{1,0:T(8,128)(2,1)} %bitcast.9, s32[1024]{0:T(1024)S(1)} %copy-done.24), kind=kOutput, calls=%fused_computation.16 | convolution fusion | flops 2016935936 | bytes 6692864 | tf_op jit(solution)/shard_map/dot_general | solution.py:897
  358.2 2.9 convert_bitcast_fusion
  361.2 3.1 bitcast_convert_fusion
  364.3 1.7 copy.38
  365.9 0.4 copy-done.1
  (57 shorter events, 0.2 us)
Async XLA Ops:
  7.2 68.6 %copy-start = (bf16[768,768]{1,0:T(8,128)(2,1)S(1)}, bf16[768,768]{1,0:T(8,128)(2,1)}, u32[]{:S(2)}) copy-start(bf16[768,768]{1,0:T(8,128)(2,1)} %param.19) | copy-start | bytes 3538948
  12.2 67.2 %copy-start.23 = (s32[1024]{0:T(1024)}, s32[1024]{0:T(1024)S(1)}, u32[]{:S(2)}) copy-start(s32[1024]{0:T(1024)S(1)} %add_select_fusion) | copy-start | bytes 12292
  17.3 6.5 %copy-start.22 = (s32[2047]{0:T(1024)S(1)}, s32[2047]{0:T(1024)}, u32[]{:S(2)}) copy-start(s32[2047]{0:T(1024)} %param.26) | copy-start | bytes 24568
  17.3 6.7 %copy-start.21 = (f32[32,12]{0,1:T(8,128)S(1)}, f32[32,12]{0,1:T(8,128)}, u32[]{:S(2)}) copy-start(f32[32,12]{0,1:T(8,128)} %param.20) | copy-start | bytes 4612
  17.3 7.0 %copy-start.16 = (bf16[768,8]{0,1:T(8,128)(2,1)S(1)}, bf16[768,8]{0,1:T(8,128)(2,1)}, u32[]{:S(2)}) copy-start(bf16[768,8]{0,1:T(8,128)(2,1)} %param.22) | copy-start | bytes 36868
  17.3 7.9 %copy-start.9 = (bf16[1024,768]{1,0:T(8,128)(2,1)S(1)}, bf16[1024,768]{1,0:T(8,128)(2,1)}, u32[]{:S(2)}) copy-start(bf16[1024,768]{1,0:T(8,128)(2,1)} %tok_h.1) | copy-start | bytes 4718596
  17.3 8.3 %copy-start.20 = (f32[768]{0:T(1024)S(1)}, f32[768]{0:T(1024)}, u32[]{:S(2)}) copy-start(f32[768]{0:T(1024)} %param.15) | copy-start | bytes 9220
  17.3 58.4 %all-to-all-start = ((bf16[8,160,768]{2,1,0:T(8,128)(2,1)}), bf16[8,160,768]{2,1,0:T(8,128)(2,1)}, u32[]{:S(2)}, u32[]{:S(2)}) async-start(bf16[8,160,768]{2,1,0:T(8,128)(2,1)} %bitcast.64), calls=%async_computation | async-start | bytes 3932160 | tf_op jit(solution)/shard_map/all_to_all | solution.py:903
  23.8 334.4 %reduce-scatter.5.cloned.1.call-start = ((), (), s32[]{:S(2)}) async-start(), calls=%async_computation.5 | async-start | bytes 5898240 | tf_op jit(solution)/shard_map/reduce_scatter | solution.py:999
  24.3 7.5 %copy-start.2 = (f32[6,2,2048]{2,1,0:T(2,128)}, f32[6,2,2048]{2,1,0:T(2,128)S(1)}, u32[]{:S(2)}) copy-start(f32[6,2,2048]{2,1,0:T(2,128)S(1)} %reshape.114.u_ref) | copy-start | bytes 294916
  25.2 1.3 copy-start.28
  26.4 3.9 %copy-start.12 = (bf16[1024,768]{1,0:T(8,128)(2,1)}, bf16[1024,768]{1,0:T(8,128)(2,1)S(1)}, u32[]{:S(2)}) copy-start(bf16[1024,768]{1,0:T(8,128)(2,1)S(1)} %fusion.8.nl_h) | copy-start | bytes 4718596
  26.5 2.5 copy-start.27
  29.0 1.4 copy-start.26
  30.4 1.4 copy-start.3
  73.9 1.1 copy-start.4
  75.0 0.7 copy-start.5
  75.7 3.6 copy-start.17
  78.7 4.5 %copy-start.6 = (f32[1024,768]{1,0:T(8,128)}, f32[1024,768]{1,0:T(8,128)S(1)}, u32[]{:S(2)}) copy-start(f32[1024,768]{1,0:T(8,128)S(1)} %get-tuple-element.73) | copy-start | bytes 9437188
  165.9 195.3 %reduce-scatter.3.cloned.1.call-start = ((), (), s32[]{:S(2)}) async-start(), calls=%async_computation.4 | async-start | bytes 5898240 | tf_op jit(solution)/shard_map/reduce_scatter | solution.py:998
  166.6 14.9 %copy-start.14 = (f32[768,128]{1,0:T(8,128)S(1)}, f32[768,128]{1,0:T(8,128)}, u32[]{:S(2)}) copy-start(f32[768,128]{1,0:T(8,128)} %get-tuple-element.32) | copy-start | bytes 1179652
  168.4 183.7 %all-to-all-start.1 = ((bf16[8,160,768]{2,1,0:T(8,128)(2,1)}), bf16[8,160,768]{2,1,0:T(8,128)(2,1)}, u32[]{:S(2)}, u32[]{:S(2)}) async-start(bf16[8,160,768]{2,1,0:T(8,128)(2,1)} %bitcast.63), calls=%async_computation.1 | async-start | bytes 3932160 | tf_op jit(solution)/shard_map/all_to_all | solution.py:903
  181.7 5.8 %copy-start.25 = (f32[96]{0:T(128)S(1)}, f32[96]{0:T(128)}, u32[]{:S(2)}) copy-start(f32[96]{0:T(128)} %pad.10.clone) | copy-start | bytes 1156
  181.7 6.5 %copy-start.7 = (f32[1024,768]{1,0:T(8,128)S(1)}, f32[1024,768]{1,0:T(8,128)}, u32[]{:S(2)}) copy-start(f32[1024,768]{1,0:T(8,128)} %copy-done.6) | copy-start | bytes 9437188
  181.7 6.5 %copy-start.13 = (bf16[1024,768]{1,0:T(8,128)(2,1)S(1)}, bf16[1024,768]{1,0:T(8,128)(2,1)}, u32[]{:S(2)}) copy-start(bf16[1024,768]{1,0:T(8,128)(2,1)} %param.27) | copy-start | bytes 4718596
  181.7 6.5 %copy-start.18 = (f32[768]{0:T(1024)S(1)}, f32[768]{0:T(1024)}, u32[]{:S(2)}) copy-start(f32[768]{0:T(1024)} %param.21) | copy-start | bytes 9220
  181.7 6.5 %copy-start.19 = (f32[1024]{0:T(1024)S(1)}, f32[1024]{0:T(1024)}, u32[]{:S(2)}) copy-start(f32[1024]{0:T(1024)} %get-tuple-element.70) | copy-start | bytes 12292
  189.3 2.6 copy-start.11
  343.0 3.3 copy-start.8
  346.3 0.7 copy-start.15
  348.3 3.8 %copy-start.24 = (s32[1024]{0:T(1024)S(1)}, s32[1024]{0:T(1024)}, u32[]{:S(2)}) copy-start(s32[1024]{0:T(1024)} %copy-done.23) | copy-start | bytes 12292
  361.2 3.1 copy-start.10
  364.3 2.1 copy-start.1
Sparse Core Ops, SparseCore 0:
  166.0 68.9 reduce-scatter.4
  238.0 87.2 reduce-scatter.2

commit v4 on v3

--- a/solution.py
+++ b/solution.py
@@ -241,9 +241,9 @@
 def expert_kernel(
     experts, capacity, tile,
     xs, gr_h, win_h, wout_h, rw,
-    gback_o, prod_o, dwin_o, dwout_o, drw_o,
-    xall, gr, gp, win, wout, act, gpre, gback, gsend, prod, logit, acc_p, acc_g, xt, gpt, stage,
-    send_x, recv_x, send_g, recv_g, local, out_sem,
+    gback_o, prod_o, dwin_o, dwout_o, drw_o, shared_o,
+    xall, gr, gp, win, wout, act, gpre, gback, gsend, prod, logit, acc_p, acc_g, xt, gpt, stage, dwt,
+    send_x, recv_x, send_g, recv_g, local, out_sem, send_s, recv_s,
 ):
     me = lax.axis_index("expert")
     place = me // 2
@@ -254,6 +254,11 @@
     barrier = pltpu.get_barrier_semaphore()
     for k in range(1, experts):
         pl.semaphore_signal(barrier, inc=1, device_id={"expert": lax.rem(me + k, experts)})
+    my_dp = lax.axis_index("dp")
+    dp_x, dp_y = lax.rem(my_dp, 2), my_dp // 2
+    peer_x, peer_y = my_dp + 1 - 2 * dp_x, my_dp + 2 - 4 * dp_y
+    for peer in (peer_x, peer_y):
+        pl.semaphore_signal(barrier, inc=1, device_id={"dp": peer})
     loads = [
         pltpu.make_async_copy(win_h, win, local.at[0]),
         pltpu.make_async_copy(wout_h, wout, local.at[1]),
@@ -264,7 +269,7 @@
     own.start()
     for copy in loads:
         copy.start()
-    pl.semaphore_wait(barrier, experts - 1)
+    pl.semaphore_wait(barrier, experts + 1)
 
     def partner(step):
         high, low = place // 2, lax.rem(place, 2)
@@ -374,24 +379,67 @@
     gpt[...] = gp[...].T
     drw_o[...] = dot_f32(xt[...], logit[...])
 
-    def weight_block(idx, carry):
+    share = width // 4
+    tiles = hidden // tile
+    split = tiles // 2
+
+    def left_copy(idx, block):
         cols = pl.ds(pl.multiple_of(idx * tile, tile), tile)
-
-        def put(slot, out):
-            return pltpu.make_async_copy(stage.at[slot], out.at[:, cols], out_sem.at[slot])
-
-        for slot, (left, right, out) in enumerate(((gpt, act, dwout_o), (xt, gpre, dwin_o))):
-            @pl.when(idx > 0)
-            def _():
-                put(slot, out).wait()
-
-            stage[slot] = dot_f32(left[...], right[:, cols]).astype(bf16)
-            put(slot, out).start()
+        rows = pl.ds(pl.multiple_of((1 - dp_x + 2 * block) * share, 16), share)
+        return pltpu.make_async_remote_copy(
+            src_ref=dwt.at[rows, cols], dst_ref=shared_o.at[pl.ds(block * share, share), cols],
+            send_sem=send_s.at[block, idx], recv_sem=recv_s.at[block, idx], device_id={"dp": peer_x},
+        )
+
+    def right_copy(idx, block):
+        cols = pl.ds(pl.multiple_of(idx * tile, tile), tile)
+        rows = pl.ds(pl.multiple_of((2 - 2 * dp_y + block) * share, 16), share)
+        dst_cols = pl.ds(pl.multiple_of((idx - split) * tile, tile), tile)
+        return pltpu.make_async_remote_copy(
+            src_ref=dwt.at[rows, cols], dst_ref=shared_o.at[pl.ds((2 + block) * share, share), dst_cols],
+            send_sem=send_s.at[block, idx], recv_sem=recv_s.at[block, idx], device_id={"dp": peer_y},
+        )
+
+    def out_block(step, carry):
+        idx = lax.rem(step, 2) * split + step // 2
+        cols = pl.ds(pl.multiple_of(idx * tile, tile), tile)
+        dwt[:, cols] = dot_f32(gpt[...], act[:, cols]).astype(bf16)
+
+        @pl.when(idx < split)
+        def _():
+            for block in range(2):
+                left_copy(idx, block).start()
+
+        @pl.when(idx >= split)
+        def _():
+            for block in range(2):
+                right_copy(idx, block).start()
+
         return carry
 
-    lax.fori_loop(0, hidden // tile, weight_block, 0)
-    for slot, out in enumerate((dwout_o, dwin_o)):
-        pltpu.make_async_copy(stage.at[slot], out.at[:, 0:tile], out_sem.at[slot]).wait()
+    lax.fori_loop(0, tiles, out_block, 0)
+    whole = pltpu.make_async_copy(dwt, dwout_o, local.at[2])
+    whole.start()
+
+    def put(slot, cols):
+        return pltpu.make_async_copy(stage.at[slot], dwin_o.at[:, cols], out_sem.at[slot])
+
+    def in_block(idx, carry):
+        cols = pl.ds(pl.multiple_of(idx * tile, tile), tile)
+        slot = lax.rem(idx, 2)
+
+        @pl.when(idx > 1)
+        def _():
+            put(slot, cols).wait()
+
+        stage[slot] = dot_f32(xt[...], gpre[:, cols]).astype(bf16)
+        put(slot, cols).start()
+        return carry
+
+    lax.fori_loop(0, tiles, in_block, 0)
+    for slot in range(2):
+        put(slot, pl.ds(0, tile)).wait()
+    whole.wait()
     for copy in outs:
         copy.wait()
     for k in range(1, experts):
@@ -401,6 +449,9 @@
         got_back(peer).wait_recv()
     back = pltpu.make_async_copy(gback, gback_o, local.at[1])
     back.start()
+    for idx in range(tiles):
+        for block in range(2):
+            (left_copy if idx < split else right_copy)(idx, block).wait()
     back.wait()
 
 
@@ -414,13 +465,14 @@
     return pl.pallas_call(
         functools.partial(expert_kernel, experts, capacity, tile),
         in_specs=[hbm, hbm, hbm, hbm, vmem],
-        out_specs=[hbm, hbm, hbm, hbm, vmem],
+        out_specs=[hbm, hbm, hbm, hbm, vmem, hbm],
         out_shape=[
             jax.ShapeDtypeStruct((slots, width), bf16),
             jax.ShapeDtypeStruct((slots, width), bf16),
             jax.ShapeDtypeStruct((width, hidden), bf16),
             jax.ShapeDtypeStruct((width, hidden), bf16),
             jax.ShapeDtypeStruct((width, router_pad.shape[1]), f32),
+            jax.ShapeDtypeStruct((width, hidden // 2), bf16),
         ],
         scratch_shapes=[
             pltpu.VMEM((slots, width), bf16),
@@ -439,12 +491,15 @@
             pltpu.VMEM((width, slots), bf16),
             pltpu.VMEM((width, slots), bf16),
             pltpu.VMEM((2, width, tile), bf16),
+            pltpu.VMEM((width, hidden), bf16),
             pltpu.SemaphoreType.DMA((experts,)),
             pltpu.SemaphoreType.DMA((experts,)),
             pltpu.SemaphoreType.DMA((experts,)),
             pltpu.SemaphoreType.DMA((experts,)),
             pltpu.SemaphoreType.DMA((4,)),
             pltpu.SemaphoreType.DMA((2,)),
+            pltpu.SemaphoreType.DMA((2, hidden // tile)),
+            pltpu.SemaphoreType.DMA((2, hidden // tile)),
         ],
         compiler_params=pltpu.CompilerParams(
             vmem_limit_bytes=60 << 20, collective_id=1, has_side_effects=True
@@ -466,16 +521,27 @@
     return [lax.rem(mine + k, count) for k in range(1, count)]
 
 
-LAGS = (1, 4, 9, 13, 15)
+PLAN = (
+    (11, 16, 19, 22, 24),
+    (12, 17, 20, 23, 25),
+    (5, 13, 16, 19, 21),
+    (9, 15, 18, 21, 23),
+    (13, 18, 21, 24, 26),
+    (17, 21, 24, 27, 29),
+    (21, 24, 27, 29, 31),
+)
+EXPERT_SLOTS = ((6, 2, 0), (14, 3, 0), (15, 2, 1), (22, 3, 1))
 
 
 def back_kernel(
     groups, experts, pairs,
     q_ref, k_ref, v_ref, g_ref, u_ref, ctxt_ref, lse_ref, wq, wk, wv, hot, gain, nl_h, tok_h, ghid_h, dwo_h, small_h,
-    wsum_o, ing_o, small_o,
+    eout_h, shared_h, ein_h,
+    wsum_o, ing_o, small_o, esum_o,
     base, acc, kaug, vaug, qaug, gaug, qz, gz, kt, dqt, dall, nt, tok,
-    part, r1, r2, r3, full, sbuf, srecv, sone, stwo,
+    part, r1, r2, r3, full, sbuf, srecv, sone, stwo, keep, other, final,
     send1, recv1, send2, recv2, send3, recv3, send4, recv4, send5, recv5, send6, recv6, send7, recv7, local,
+    send_a, recv_a, send_b, recv_b, out_sem, copy_sem,
 ):
     seq = q_ref.shape[0]
     width = tok.shape[1]
@@ -554,8 +620,123 @@
             copy4(c, peer, peer).wait_recv()
         copy5(c, core).start()
 
+    def put_first(c):
+        return pltpu.make_async_copy(full.at[c], wsum_o.at[0, :, thick * c : thick * c + thick], out_sem.at[c, 0])
+
+    def put_pair(c, which):
+        cols = pl.ds(128 * (c - 2) if isinstance(c, int) else pl.multiple_of(128 * (c - 2), 128), 128)
+        return pltpu.make_async_copy(
+            full.at[c, :, 128 * which : 128 * which + 128], wsum_o.at[1 + which, :, cols], out_sem.at[c, which]
+        )
+
     def stage6(c):
         copy5(c, 1 - core).wait_recv()
+
+        if c < 2:
+            put_first(c).start()
+        else:
+            for which in range(3):
+                put_pair(c, which).start()
+
+    share = width // 4
+    dp_x, dp_y = lax.rem(my_dp, 2), my_dp // 2
+    peer_x, peer_y = my_dp + 1 - 2 * dp_x, my_dp + 2 - 4 * dp_y
+    middle = keep.shape[1]
+    left, right = pl.ds(0, middle), pl.ds(middle, middle)
+
+    def share_rows(which):
+        return pl.ds(pl.multiple_of(which * share, 16), share)
+
+    def first_left(block):
+        return remote(
+            ein_h.at[share_rows(1 - dp_x + 2 * block), left], other.at[1, share_rows(block), :],
+            send_a.at[0, block], recv_a.at[0, block], "dp", peer_x,
+        )
+
+    def first_right(block):
+        return remote(
+            ein_h.at[share_rows(2 - 2 * dp_y + block), right], other.at[1, share_rows(2 + block), :],
+            send_a.at[1, block], recv_a.at[1, block], "dp", peer_y,
+        )
+
+    def second_left(which):
+        return remote(
+            keep.at[share_rows(1 - dp_y), :], final.at[which, :, left],
+            send_b.at[which, 0], recv_b.at[which, 0], "dp", peer_y,
+        )
+
+    def second_right(which):
+        return remote(
+            keep.at[share_rows(2 + 1 - dp_x), :], final.at[which, :, right],
+            send_b.at[which, 1], recv_b.at[which, 1], "dp", peer_x,
+        )
+
+    def own_loads(src):
+        loads = []
+        for block in range(2):
+            loads.append(
+                pltpu.make_async_copy(
+                    src.at[share_rows(dp_x + 2 * block), left], keep.at[share_rows(block), :], copy_sem.at[block]
+                )
+            )
+            loads.append(
+                pltpu.make_async_copy(
+                    src.at[share_rows(2 * dp_y + block), right], keep.at[share_rows(2 + block), :], copy_sem.at[2 + block]
+                )
+            )
+        return loads
+
+    def shared_load():
+        return pltpu.make_async_copy(shared_h, other.at[0], copy_sem.at[4])
+
+    def save(which):
+        return pltpu.make_async_copy(final.at[which], esum_o.at[which], copy_sem.at[5])
+
+    def experts_begin():
+        for copy in own_loads(eout_h) + [shared_load()]:
+            copy.start()
+        for block in range(2):
+            first_left(block).start()
+            first_right(block).start()
+
+    def experts_second(which):
+        for copy in own_loads(eout_h if which == 0 else ein_h):
+            copy.wait()
+        if which == 0:
+            shared_load().wait()
+        else:
+            for block in range(2):
+                first_left(block).wait_recv()
+                first_right(block).wait_recv()
+
+        def block(idx, carry):
+            rows = pl.ds(pl.multiple_of(idx * 64, 64), 64)
+            keep[rows, :] = (keep[rows, :].astype(f32) + other[which, rows, :].astype(f32)).astype(bf16)
+            return carry
+
+        lax.fori_loop(0, width // 64, block, 0)
+        second_left(which).start()
+        second_right(which).start()
+
+    def experts_last(which):
+        second_left(which).wait()
+        second_right(which).wait()
+
+        def block(idx, carry):
+            rows = pl.ds(pl.multiple_of(idx * 64, 64), 64)
+            mine_left = pl.ds(pl.multiple_of(dp_y * share + idx * 64, 64), 64)
+            mine_right = pl.ds(pl.multiple_of((2 + dp_x) * share + idx * 64, 64), 64)
+            final[which, rows, left] = (final[which, rows, left].astype(f32) + keep[mine_left, :].astype(f32)).astype(bf16)
+            final[which, rows, right] = (final[which, rows, right].astype(f32) + keep[mine_right, :].astype(f32)).astype(bf16)
+            return carry
+
+        lax.fori_loop(0, share // 64, block, 0)
+        if which == 0:
+            for copy in own_loads(ein_h):
+                copy.start()
+        else:
+            save(0).wait()
+        save(which).start()
 
     early = pl.ds(8 + hot.shape[0], sbuf.shape[0] - 8 - hot.shape[0])
     late = pl.ds(0, 8 + hot.shape[0])
@@ -599,12 +780,10 @@
     stages = (stage2, stage3, stage4, stage5, stage6)
 
     def advance(slot):
-        for lag, stage in reversed(list(zip(LAGS, stages))):
-            since = slot - lag
-
-            @pl.when((since >= 0) & (since <= 4 * pairs) & ((lax.rem(since, 4) == 0) | (since == 2)))
-            def _():
-                stage(since // 4 + jnp.minimum(since, 1))
+        for c, slots in enumerate(PLAN):
+            for at, stage in reversed(list(zip(slots, stages))):
+                if at < 4 * pairs:
+                    pl.when(slot == at)(functools.partial(stage, c))
 
     loads = [
         pltpu.make_async_copy(nl_h, tok, local.at[0]),
@@ -630,6 +809,7 @@
         stage1(0)
         stage1(1)
         small1(0, early)
+        experts_begin()
 
     mine = pl.ds(pl.multiple_of(128 * pair, 128), 128)
     lane = lax.broadcasted_iota(jnp.int32, (seq, 128), 1)
@@ -687,6 +867,11 @@
         dall[2, rows, mine] = dv.astype(bf16)
         advance(4 * pair + idx)
 
+        for at, task, which in EXPERT_SLOTS:
+            @pl.when(4 * pair + idx == at)
+            def _():
+                (experts_second if task == 2 else experts_last)(which)
+
         @pl.when(4 * pair + idx == 7)
         def _():
             small2(0, early)
@@ -743,16 +928,16 @@
         last = pairs + 1
         first = 4 * pairs
         older = sorted(
-            (4 * c - 4 + lag, c, stage)
-            for c in range(2, last)
-            for lag, stage in zip(LAGS, range(2, 7))
-            if 4 * c - 4 + lag >= first
+            (at, c, stage)
+            for c, slots in enumerate(PLAN)
+            for stage, at in enumerate(slots)
+            if at >= first
         )
 
         def drain(until):
             while older and older[0][0] < first + until:
                 _, c, stage = older.pop(0)
-                stages[stage - 2](c)
+                stages[stage](c)
 
         def tokens_done(lower, upper, gain_grad):
             return lax.fori_loop(lower, upper, token_block, gain_grad)
@@ -777,10 +962,11 @@
         stage5(last)
         stage6(last)
         for c in range(2):
-            wsum_o[0, :, thick * c : thick * c + thick] = full[c]
-        for c in range(pairs):
-            for which in range(3):
-                wsum_o[1 + which, :, 128 * c : 128 * c + 128] = full[c + 2, :, 128 * which : 128 * which + 128]
+            put_first(c).wait()
+        save(1).wait()
+        for block in range(2):
+            first_left(block).wait_send()
+            first_right(block).wait_send()
 
         def finish(c, carry):
             copy1(c).wait_send()
@@ -790,6 +976,12 @@
             for peer in others(chips, place):
                 copy3(c, peer, place).wait_send()
             copy5(c, core).wait_send()
+
+            @pl.when(c >= 2)
+            def _():
+                for which in range(3):
+                    put_pair(c, which).wait()
+
             return carry
 
         lax.fori_loop(0, pairs + 2, finish, 0)
@@ -801,11 +993,13 @@
 
 
 def back_pass(
-    q, k, v, g, u, ctxt, lse, wq, wk, wv, hot, gain, normed_low, tokens, grad_hidden, dwo, small, groups, experts
+    q, k, v, g, u, ctxt, lse, wq, wk, wv, hot, gain, normed_low, tokens, grad_hidden, dwo, small,
+    expert_out_grad, shared, expert_in_grad, groups, experts
 ):
     seq, width = q.shape
     pairs = width // 128
     chunks = pairs + 2
+    hidden = expert_in_grad.shape[1]
     thick = width // 2
     half = width // 2
     piece = half // groups
@@ -824,13 +1018,14 @@
             pl.BlockSpec((1, 8, seq), lambda p: (p, 0, 0)),
             fixed((width, width)), fixed((width, width)), fixed((width, width)),
             fixed(hot.shape), fixed(gain.shape),
-            hbm, hbm, hbm, hbm, hbm,
+            hbm, hbm, hbm, hbm, hbm, hbm, hbm, hbm,
         ],
-        out_specs=[fixed((4, width, width)), fixed((seq, width)), fixed(small.shape)],
+        out_specs=[hbm, fixed((seq, width)), fixed(small.shape), hbm],
         out_shape=[
             jax.ShapeDtypeStruct((4, width, width), bf16),
             jax.ShapeDtypeStruct((seq, width), f32),
             jax.ShapeDtypeStruct(small.shape, f32),
+            jax.ShapeDtypeStruct((2, width // 4, hidden), bf16),
         ],
         scratch_shapes=[
             pltpu.VMEM((2, 128, 2 * seq), f32),
@@ -855,6 +1050,9 @@
             pltpu.VMEM((experts,) + small.shape, f32),
             pltpu.VMEM(small.shape, f32),
             pltpu.VMEM((groups,) + small.shape, f32),
+            pltpu.VMEM((width, hidden // 2), bf16),
+            pltpu.VMEM((2, width, hidden // 2), bf16),
+            pltpu.VMEM((2, width // 4, hidden), bf16),
             dma((chunks,)), dma((chunks,)),
             dma((chunks, groups)), dma((chunks, groups)),
             dma((chunks, chips)), dma((chunks, chips)),
@@ -863,6 +1061,9 @@
             dma((2, experts)), dma((2, experts)),
             dma((2, groups)), dma((2, groups)),
             dma((6,)),
+            dma((2, 2)), dma((2, 2)),
+            dma((2, 2)), dma((2, 2)),
+            dma((chunks, 3)), dma((6,)),
         ],
         compiler_params=pltpu.CompilerParams(
             vmem_limit_bytes=62 << 20, collective_id=2, has_side_effects=True
@@ -872,7 +1073,7 @@
             bytes_accessed=40 * seq * width, transcendentals=seq * seq * 12,
         ),
         name="attend_back",
-    )(q, k, v, g, u, ctxt, lse, wq, wk, wv, hot, gain, normed_low, tokens, grad_hidden, dwo, small)
+    )(q, k, v, g, u, ctxt, lse, wq, wk, wv, hot, gain, normed_low, tokens, grad_hidden, dwo, small, expert_out_grad, shared, expert_in_grad)
 
 
 def rms_backward(grad_norm, values, row_scale, gain_vec):
@@ -986,7 +1187,7 @@
     send = scatter_rows(normed_two_low)
     if kernels:
         router_pad = jnp.pad(router_w, ((0, 0), (0, 128 - experts)))
-        grad_rows, produced, in_grad, out_grad_t, router_grad = expert_pass(
+        grad_rows, produced, in_grad, out_grad_t, router_grad, shared = expert_pass(
             send, grad_recv, weight_in, weight_out, router_pad, experts, capacity
         )
         router_grad = router_grad[:, :experts]
@@ -995,8 +1196,6 @@
             send, grad_recv, weight_in, weight_out, router_w, experts
         )
     returned = exchange(produced, experts)
-    in_share = lax.psum_scatter(in_grad, "dp", scatter_dimension=0, tiled=True).astype(f32)
-    out_share = lax.psum_scatter(out_grad_t, "dp", scatter_dimension=0, tiled=True).astype(f32).T
 
     router_probs = jax.nn.softmax(contract(normed_two_low, router_w, (1, 0)), axis=-1)
     gate_value = jnp.sum(router_probs * route_float, axis=-1, keepdims=True)
@@ -1017,9 +1216,10 @@
                 router_grad.T.reshape(-1, 128),
             ]
         )
-        grads, input_grad, small = back_pass(
+        grads, input_grad, small, shares = back_pass(
             queries, key_rows, value_rows, grad_context, spread, context_t, logsum, query_w, key_w, value_w,
-            bucket_hot, gain_one[None], normed_low, tokens, grad_hidden, out_w_grad, small, groups, experts,
+            bucket_hot, gain_one[None], normed_low, tokens, grad_hidden, out_w_grad, small,
+            out_grad_t, shared, in_grad, groups, experts,
         )
         tiles = width // 128
         first = 8 + rel_table.shape[0]
@@ -1027,7 +1227,10 @@
         rel_grad = small[8:first, :heads]
         gain_two_grad = small[first : first + tiles].reshape(-1)
         router_grad = small[first + 8 :].reshape(experts, width).T
+        out_share, in_share = shares[0], shares[1]
     else:
+        in_share = lax.psum_scatter(in_grad, "dp", scatter_dimension=0, tiled=True)
+        out_share = lax.psum_scatter(out_grad_t, "dp", scatter_dimension=0, tiled=True)
         query_grad, key_grad, value_grad, diagonals = attend_back(
             queries, key_rows, value_rows, grad_context, spread, context_t, logsum
         )
@@ -1041,7 +1244,7 @@
     grads = grads.astype(f32)
     return (
         output, input_grad, grads[1], grads[2], grads[3], grads[0], rel_grad,
-        gain_one_grad, gain_two_grad, router_grad, in_share[None], out_share[None],
+        gain_one_grad, gain_two_grad, router_grad, in_share.astype(f32)[None], out_share.astype(f32).T[None],
     )
 
 

time: 380 us -> 359 us (0.945)
  between operations: 14.6 us -> 1.24 us
  starting transfers between devices: 19.6 us -> 15.6 us
  Pallas kernels: 271 us -> 275 us
  other arithmetic: 18.1 us -> 14.2 us
    pallas_call x1, Pallas kernels: 82.6 us -> 87.5 us  [expert_pass(): pl.pallas_call(functools.partial(expert_kernel, experts, capacity, tile),...]
    all_to_all x2, starting transfers between devices: 19.6 us -> 15.6 us  [exchange(): lax.all_to_all(rows, 'expert', split_axis=0, concat_axis=0, tiled=True)]
  transfers between devices with their start and end apart: 4 -> 2, of which waited for: 0 -> 0; matrix products, arithmetic and copies ran while one was open for 11% -> 7% of each run, Pallas kernels for 50% -> 53%
where the time goes in v4:
time: 359 us; the launch traced here: 355 us
  Pallas kernels  275 us (77%)
  matrix products  34.9 us (10%)
  starting transfers between devices  15.6 us (4%)
  local copies, waits for them, and re-layouts  14.4 us (4%)
  other arithmetic  14.2 us (4%)
    pallas_call x1, Pallas kernels, back_pass(): pl.pallas_call(functools.partial(back_kernel, groups, experts, pairs), gr...  146 us
    pallas_call x1, Pallas kernels, expert_pass(): pl.pallas_call(functools.partial(expert_kernel, experts, capacity, tile),...  87.5 us
    pallas_call x1, Pallas kernels, attend(): pl.pallas_call(attend_kernel, grid=(pairs,), in_specs=[blk, blk, blk, pl....  41.5 us
    dot_general x11, matrix products, contract(): lax.dot_general(left, right, (((dims[0],), (dims[1],)), ((), ())), prefer...  34.7 us
    all_to_all x2, starting transfers between devices, exchange(): lax.all_to_all(rows, 'expert', split_axis=0, concat_axis=0, tiled=True)  15.6 us
  transfers between devices with their start and end apart: 2, of which 0 were waited for; matrix products, arithmetic and copies ran while one was open for 7% of the time, Pallas kernels for 53%

profile of v4, /device:TPU:1, one launch (start us, length us, event | category | flops | bytes accessed | tf_op | source)
XLA Modules:
  0.0 355.3 jit_solution(8785681622513657597)
XLA Ops:
  0.6 0.0 copy-start
  0.7 0.8 fusion.21
  1.4 2.3 reduce-window.6
  3.7 0.3 slice_reduce_fusion
  4.0 0.2 reduce-window.9
  4.1 0.1 add_bitcast_fusion
  4.2 0.7 fusion.20
  4.9 0.7 add_select_fusion
  5.6 5.1 %fusion.4 = bf16[1280,768]{1,0:T(8,128)(2,1)} fusion(bf16[1024,768]{1,0:T(8,128)(2,1)} %param.27, s32[1024]{0:T(1024)S(1)} %add_select_fusion), kind=kOutput, calls=%fused_computation.8 | convolution fusion | flops 2015559680 | bytes 3543040 | tf_op jit(solution)/shard_map/dot_general | solution.py:1098
  10.7 0.0 copy-start.9
  10.8 7.1 %all-to-all-start = ((bf16[8,160,768]{2,1,0:T(8,128)(2,1)}), bf16[8,160,768]{2,1,0:T(8,128)(2,1)}, u32[]{:S(2)}, u32[]{:S(2)}) async-start(bf16[8,160,768]{2,1,0:T(8,128)(2,1)} %bitcast.63), calls=%async_computation | async-start | bytes 3932160 | tf_op jit(solution)/shard_map/all_to_all | solution.py:1104
  17.9 0.0 copy-done.19
  17.9 0.6 broadcast_in_dim.14.gain
  18.5 0.0 copy-done.21
  18.5 0.1 pad_add_fusion
  18.5 0.1 rev.3
  18.6 0.0 copy-done.20
  18.6 0.2 convolution_bitcast_fusion
  18.8 0.1 reshape.116.u_ref
  18.9 0.2 copy.31
  19.1 0.7 pad.8.rw
  19.8 0.0 copy-done.9
  19.8 0.4 fusion.6
  20.2 0.4 fusion.8.nl_h
  20.7 0.4 copy-done.24
  21.1 2.5 convolution_convert_fusion.1.v_ref
  23.6 1.4 convolution_convert_fusion.2.k_ref
  25.1 0.0 copy-start.3
  25.1 1.4 convolution_convert_fusion.3.q_ref
  26.5 0.7 fusion.15.hot
  27.2 0.0 copy-done.3
  27.2 41.5 %attend.1 = (bf16[1024,768]{1,0:T(8,128)(2,1)S(1)}, f32[768,1024]{1,0:T(8,128)}, f32[6,8,1024]{2,1,0:T(8,128)S(1)}) custom-call(bf16[1024,768]{1,0:T(8,128)(2,1)S(1)} %convolution_convert_fusion.3.q_ref, bf16[1024,768]{1,0:T(8,128)(2,1)S(1)} %convolution_convert_fusion.2.k_ref, bf16[1024,768]{1,0:T(8,128)(2,1)} %convolution_convert_fusion.1.v_ref, ...), custom_call_target="tpu_custom_call" | custom-call | flops 12884901888 | bytes 15728640 | tf_op jit(solution)/shard_map/attend/pallas_call | solution.py:84
  68.7 1.1 copy-done.4
  69.9 0.7 copy-done.5
  70.6 0.0 all-to-all-done
  70.6 2.9 multiply_reduce_fusion.2
  73.5 3.9 %fusion.5.xs = bf16[1280,768]{1,0:T(8,128)(2,1)} fusion(s32[1024]{0:T(1024)S(1)} %add_select_fusion, f32[1024,768]{1,0:T(8,128)S(1)} %get-tuple-element.79, f32[768]{0:T(1024)S(1)} %copy-done.18, f32[1024]{0:T(1024)S(1)} %get-tuple-element.77), kind=kOutput, calls=%fused_computation.9 | convolution fusion | flops 2017918976 | bytes 5123072 | tf_op jit(solution)/shard_map/dot_general | solution.py:1098
  77.4 87.5 %experts.1 = (bf16[1280,768]{1,0:T(8,128)(2,1)}, bf16[1280,768]{1,0:T(8,128)(2,1)}, bf16[768,3072]{1,0:T(8,128)(2,1)}, bf16[768,3072]{1,0:T(8,128)(2,1)}, f32[768,128]{1,0:T(8,128)}, /*index=5*/bf16[768,1536]{1,0:T(8,128)(2,1)}) custom-call(bf16[1280,768]{1,0:T(8,128)(2,1)} %fusion.5.xs, bf16[1280,768]{1,0:T(8,128)(2,1)} %bitcast.5.gr_h, ...), custom_call_target="tpu_custom_call" | custom-call | flops 36238786560 | bytes 18874368 | tf_op jit(solution)/shard_map/experts/pallas_call | solution.py:465
  164.9 0.0 copy-start.14
  164.9 5.6 %multiply_reduce_fusion = (f32[768]{0:T(1024)S(1)}, f32[1024]{0:T(1024)S(1)}, f32[1024,768]{1,0:T(8,128)S(1)}) fusion(f32[1024,768]{1,0:T(8,128)} %copy-done.6, f32[1024]{0:T(1024)S(1)} %get-tuple-element.77, f32[768]{0:T(1024)S(1)} %copy-done.18, bf16[1280,768]{1,0:T(8,128)(2,1)} %get-tuple-element.31, s32[1024]{0:T(1024)S(1)} %add_select_fusion), kind=kOutput, calls=%fused_computation.13 | convolution fusion | flops 2019293440 | bytes 8275968 | tf_op jit(solution)/shard_map/dot_general | solution.py:1098
  170.6 1.0 subtract_add_fusion.ghid_h
  171.6 0.0 copy-start.11
  171.6 2.5 convolution_convert_fusion.4.dwo_h
  174.1 2.6 convolution_convert_fusion.g_ref
  176.7 8.5 %all-to-all-start.1 = ((bf16[8,160,768]{2,1,0:T(8,128)(2,1)}), bf16[8,160,768]{2,1,0:T(8,128)(2,1)}, u32[]{:S(2)}, u32[]{:S(2)}) async-start(bf16[8,160,768]{2,1,0:T(8,128)(2,1)} %bitcast.8), calls=%async_computation.1 | async-start | bytes 3932160 | tf_op jit(solution)/shard_map/all_to_all | solution.py:1104
  185.2 0.1 copy.32
  185.4 0.7 fusion.17.small_h
  186.1 145.9 %attend_back.1 = (bf16[4,768,768]{2,1,0:T(8,128)(2,1)}, f32[1024,768]{1,0:T(8,128)}, f32[96,128]{1,0:T(8,128)}, bf16[2,192,3072]{2,1,0:T(8,128)(2,1)}) custom-call(bf16[1024,768]{1,0:T(8,128)(2,1)} %copy-done.4, bf16[1024,768]{1,0:T(8,128)(2,1)} %copy-done.3, bf16[1024,768]{1,0:T(8,128)(2,1)} %convolution_convert_fusion.1.v_ref, ...), custom_call_target="tpu_custom_call" | custom-call | flops 39460012032 | bytes 31457280 | tf_op jit(solution)/shard_map/attend_back/pallas_call | solution.py:1011
  332.0 0.7 slice.46
  332.7 0.7 slice.49
  333.5 0.7 copy.33
  334.2 0.6 reshape.126
  334.8 3.3 convert_element_type.79
  338.1 0.0 copy-start.16
  338.1 0.6 fusion.24
  338.7 0.0 copy-done.16
  338.8 1.3 slice_bitcast_fusion.5
  340.1 3.8 %slice_bitcast_fusion = (f32[768,768]{1,0:T(8,128)}, f32[768,768]{1,0:T(8,128)}, f32[768,768]{1,0:T(8,128)}, f32[768,768]{1,0:T(8,128)}) fusion(f32[4,768,768]{2,1,0:T(8,128)S(1)} %convert_element_type.79), kind=kLoop, calls=%fused_computation.23 | loop fusion | bytes 18874368 | tf_op jit(solution)/shard_map/squeeze | solution.py:1246
  343.9 0.0 copy-done.12
  343.9 2.7 convert_bitcast_fusion
  346.7 0.0 all-to-all-done.1
  346.7 6.2 %add_convert_fusion = bf16[1024,768]{1,0:T(8,128)(2,1)} fusion(f32[1024,768]{1,0:T(8,128)} %copy-done.6, f32[1024]{0:T(1024)S(1)} %select_reduce_fusion, bf16[1280,768]{1,0:T(8,128)(2,1)} %bitcast.9, s32[1024]{0:T(1024)S(1)} %add_select_fusion), kind=kOutput, calls=%fused_computation.16 | convolution fusion | flops 2016935936 | bytes 6692864 | tf_op jit(solution)/shard_map/dot_general | solution.py:1098
  352.9 1.7 copy.38
  354.6 0.4 copy-done.1
  (42 shorter events, 0.2 us)
Async XLA Ops:
  0.6 69.9 %copy-start = (bf16[768,768]{1,0:T(8,128)(2,1)S(1)}, bf16[768,768]{1,0:T(8,128)(2,1)}, u32[]{:S(2)}) copy-start(bf16[768,768]{1,0:T(8,128)(2,1)} %param.19) | copy-start | bytes 3538948
  10.7 7.1 %copy-start.19 = (f32[768]{0:T(1024)S(1)}, f32[768]{0:T(1024)}, u32[]{:S(2)}) copy-start(f32[768]{0:T(1024)} %param.15) | copy-start | bytes 9220
  10.7 7.7 %copy-start.21 = (s32[2047]{0:T(1024)S(1)}, s32[2047]{0:T(1024)}, u32[]{:S(2)}) copy-start(s32[2047]{0:T(1024)} %param.26) | copy-start | bytes 24568
  10.7 7.9 %copy-start.20 = (f32[32,12]{0,1:T(8,128)S(1)}, f32[32,12]{0,1:T(8,128)}, u32[]{:S(2)}) copy-start(f32[32,12]{0,1:T(8,128)} %param.20) | copy-start | bytes 4612
  10.7 8.2 %copy-start.17 = (bf16[768,8]{0,1:T(8,128)(2,1)S(1)}, bf16[768,8]{0,1:T(8,128)(2,1)}, u32[]{:S(2)}) copy-start(bf16[768,8]{0,1:T(8,128)(2,1)} %param.22) | copy-start | bytes 36868
  10.7 9.1 %copy-start.9 = (bf16[1024,768]{1,0:T(8,128)(2,1)S(1)}, bf16[1024,768]{1,0:T(8,128)(2,1)}, u32[]{:S(2)}) copy-start(bf16[1024,768]{1,0:T(8,128)(2,1)} %tok_h.1) | copy-start | bytes 4718596
  10.8 59.8 %all-to-all-start = ((bf16[8,160,768]{2,1,0:T(8,128)(2,1)}), bf16[8,160,768]{2,1,0:T(8,128)(2,1)}, u32[]{:S(2)}, u32[]{:S(2)}) async-start(bf16[8,160,768]{2,1,0:T(8,128)(2,1)} %bitcast.63), calls=%async_computation | async-start | bytes 3932160 | tf_op jit(solution)/shard_map/all_to_all | solution.py:1104
  18.9 8.3 %copy-start.2 = (f32[6,2,2048]{2,1,0:T(2,128)}, f32[6,2,2048]{2,1,0:T(2,128)S(1)}, u32[]{:S(2)}) copy-start(f32[6,2,2048]{2,1,0:T(2,128)S(1)} %reshape.116.u_ref) | copy-start | bytes 294916
  19.8 1.3 copy-start.24
  21.1 3.9 %copy-start.13 = (bf16[1024,768]{1,0:T(8,128)(2,1)}, bf16[1024,768]{1,0:T(8,128)(2,1)S(1)}, u32[]{:S(2)}) copy-start(bf16[1024,768]{1,0:T(8,128)(2,1)S(1)} %fusion.8.nl_h) | copy-start | bytes 4718596
  21.1 2.5 copy-start.23
  23.6 1.4 copy-start.22
  25.1 2.1 copy-start.3
  68.7 1.1 copy-start.4
  69.9 0.7 copy-start.5
  70.6 2.9 copy-start.18
  73.5 3.9 %copy-start.6 = (f32[1024,768]{1,0:T(8,128)}, f32[1024,768]{1,0:T(8,128)S(1)}, u32[]{:S(2)}) copy-start(f32[1024,768]{1,0:T(8,128)S(1)} %get-tuple-element.79) | copy-start | bytes 9437188
  164.9 5.6 %copy-start.7 = (f32[1024,768]{1,0:T(8,128)S(1)}, f32[1024,768]{1,0:T(8,128)}, u32[]{:S(2)}) copy-start(f32[1024,768]{1,0:T(8,128)} %copy-done.6) | copy-start | bytes 9437188
  164.9 5.6 %copy-start.14 = (bf16[1024,768]{1,0:T(8,128)(2,1)S(1)}, bf16[1024,768]{1,0:T(8,128)(2,1)}, u32[]{:S(2)}) copy-start(bf16[1024,768]{1,0:T(8,128)(2,1)} %param.27) | copy-start | bytes 4718596
  171.6 2.5 copy-start.11
  176.7 8.5 %copy-start.15 = (f32[768,128]{1,0:T(8,128)S(1)}, f32[768,128]{1,0:T(8,128)}, u32[]{:S(2)}) copy-start(f32[768,128]{1,0:T(8,128)} %get-tuple-element.34) | copy-start | bytes 1179652
  176.7 170.0 %all-to-all-start.1 = ((bf16[8,160,768]{2,1,0:T(8,128)(2,1)}), bf16[8,160,768]{2,1,0:T(8,128)(2,1)}, u32[]{:S(2)}, u32[]{:S(2)}) async-start(bf16[8,160,768]{2,1,0:T(8,128)(2,1)} %bitcast.8), calls=%async_computation.1 | async-start | bytes 3932160 | tf_op jit(solution)/shard_map/all_to_all | solution.py:1104
  334.8 3.3 copy-start.8
  338.1 0.7 copy-start.16
  340.1 3.8 %copy-start.12 = (bf16[2,192,3072]{2,1,0:T(8,128)(2,1)S(1)}, bf16[2,192,3072]{2,1,0:T(8,128)(2,1)}, u32[]{:S(2)}) copy-start(bf16[2,192,3072]{2,1,0:T(8,128)(2,1)} %get-tuple-element.41) | copy-start | bytes 7077892
  346.7 6.2 %copy-start.10 = (f32[1024,768]{1,0:T(8,128)S(1)}, f32[1024,768]{1,0:T(8,128)}, u32[]{:S(2)}) copy-start(f32[1024,768]{1,0:T(8,128)} %get-tuple-element.96) | copy-start | bytes 9437188
  352.9 2.1 copy-start.1

commit v5 on v4

--- a/solution.py
+++ b/solution.py
@@ -30,7 +30,9 @@
         )
 
 
-def attend_kernel(q_ref, k_ref, v_ref, u_ref, ctx_ref, ctxt_ref, lse_ref, base, qt, vt, s_scr, p_scr):
+def attend_kernel(
+    q_ref, k_ref, v_ref, u_ref, ctx_ref, ctxt_ref, lse_ref, p_h, base, qt, vt, s_scr, p_scr, p_sem
+):
     seq = q_ref.shape[0]
     span = 256
     half = seq
@@ -39,8 +41,19 @@
     for head in range(2):
         fill_toeplitz(base, head, u_ref[0, head : head + 1, :])
     zeros = jnp.zeros((64, span), bf16)
+    pair = pl.program_id(0)
+
+    def save(idx, slot):
+        cols = pl.ds(pl.multiple_of(idx * span, span), span)
+        return pltpu.make_async_copy(p_scr.at[slot], p_h.at[pl.ds(2 * pair, 2), :, cols], p_sem.at[slot])
 
     def step(idx, carry):
+        slot = lax.rem(idx, 2)
+
+        @pl.when((pair > 0) | (idx > 1))
+        def _():
+            save(idx, slot).wait()
+
         cols = pl.ds(pl.multiple_of(idx * span, span), span)
         outs = []
         for head in range(2):
@@ -66,15 +79,21 @@
             inv = 1.0 / total
             for kb in range(seq // 128):
                 rows = slice(128 * kb, 128 * kb + 128)
-                p_scr[head, rows, :] = (s_scr[head, rows, :] * inv).astype(bf16)
+                p_scr[slot, head, rows, :] = (s_scr[head, rows, :] * inv).astype(bf16)
             lse_ref[0, head : head + 1, cols] = peak + jnp.log(total)
-            outs.append(dot_f32(vt[64 * head : 64 * head + 64, :], p_scr[head]))
+            outs.append(dot_f32(vt[64 * head : 64 * head + 64, :], p_scr[slot, head]))
+        save(idx, slot).start()
         both = jnp.concatenate(outs, axis=0)
         ctxt_ref[:, cols] = both
         ctx_ref[cols, :] = both.T.astype(bf16)
         return carry
 
     lax.fori_loop(0, seq // span, step, 0)
+
+    @pl.when(pair == pl.num_programs(0) - 1)
+    def _():
+        for slot in range(2):
+            save(slot, slot).wait()
 
 
 def attend(q, k, v, u):
@@ -89,18 +108,21 @@
             blk,
             pl.BlockSpec((128, seq), lambda p: (p, 0)),
             pl.BlockSpec((1, 8, seq), lambda p: (p, 0, 0)),
+            pl.BlockSpec(memory_space=pl.ANY),
         ],
         out_shape=[
             jax.ShapeDtypeStruct((seq, width), bf16),
             jax.ShapeDtypeStruct((width, seq), f32),
             jax.ShapeDtypeStruct((pairs, 8, seq), f32),
+            jax.ShapeDtypeStruct((2 * pairs, seq, seq), bf16),
         ],
         scratch_shapes=[
             pltpu.VMEM((2, 128, 2 * seq), f32),
             pltpu.VMEM((128, seq), bf16),
             pltpu.VMEM((128, seq), bf16),
             pltpu.VMEM((2, seq, 256), f32),
-            pltpu.VMEM((2, seq, 256), bf16),
+            pltpu.VMEM((2, 2, seq, 256), bf16),
+            pltpu.SemaphoreType.DMA((2,)),
         ],
         compiler_params=pltpu.CompilerParams(vmem_limit_bytes=48 << 20),
         cost_estimate=pl.CostEstimate(
@@ -530,18 +552,19 @@
     (17, 21, 24, 27, 29),
     (21, 24, 27, 29, 31),
 )
+OUTPUT_SLOT = 17
 EXPERT_SLOTS = ((6, 2, 0), (14, 3, 0), (15, 2, 1), (22, 3, 1))
 
 
 def back_kernel(
     groups, experts, pairs,
-    q_ref, k_ref, v_ref, g_ref, u_ref, ctxt_ref, lse_ref, wq, wk, wv, hot, gain, nl_h, tok_h, ghid_h, dwo_h, small_h,
-    eout_h, shared_h, ein_h,
-    wsum_o, ing_o, small_o, esum_o,
-    base, acc, kaug, vaug, qaug, gaug, qz, gz, kt, dqt, dall, nt, tok,
+    q_ref, k_ref, v_ref, g_ref, ctxt_ref, wq, wk, wv, hot, gain, nl_h, tok_h, ghid_h, dwo_h, small_h,
+    eout_h, shared_h, ein_h, p_h, prod_h, hid_h, meta,
+    wsum_o, ing_o, small_o, esum_o, out_o,
+    acc, vaug, gaug, qz, gz, kt, dqt, pbuf, pret, hbuf, obuf, dall, nt, tok,
     part, r1, r2, r3, full, sbuf, srecv, sone, stwo, keep, other, final,
     send1, recv1, send2, recv2, send3, recv3, send4, recv4, send5, recv5, send6, recv6, send7, recv7, local,
-    send_a, recv_a, send_b, recv_b, out_sem, copy_sem,
+    send_a, recv_a, send_b, recv_b, out_sem, copy_sem, p_sem, send_p, recv_p, o_sem,
 ):
     seq = q_ref.shape[0]
     width = tok.shape[1]
@@ -785,6 +808,53 @@
                 if at < 4 * pairs:
                     pl.when(slot == at)(functools.partial(stage, c))
 
+    def load_p(slot_idx, slot):
+        rows = pl.ds(pl.multiple_of(lax.rem(slot_idx, 4) * span, span), span)
+        return pltpu.make_async_copy(p_h.at[pl.ds(2 * (slot_idx // 4), 2), rows, :], pbuf.at[slot], p_sem.at[slot])
+
+    slots_each = pret.shape[0] // experts
+
+    def slot_rows(which):
+        return pl.ds(pl.multiple_of(which * slots_each, 16), slots_each)
+
+    def give_back(peer):
+        return remote(
+            prod_h.at[slot_rows(peer), :], pret.at[slot_rows(me), :], send_p.at[peer], recv_p.at[me], "expert", peer
+        )
+
+    def got_back(peer):
+        return remote(
+            prod_h.at[slot_rows(peer), :], pret.at[slot_rows(peer), :], send_p.at[peer], recv_p.at[peer], "expert", peer
+        )
+
+    def own_back():
+        return pltpu.make_async_copy(prod_h.at[slot_rows(me), :], pret.at[slot_rows(me), :], o_sem.at[0])
+
+    def out_rows(block):
+        return pl.ds(block * span, span)
+
+    def load_hidden(block):
+        return pltpu.make_async_copy(hid_h.at[out_rows(block), :], hbuf, o_sem.at[1])
+
+    def save_out(block):
+        return pltpu.make_async_copy(obuf, out_o.at[out_rows(block), :], o_sem.at[2])
+
+    def output_block(block):
+        if block == 0:
+            own_back().wait()
+            for peer in others(experts, me):
+                got_back(peer).wait_recv()
+        load_hidden(block).wait()
+        where = lax.broadcasted_iota(jnp.int32, (span, pret.shape[0]), 1).astype(f32)
+        pick = jnp.where(meta[out_rows(block), 1:2] == where, 1.0, 0.0).astype(bf16)
+        gathered = dot_f32(pick, pret[...])
+        if block > 0:
+            save_out(block - 1).wait()
+        obuf[...] = (hbuf[...] + meta[out_rows(block), 0:1] * gathered).astype(bf16)
+        save_out(block).start()
+        if (block + 1) * span < seq:
+            load_hidden(block + 1).start()
+
     loads = [
         pltpu.make_async_copy(nl_h, tok, local.at[0]),
         pltpu.make_async_copy(ghid_h, ing_o, local.at[2]),
@@ -802,6 +872,9 @@
             pl.semaphore_signal(barrier, inc=1, device_id={"dp": peer})
         for copy in loads:
             copy.start()
+        load_p(0, 0).start()
+        own_back().start()
+        load_hidden(0).start()
         for copy in loads:
             copy.wait()
         nt[...] = tok[...].T
@@ -810,11 +883,12 @@
         stage1(1)
         small1(0, early)
         experts_begin()
+        for peer in others(experts, me):
+            give_back(peer).start()
 
     mine = pl.ds(pl.multiple_of(128 * pair, 128), 128)
     lane = lax.broadcasted_iota(jnp.int32, (seq, 128), 1)
     gt = g_ref[...].T
-    qtv = q_ref[...].T
     kt[...] = k_ref[...].T
     gtf = gt.astype(f32)
     pad = jnp.zeros((48, seq), bf16)
@@ -822,21 +896,18 @@
     nil = jnp.zeros((seq, 128), bf16)
     acc[...] = jnp.zeros_like(acc)
     for head in range(2):
-        fill_toeplitz(base, head, u_ref[0, head : head + 1, :])
         own = (lane < 64) if head == 0 else (lane >= 64)
         origin = 64 if head == 0 else 0
         extra = jnp.where((lane >= origin) & (lane < origin + 3), one, nil)
-        kaug[head] = jnp.where(own, k_ref[...], extra)
         vaug[head] = jnp.where(own, v_ref[...], extra)
         qz[head] = jnp.where(own, q_ref[...], nil)
         gz[head] = jnp.where(own, g_ref[...], nil)
         rows = slice(64 * head, 64 * head + 64)
-        lse = split_rows(-lse_ref[0, head : head + 1, :])
-        dsum = split_rows(-jnp.sum(gtf[rows] * ctxt_ref[rows, :], axis=0, keepdims=True))
-        for dst, src, aug in ((qaug, qtv, lse), (gaug, gt, dsum)):
-            dst[head, rows, :] = src[rows]
-            dst[head, origin : origin + 16, :] = aug
-            dst[head, origin + 16 : origin + 64, :] = pad
+        gaug[head, rows, :] = gt[rows]
+        gaug[head, origin : origin + 16, :] = split_rows(
+            -jnp.sum(gtf[rows] * ctxt_ref[rows, :], axis=0, keepdims=True)
+        )
+        gaug[head, origin + 16 : origin + 64, :] = pad
 
     dqt[...] = jnp.zeros_like(dqt)
 
@@ -844,21 +915,24 @@
         rows = pl.ds(pl.multiple_of(idx * span, span), span)
         dv = None
         dk = None
+        slot = lax.rem(idx, 2)
+        load_p(4 * pair + idx, slot).wait()
+
+        @pl.when(4 * pair + idx + 1 < 4 * pairs)
+        def _():
+            load_p(4 * pair + idx + 1, 1 - slot).start()
+
         for head in range(2):
-            s = dot_f32(kaug[head, rows, :], qaug[head])
             dp = dot_f32(vaug[head, rows, :], gaug[head])
-            tops = []
             grads = []
-            for piece_idx in range(2):
-                offs = pl.ds(pl.multiple_of(seq - span * idx - 128 * piece_idx, 128), seq)
-                p = jnp.exp(s[128 * piece_idx : 128 * piece_idx + 128] + base[head, :, offs])
-                ds_ = p * dp[128 * piece_idx : 128 * piece_idx + 128]
+            for part_idx in range(2):
+                offs = pl.ds(pl.multiple_of(seq - span * idx - 128 * part_idx, 128), seq)
+                band = slice(128 * part_idx, 128 * part_idx + 128)
+                ds_ = pbuf[slot, head, band, :].astype(f32) * dp[band]
                 acc[head, :, offs] += ds_
-                tops.append(p.astype(bf16))
                 grads.append(ds_.astype(bf16))
-            p = jnp.concatenate(tops, axis=0)
             ds_ = jnp.concatenate(grads, axis=0)
-            now = dot_f32(p, gz[head])
+            now = dot_f32(pbuf[slot, head], gz[head])
             dv = now if dv is None else dv + now
             now = dot_f32(ds_, qz[head])
             dk = now if dk is None else dk + now
@@ -866,6 +940,11 @@
         dall[1, rows, mine] = dk.astype(bf16)
         dall[2, rows, mine] = dv.astype(bf16)
         advance(4 * pair + idx)
+
+        for block in range(seq // span):
+            @pl.when(4 * pair + idx == OUTPUT_SLOT + block)
+            def _():
+                output_block(block)
 
         for at, task, which in EXPERT_SLOTS:
             @pl.when(4 * pair + idx == at)
@@ -964,6 +1043,9 @@
         for c in range(2):
             put_first(c).wait()
         save(1).wait()
+        save_out(seq // span - 1).wait()
+        for peer in others(experts, me):
+            give_back(peer).wait_send()
         for block in range(2):
             first_left(block).wait_send()
             first_right(block).wait_send()
@@ -993,8 +1075,8 @@
 
 
 def back_pass(
-    q, k, v, g, u, ctxt, lse, wq, wk, wv, hot, gain, normed_low, tokens, grad_hidden, dwo, small,
-    expert_out_grad, shared, expert_in_grad, groups, experts
+    q, k, v, g, ctxt, wq, wk, wv, hot, gain, normed_low, tokens, grad_hidden, dwo, small,
+    expert_out_grad, shared, expert_in_grad, weights, produced, hidden_rows, meta, groups, experts
 ):
     seq, width = q.shape
     pairs = width // 128
@@ -1013,31 +1095,32 @@
         grid=(pairs,),
         in_specs=[
             blk, blk, blk, blk,
-            pl.BlockSpec((1, 2, 2 * seq), lambda p: (p, 0, 0)),
             pl.BlockSpec((128, seq), lambda p: (p, 0)),
-            pl.BlockSpec((1, 8, seq), lambda p: (p, 0, 0)),
             fixed((width, width)), fixed((width, width)), fixed((width, width)),
             fixed(hot.shape), fixed(gain.shape),
             hbm, hbm, hbm, hbm, hbm, hbm, hbm, hbm,
+            hbm, hbm, hbm, fixed(meta.shape),
         ],
-        out_specs=[hbm, fixed((seq, width)), fixed(small.shape), hbm],
+        out_specs=[hbm, fixed((seq, width)), fixed(small.shape), hbm, hbm],
         out_shape=[
             jax.ShapeDtypeStruct((4, width, width), bf16),
             jax.ShapeDtypeStruct((seq, width), f32),
             jax.ShapeDtypeStruct(small.shape, f32),
             jax.ShapeDtypeStruct((2, width // 4, hidden), bf16),
+            jax.ShapeDtypeStruct((seq, width), bf16),
         ],
         scratch_shapes=[
             pltpu.VMEM((2, 128, 2 * seq), f32),
-            pltpu.VMEM((2, 128, 2 * seq), f32),
             pltpu.VMEM((2, seq, 128), bf16),
-            pltpu.VMEM((2, seq, 128), bf16),
-            pltpu.VMEM((2, 128, seq), bf16),
             pltpu.VMEM((2, 128, seq), bf16),
             pltpu.VMEM((2, seq, 128), bf16),
             pltpu.VMEM((2, seq, 128), bf16),
             pltpu.VMEM((128, seq), bf16),
             pltpu.VMEM((128, seq), f32),
+            pltpu.VMEM((2, 2, 256, seq), bf16),
+            pltpu.VMEM(produced.shape, bf16),
+            pltpu.VMEM((256, width), f32),
+            pltpu.VMEM((256, width), bf16),
             pltpu.VMEM((3, seq, width), bf16),
             pltpu.VMEM((width, seq), bf16),
             pltpu.VMEM((seq, width), bf16),
@@ -1064,6 +1147,7 @@
             dma((2, 2)), dma((2, 2)),
             dma((2, 2)), dma((2, 2)),
             dma((chunks, 3)), dma((6,)),
+            dma((2,)), dma((experts,)), dma((experts,)), dma((3,)),
         ],
         compiler_params=pltpu.CompilerParams(
             vmem_limit_bytes=62 << 20, collective_id=2, has_side_effects=True
@@ -1073,7 +1157,10 @@
             bytes_accessed=40 * seq * width, transcendentals=seq * seq * 12,
         ),
         name="attend_back",
-    )(q, k, v, g, u, ctxt, lse, wq, wk, wv, hot, gain, normed_low, tokens, grad_hidden, dwo, small, expert_out_grad, shared, expert_in_grad)
+    )(
+        q, k, v, g, ctxt, wq, wk, wv, hot, gain, normed_low, tokens, grad_hidden, dwo, small,
+        expert_out_grad, shared, expert_in_grad, weights, produced, hidden_rows, meta,
+    )
 
 
 def rms_backward(grad_norm, values, row_scale, gain_vec):
@@ -1178,7 +1265,7 @@
     bucket_hot = (jnp.arange(rel_table.shape[0], dtype=jnp.int32)[:, None] == reach[None, :]).astype(f32)
     spread = jnp.einsum("bh,bx->hx", rel_table, bucket_hot, precision=highest)
     spread = spread.reshape(heads // 2, 2, 2 * seq_len)
-    context, context_t, logsum = attend(queries, key_rows, value_rows, spread)
+    context, context_t, logsum, weights = attend(queries, key_rows, value_rows, spread)
     context, grad_recv = lax.optimization_barrier((context, grad_recv))
     hidden = tokens_f + contract(context, out_w, (1, 0))
     normed_two, scale_two = rms_forward(hidden, gain_two)
@@ -1195,11 +1282,9 @@
         grad_rows, produced, in_grad, out_grad_t, router_grad = expert_native(
             send, grad_recv, weight_in, weight_out, router_w, experts
         )
-    returned = exchange(produced, experts)
 
     router_probs = jax.nn.softmax(contract(normed_two_low, router_w, (1, 0)), axis=-1)
     gate_value = jnp.sum(router_probs * route_float, axis=-1, keepdims=True)
-    output = (hidden + gate_value * gather_rows(returned)).astype(bf16)
 
     grad_out = cotangent.astype(f32)
     grad_normed_two = gather_rows(grad_rows)
@@ -1216,10 +1301,11 @@
                 router_grad.T.reshape(-1, 128),
             ]
         )
-        grads, input_grad, small, shares = back_pass(
-            queries, key_rows, value_rows, grad_context, spread, context_t, logsum, query_w, key_w, value_w,
+        grads, input_grad, small, shares, output = back_pass(
+            queries, key_rows, value_rows, grad_context, context_t, query_w, key_w, value_w,
             bucket_hot, gain_one[None], normed_low, tokens, grad_hidden, out_w_grad, small,
-            out_grad_t, shared, in_grad, groups, experts,
+            out_grad_t, shared, in_grad, weights, produced, hidden,
+            jnp.concatenate([gate_value, slot_index[:, None].astype(f32)], axis=1), groups, experts,
         )
         tiles = width // 128
         first = 8 + rel_table.shape[0]
@@ -1229,6 +1315,7 @@
         router_grad = small[first + 8 :].reshape(experts, width).T
         out_share, in_share = shares[0], shares[1]
     else:
+        output = (hidden + gate_value * gather_rows(exchange(produced, experts))).astype(bf16)
         in_share = lax.psum_scatter(in_grad, "dp", scatter_dimension=0, tiled=True)
         out_share = lax.psum_scatter(out_grad_t, "dp", scatter_dimension=0, tiled=True)
         query_grad, key_grad, value_grad, diagonals = attend_back(

time: 359 us -> 344 us (0.958)
  starting transfers between devices: 15.6 us -> 6.74 us
  matrix products: 34.9 us -> 28.7 us
    all_to_all x2 -> x1, starting transfers between devices: 15.6 us -> 6.74 us  [exchange(): lax.all_to_all(rows, 'expert', split_axis=0, concat_axis=0, tiled=True)]
    pallas_call x1, Pallas kernels: 146 us -> 139 us  [back_pass(): pl.pallas_call(functools.partial(back_kernel, groups, experts, pairs), gr...]
    dot_general x11 -> x10, matrix products: 34.7 us -> 28.5 us  [contract(): lax.dot_general(left, right, (((dims[0],), (dims[1],)), ((), ())), prefer...]
    pallas_call x1, Pallas kernels: 41.5 us -> 47.2 us  [attend(): pl.pallas_call(attend_kernel, grid=(pairs,), in_specs=[blk, blk, blk, pl....]
  transfers between devices with their start and end apart: 2 -> 1, of which waited for: 0 -> 0; matrix products, arithmetic and copies ran while one was open for 7% -> 3% of each run, Pallas kernels for 53% -> 14%
where the time goes in v5:
time: 344 us; the launch traced here: 341 us
  Pallas kernels  274 us (80%)
  matrix products  28.7 us (8%)
  local copies, waits for them, and re-layouts  16.4 us (5%)
  other arithmetic  13.4 us (4%)
  starting transfers between devices  6.74 us (2%)
    pallas_call x1, Pallas kernels, back_pass(): pl.pallas_call(functools.partial(back_kernel, groups, experts, pairs), gr...  139 us
    pallas_call x1, Pallas kernels, expert_pass(): pl.pallas_call(functools.partial(expert_kernel, experts, capacity, tile),...  87.5 us
    pallas_call x1, Pallas kernels, attend(): pl.pallas_call(attend_kernel, grid=(pairs,), in_specs=[blk, blk, blk, pl....  47.2 us
    dot_general x10, matrix products, contract(): lax.dot_general(left, right, (((dims[0],), (dims[1],)), ((), ())), prefer...  28.5 us
  transfers between devices with their start and end apart: 1, of which 0 were waited for; matrix products, arithmetic and copies ran while one was open for 3% of the time, Pallas kernels for 14%

profile of v5, /device:TPU:1, one launch (start us, length us, event | category | flops | bytes accessed | tf_op | source)
XLA Modules:
  0.0 340.9 jit_solution(15886938919679531559)
XLA Ops:
  0.6 0.0 copy-start
  0.7 0.8 fusion.19
  1.4 2.3 reduce-window.6
  3.7 0.3 slice_reduce_fusion
  4.0 0.2 reduce-window.9
  4.1 0.1 add_bitcast_fusion
  4.2 0.7 fusion.18
  4.9 0.7 add_select_fusion
  5.6 5.1 %fusion.3 = bf16[1280,768]{1,0:T(8,128)(2,1)} fusion(bf16[1024,768]{1,0:T(8,128)(2,1)} %param.27, s32[1024]{0:T(1024)S(1)} %add_select_fusion), kind=kOutput, calls=%fused_computation.7 | convolution fusion | flops 2015559680 | bytes 3543040 | tf_op jit(solution)/shard_map/dot_general | solution.py:1185
  10.7 0.0 copy-start.14
  10.8 0.0 copy-start.13
  10.8 6.7 %all-to-all-start = ((bf16[8,160,768]{2,1,0:T(8,128)(2,1)}), bf16[8,160,768]{2,1,0:T(8,128)(2,1)}, u32[]{:S(2)}, u32[]{:S(2)}) async-start(bf16[8,160,768]{2,1,0:T(8,128)(2,1)} %bitcast.62), calls=%async_computation | async-start | bytes 3932160 | tf_op jit(solution)/shard_map/all_to_all | solution.py:1191
  17.5 0.6 broadcast_in_dim.18.gain
  18.1 0.4 fusion.5
  18.5 0.1 pad_add_fusion
  18.6 0.1 rev.3
  18.7 0.2 convolution_bitcast_fusion
  18.9 0.1 reshape.117.u_ref
  18.9 0.0 copy-done.14
  19.0 0.2 copy.42
  19.1 0.0 copy-start.21
  19.2 0.7 pad.8.rw
  19.9 0.0 copy-done.13
  19.9 0.4 fusion.7.nl_h
  20.3 0.1 copy-done.21
  20.5 2.5 convolution_convert_fusion.1.v_ref
  23.0 1.4 convolution_convert_fusion.2.k_ref
  24.4 0.0 copy-done.9
  24.4 0.0 copy-done.19
  24.4 0.0 copy-start.1
  24.4 1.4 convolution_convert_fusion.3.q_ref
  25.8 0.7 fusion.13.hot
  26.6 0.0 copy-done.1
  26.6 47.2 %attend.1 = (bf16[1024,768]{1,0:T(8,128)(2,1)S(1)}, f32[768,1024]{1,0:T(8,128)}, f32[6,8,1024]{2,1,0:T(8,128)}, bf16[12,1024,1024]{2,1,0:T(8,128)(2,1)}) custom-call(bf16[1024,768]{1,0:T(8,128)(2,1)S(1)} %convolution_convert_fusion.3.q_ref, bf16[1024,768]{1,0:T(8,128)(2,1)S(1)} %convolution_convert_fusion.2.k_ref, ...), custom_call_target="tpu_custom_call" | custom-call | flops 12884901888 | bytes 15728640 | tf_op jit(solution)/shard_map/attend/pallas_call | solution.py:103
  73.8 0.0 copy-start.2
  73.8 1.1 copy-done.2
  74.9 0.0 all-to-all-done
  74.9 2.9 multiply_reduce_fusion.2
  77.9 0.0 copy-done.15
  77.9 0.6 fusion.23
  78.5 3.9 %fusion.4.xs = bf16[1280,768]{1,0:T(8,128)(2,1)} fusion(s32[1024]{0:T(1024)S(1)} %add_select_fusion, f32[1024,768]{1,0:T(8,128)S(1)} %get-tuple-element.93.hid_h, f32[768]{0:T(1024)S(1)} %copy-done.15, f32[1024]{0:T(1024)S(1)} %get-tuple-element.91), kind=kOutput, calls=%fused_computation.8 | convolution fusion | flops 2017918976 | bytes 5123072 | tf_op jit(solution)/shard_map/dot_general | solution.py:1185
  82.4 0.0 copy-done.3
  82.4 87.5 %experts.1 = (bf16[1280,768]{1,0:T(8,128)(2,1)}, bf16[1280,768]{1,0:T(8,128)(2,1)}, bf16[768,3072]{1,0:T(8,128)(2,1)}, bf16[768,3072]{1,0:T(8,128)(2,1)}, f32[768,128]{1,0:T(8,128)}, /*index=5*/bf16[768,1536]{1,0:T(8,128)(2,1)}) custom-call(bf16[1280,768]{1,0:T(8,128)(2,1)} %fusion.4.xs, bf16[1280,768]{1,0:T(8,128)(2,1)} %bitcast.5.gr_h, ...), custom_call_target="tpu_custom_call" | custom-call | flops 36238786560 | bytes 18874368 | tf_op jit(solution)/shard_map/experts/pallas_call | solution.py:487
  169.9 0.0 copy-start.11
  169.9 5.6 %multiply_reduce_fusion = (f32[768]{0:T(1024)S(1)}, f32[1024]{0:T(1024)S(1)}, f32[1024,768]{1,0:T(8,128)S(1)}) fusion(f32[1024,768]{1,0:T(8,128)} %copy-done.3, f32[1024]{0:T(1024)S(1)} %get-tuple-element.91, f32[768]{0:T(1024)S(1)} %copy-done.15, bf16[1280,768]{1,0:T(8,128)(2,1)} %get-tuple-element.31, s32[1024]{0:T(1024)S(1)} %add_select_fusion), kind=kOutput, calls=%fused_computation.12 | convolution fusion | flops 2019293440 | bytes 8275968 | tf_op jit(solution)/shard_map/dot_general | solution.py:1185
  175.5 1.0 subtract_add_fusion.ghid_h
  176.5 2.5 convolution_convert_fusion.4.dwo_h
  179.0 0.0 copy-done.8
  179.0 2.6 convolution_convert_fusion.g_ref
  181.7 1.0 copy.44.meta
  182.8 0.1 copy.43
  182.9 0.7 fusion.15.small_h
  183.6 139.5 %attend_back.1 = (bf16[4,768,768]{2,1,0:T(8,128)(2,1)}, f32[1024,768]{1,0:T(8,128)}, f32[96,128]{1,0:T(8,128)}, bf16[2,192,3072]{2,1,0:T(8,128)(2,1)}, bf16[1024,768]{1,0:T(8,128)(2,1)}) custom-call(bf16[1024,768]{1,0:T(8,128)(2,1)} %copy-done.2, bf16[1024,768]{1,0:T(8,128)(2,1)} %copy-done.1, bf16[1024,768]{1,0:T(8,128)(2,1)} %convolution_convert_fusion.1.v_ref, ...), custom_call_target="tpu_custom_call" | custom-call | flops 39460012032 | bytes 31457280 | tf_op jit(solution)/shard_map/attend_back/pallas_call | solution.py:1093
  323.1 1.3 slice_bitcast_fusion.5
  324.4 0.7 slice.46
  325.1 0.7 slice.49
  325.8 0.7 copy.45
  326.5 0.6 reshape.125
  327.1 4.5 %convert_bitcast_fusion = (f32[1,3072,192]{1,2,0:T(8,128)}, f32[1,192,3072]{2,1,0:T(8,128)}) fusion(bf16[2,192,3072]{2,1,0:T(8,128)(2,1)} %get-tuple-element.43), kind=kLoop, calls=%fused_computation.24 | loop fusion | flops 1179648 | bytes 7077888 | tf_op jit(solution)/shard_map/broadcast_in_dim | solution.py:1334
  331.7 0.8 convert_element_type.81
  332.5 3.8 %slice_bitcast_fusion = (f32[768,768]{1,0:T(8,128)}, f32[768,768]{1,0:T(8,128)}, f32[768,768]{1,0:T(8,128)}, f32[768,768]{1,0:T(8,128)}) fusion(f32[4,768,768]{2,1,0:T(8,128)S(1)} %convert_element_type.81), kind=kLoop, calls=%fused_computation.20 | loop fusion | bytes 18874368 | tf_op jit(solution)/shard_map/squeeze | solution.py:1333
  336.3 1.1 copy.51
  337.5 1.3 copy-done.7
  338.8 1.7 copy.52
  (37 shorter events, 0.2 us)
Async XLA Ops:
  0.6 74.3 %copy-start = (bf16[768,768]{1,0:T(8,128)(2,1)S(1)}, bf16[768,768]{1,0:T(8,128)(2,1)}, u32[]{:S(2)}) copy-start(bf16[768,768]{1,0:T(8,128)(2,1)} %param.19) | copy-start | bytes 3538948
  10.7 6.8 %copy-start.16 = (f32[768]{0:T(1024)S(1)}, f32[768]{0:T(1024)}, u32[]{:S(2)}) copy-start(f32[768]{0:T(1024)} %param.15) | copy-start | bytes 9220
  10.7 7.4 %copy-start.5 = (bf16[1024,768]{1,0:T(8,128)(2,1)S(1)}, bf16[1024,768]{1,0:T(8,128)(2,1)}, u32[]{:S(2)}) copy-start(bf16[1024,768]{1,0:T(8,128)(2,1)} %tok_h.1) | copy-start | bytes 4718596
  10.7 7.8 %copy-start.18 = (s32[2047]{0:T(1024)S(1)}, s32[2047]{0:T(1024)}, u32[]{:S(2)}) copy-start(s32[2047]{0:T(1024)} %param.26) | copy-start | bytes 24568
  10.7 7.9 %copy-start.17 = (f32[32,12]{0,1:T(8,128)S(1)}, f32[32,12]{0,1:T(8,128)}, u32[]{:S(2)}) copy-start(f32[32,12]{0,1:T(8,128)} %param.20) | copy-start | bytes 4612
  10.7 8.2 %copy-start.14 = (bf16[768,8]{0,1:T(8,128)(2,1)S(1)}, bf16[768,8]{0,1:T(8,128)(2,1)}, u32[]{:S(2)}) copy-start(bf16[768,8]{0,1:T(8,128)(2,1)} %param.22) | copy-start | bytes 36868
  10.8 9.1 %copy-start.13 = (s32[1024,1]{0,1:T(1,128)S(1)}, s32[1024,1]{0,1:T(1,128)}, u32[]{:S(2)}) copy-start(s32[1024,1]{0,1:T(1,128)} %param.25) | copy-start | bytes 12292
  10.8 64.2 %all-to-all-start = ((bf16[8,160,768]{2,1,0:T(8,128)(2,1)}), bf16[8,160,768]{2,1,0:T(8,128)(2,1)}, u32[]{:S(2)}, u32[]{:S(2)}) async-start(bf16[8,160,768]{2,1,0:T(8,128)(2,1)} %bitcast.62), calls=%async_computation | async-start | bytes 3932160 | tf_op jit(solution)/shard_map/all_to_all | solution.py:1191
  19.1 1.3 copy-start.21
  20.5 3.9 %copy-start.9 = (bf16[1024,768]{1,0:T(8,128)(2,1)}, bf16[1024,768]{1,0:T(8,128)(2,1)S(1)}, u32[]{:S(2)}) copy-start(bf16[1024,768]{1,0:T(8,128)(2,1)S(1)} %fusion.7.nl_h) | copy-start | bytes 4718596
  20.5 2.5 copy-start.20
  23.0 1.4 copy-start.19
  24.4 2.1 copy-start.1
  73.8 1.1 copy-start.2
  74.9 2.9 copy-start.15
  77.9 4.5 %copy-start.3 = (f32[1024,768]{1,0:T(8,128)}, f32[1024,768]{1,0:T(8,128)S(1)}, u32[]{:S(2)}) copy-start(f32[1024,768]{1,0:T(8,128)S(1)} %get-tuple-element.93.hid_h) | copy-start | bytes 9437188
  169.9 5.6 %copy-start.4 = (f32[1024,768]{1,0:T(8,128)S(1)}, f32[1024,768]{1,0:T(8,128)}, u32[]{:S(2)}) copy-start(f32[1024,768]{1,0:T(8,128)} %copy-done.3) | copy-start | bytes 9437188
  169.9 5.6 %copy-start.11 = (bf16[1024,768]{1,0:T(8,128)(2,1)S(1)}, bf16[1024,768]{1,0:T(8,128)(2,1)}, u32[]{:S(2)}) copy-start(bf16[1024,768]{1,0:T(8,128)(2,1)} %param.27) | copy-start | bytes 4718596
  176.5 2.5 copy-start.8
  179.0 3.7 %copy-start.12 = (f32[768,128]{1,0:T(8,128)S(1)}, f32[768,128]{1,0:T(8,128)}, u32[]{:S(2)}) copy-start(f32[768,128]{1,0:T(8,128)} %get-tuple-element.33) | copy-start | bytes 1179652
  327.1 4.5 %copy-start.6 = (bf16[4,768,768]{2,1,0:T(8,128)(2,1)S(1)}, bf16[4,768,768]{2,1,0:T(8,128)(2,1)}, u32[]{:S(2)}) copy-start(bf16[4,768,768]{2,1,0:T(8,128)(2,1)} %get-tuple-element.41) | copy-start | bytes 14155780
  332.5 3.8 %copy-start.10 = (bf16[1024,768]{1,0:T(8,128)(2,1)S(1)}, bf16[1024,768]{1,0:T(8,128)(2,1)}, u32[]{:S(2)}) copy-start(bf16[1024,768]{1,0:T(8,128)(2,1)} %get-tuple-element.109) | copy-start | bytes 4718596
  336.3 2.5 copy-start.7

commit v6 on v5

--- a/solution.py
+++ b/solution.py
@@ -31,7 +31,8 @@
 
 
 def attend_kernel(
-    q_ref, k_ref, v_ref, u_ref, ctx_ref, ctxt_ref, lse_ref, p_h, base, qt, vt, s_scr, p_scr, p_sem
+    experts, q_ref, k_ref, v_ref, u_ref, gsend_h, ctx_ref, ctxt_ref, lse_ref, p_h, grecv_h,
+    base, qt, vt, s_scr, p_scr, p_sem, send_g, recv_g, own_sem,
 ):
     seq = q_ref.shape[0]
     span = 256
@@ -42,6 +43,26 @@
         fill_toeplitz(base, head, u_ref[0, head : head + 1, :])
     zeros = jnp.zeros((64, span), bf16)
     pair = pl.program_id(0)
+
+    if experts:
+        me = lax.axis_index("expert")
+        count = grecv_h.shape[0] // experts
+        rows_of = lambda who: pl.ds(pl.multiple_of(who * count, 16), count)
+        peers = [lax.rem(me + k, experts) for k in range(1, experts)]
+        barrier = pltpu.get_barrier_semaphore()
+        own = pltpu.make_async_copy(gsend_h.at[rows_of(me), :], grecv_h.at[rows_of(me), :], own_sem)
+
+        def give(peer, slot):
+            return pltpu.make_async_remote_copy(
+                src_ref=gsend_h.at[rows_of(peer), :], dst_ref=grecv_h.at[rows_of(slot), :],
+                send_sem=send_g.at[peer], recv_sem=recv_g.at[slot], device_id={"expert": peer},
+            )
+
+        @pl.when(pair == 0)
+        def _():
+            for peer in peers:
+                pl.semaphore_signal(barrier, inc=1, device_id={"expert": peer})
+            own.start()
 
     def save(idx, slot):
         cols = pl.ds(pl.multiple_of(idx * span, span), span)
@@ -86,6 +107,13 @@
         both = jnp.concatenate(outs, axis=0)
         ctxt_ref[:, cols] = both
         ctx_ref[cols, :] = both.T.astype(bf16)
+        if experts:
+            @pl.when((pair == 0) & (idx == 0))
+            def _():
+                pl.semaphore_wait(barrier, experts - 1)
+                for peer in peers:
+                    give(peer, me).start()
+
         return carry
 
     lax.fori_loop(0, seq // span, step, 0)
@@ -94,20 +122,29 @@
     def _():
         for slot in range(2):
             save(slot, slot).wait()
-
-
-def attend(q, k, v, u):
+        if experts:
+            own.wait()
+            for peer in peers:
+                give(peer, me).wait_send()
+                give(peer, peer).wait_recv()
+
+
+def attend(q, k, v, u, gsend, experts=0):
     seq, width = q.shape
     pairs = width // 128
     blk = pl.BlockSpec((seq, 128), lambda p: (0, p))
+    dma = pltpu.SemaphoreType.DMA
     return pl.pallas_call(
-        attend_kernel,
+        functools.partial(attend_kernel, experts),
         grid=(pairs,),
-        in_specs=[blk, blk, blk, pl.BlockSpec((1, 2, 2 * seq), lambda p: (p, 0, 0))],
+        in_specs=[
+            blk, blk, blk, pl.BlockSpec((1, 2, 2 * seq), lambda p: (p, 0, 0)), pl.BlockSpec(memory_space=pl.ANY),
+        ],
         out_specs=[
             blk,
             pl.BlockSpec((128, seq), lambda p: (p, 0)),
             pl.BlockSpec((1, 8, seq), lambda p: (p, 0, 0)),
+            pl.BlockSpec(memory_space=pl.ANY),
             pl.BlockSpec(memory_space=pl.ANY),
         ],
         out_shape=[
@@ -115,6 +152,7 @@
             jax.ShapeDtypeStruct((width, seq), f32),
             jax.ShapeDtypeStruct((pairs, 8, seq), f32),
             jax.ShapeDtypeStruct((2 * pairs, seq, seq), bf16),
+            jax.ShapeDtypeStruct(gsend.shape, bf16),
         ],
         scratch_shapes=[
             pltpu.VMEM((2, 128, 2 * seq), f32),
@@ -122,14 +160,69 @@
             pltpu.VMEM((128, seq), bf16),
             pltpu.VMEM((2, seq, 256), f32),
             pltpu.VMEM((2, 2, seq, 256), bf16),
-            pltpu.SemaphoreType.DMA((2,)),
+            dma((2,)),
+            dma((max(experts, 1),)), dma((max(experts, 1),)), dma(()),
         ],
-        compiler_params=pltpu.CompilerParams(vmem_limit_bytes=48 << 20),
-        cost_estimate=pl.CostEstimate(
-            flops=16 * seq * seq * width, bytes_accessed=20 * seq * width, transcendentals=seq * seq * 12
+        compiler_params=pltpu.CompilerParams(
+            vmem_limit_bytes=48 << 20, has_side_effects=experts > 0, collective_id=3 if experts else None
         ),
         name="attend",
-    )(q, k, v, u)
+    )(q, k, v, u, gsend)
+
+
+def first_kernel(
+    capacity, experts, tok, gain, wq, wk, wv, route, cot, q_o, k_o, v_o, nl_o, gsend_o, slot_o, slot
+):
+    step = pl.program_id(0)
+    slots = experts * capacity
+    seq = route.shape[1]
+
+    @pl.when(step == 0)
+    def _():
+        lane = lax.broadcasted_iota(jnp.int32, (8, seq), 1)
+        hot = jnp.where(lax.broadcasted_iota(jnp.int32, (8, seq), 0) == route[...], 1.0, 0.0)
+        count = hot
+        shift = 1
+        while shift < seq:
+            count = count + jnp.where(lane >= shift, pltpu.roll(count, shift, 1), 0.0)
+            shift *= 2
+        position = jnp.sum(hot * (count - 1.0), axis=0, keepdims=True)
+        place = route[...].astype(f32) * capacity + position
+        slot[...] = jnp.where(position < capacity, place, float(slots))
+        slot_o[...] = slot[...]
+
+    values = tok[...].astype(f32)
+    scale = lax.rsqrt(jnp.mean(values * values, axis=-1, keepdims=True) + epsilon)
+    normed = (values * scale * gain[...]).astype(bf16)
+    nl_o[...] = normed
+    for weight, out in ((wq, q_o), (wk, k_o), (wv, v_o)):
+        out[...] = dot_f32(normed, weight[...]).astype(bf16)
+    rows = gsend_o.shape[0]
+    number = lax.broadcasted_iota(jnp.int32, (rows, seq), 0) + step * rows
+    pick = jnp.where(number.astype(f32) == slot[...], 1.0, 0.0).astype(bf16)
+    gsend_o[...] = dot_f32(pick, cot[...]).astype(bf16)
+
+
+def first_pass(tokens, gain, wq, wk, wv, route, cotangent, capacity, experts):
+    seq, width = tokens.shape
+    slots = experts * capacity
+    steps = 4
+    rows = pl.BlockSpec((seq // steps, width), lambda i: (i, 0))
+    fixed = lambda shape: pl.BlockSpec(shape, lambda i: (0, 0))
+    return pl.pallas_call(
+        functools.partial(first_kernel, capacity, experts),
+        grid=(steps,),
+        in_specs=[rows, fixed(gain.shape)] + [fixed(wq.shape)] * 3 + [fixed(route.shape), fixed(cotangent.shape)],
+        out_specs=[rows] * 4 + [pl.BlockSpec((slots // steps, width), lambda i: (i, 0)), fixed(route.shape)],
+        out_shape=[jax.ShapeDtypeStruct((seq, width), bf16)] * 4
+        + [jax.ShapeDtypeStruct((slots, width), bf16), jax.ShapeDtypeStruct(route.shape, f32)],
+        scratch_shapes=[pltpu.VMEM(route.shape, f32)],
+        compiler_params=pltpu.CompilerParams(vmem_limit_bytes=40 << 20),
+        cost_estimate=pl.CostEstimate(
+            flops=6 * seq * width * width + 2 * slots * seq * width, bytes_accessed=20 * seq * width, transcendentals=seq
+        ),
+        name="first",
+    )(tokens, gain, wq, wk, wv, route, cotangent)
 
 
 def split_rows(row):
@@ -1253,20 +1346,28 @@
     def gather_rows(rows):
         return contract(pick, rows, (0, 0))
 
-    grad_recv = exchange(scatter_rows(cotangent), experts)
-
     tokens_f = tokens.astype(f32)
-    normed, scale_one = rms_forward(tokens_f, gain_one)
-    normed_low = normed.astype(bf16)
-    queries = contract(normed_low, query_w, (1, 0)).astype(bf16)
-    key_rows = contract(normed_low, key_w, (1, 0)).astype(bf16)
-    value_rows = contract(normed_low, value_w, (1, 0)).astype(bf16)
+    if kernels:
+        queries, key_rows, value_rows, normed_low, grad_send, slot_row = first_pass(
+            tokens, gain_one[None], query_w, key_w, value_w, routes.reshape(1, seq_len), cotangent, capacity, experts
+        )
+        slot_index = slot_row[0].astype(jnp.int32)
+        pick = (jnp.arange(slots, dtype=jnp.int32)[:, None] == slot_index[None, :]).astype(bf16)
+    else:
+        grad_send = scatter_rows(cotangent)
+        normed_low = rms_forward(tokens_f, gain_one)[0].astype(bf16)
+        queries = contract(normed_low, query_w, (1, 0)).astype(bf16)
+        key_rows = contract(normed_low, key_w, (1, 0)).astype(bf16)
+        value_rows = contract(normed_low, value_w, (1, 0)).astype(bf16)
     reach = jnp.concatenate([buckets, jnp.full((1,), -1, jnp.int32)])[::-1]
     bucket_hot = (jnp.arange(rel_table.shape[0], dtype=jnp.int32)[:, None] == reach[None, :]).astype(f32)
     spread = jnp.einsum("bh,bx->hx", rel_table, bucket_hot, precision=highest)
     spread = spread.reshape(heads // 2, 2, 2 * seq_len)
-    context, context_t, logsum, weights = attend(queries, key_rows, value_rows, spread)
-    context, grad_recv = lax.optimization_barrier((context, grad_recv))
+    context, context_t, logsum, weights, grad_recv = attend(
+        queries, key_rows, value_rows, spread, grad_send, experts if kernels else 0
+    )
+    if not kernels:
+        grad_recv = exchange(grad_send, experts)
     hidden = tokens_f + contract(context, out_w, (1, 0))
     normed_two, scale_two = rms_forward(hidden, gain_two)
     normed_two_low = normed_two.astype(bf16)

time: 344 us -> 344 us (level)
  Pallas kernels: 274 us -> 286 us
  local copies, waits for them, and re-layouts: 16.4 us -> 27.7 us
  matrix products: 28.7 us -> 19.5 us
  starting transfers between devices: 6.74 us -> 0 us
  other arithmetic: 13.4 us -> 8.63 us
    pallas_call x1 -> x2, Pallas kernels: 47.2 us -> 60.1 us  [the longest x1 51.7 us: attend(): pl.pallas_call(functools.partial(attend_kernel, experts), grid=(pairs,),...]
    unnamed x48 -> x56, local copies, waits for them, and re-layouts: 6.32 us -> 16.7 us
    dot_general x10 -> x6, matrix products: 28.5 us -> 18.6 us  [contract(): lax.dot_general(left, right, (((dims[0],), (dims[1],)), ((), ())), prefer...]
    all_to_all x1 -> x0, starting transfers between devices: 6.74 us -> none  [exchange(): lax.all_to_all(rows, 'expert', split_axis=0, concat_axis=0, tiled=True)]
  transfers between devices with their start and end apart: 1 -> 0, of which waited for: 0 -> 0; matrix products, arithmetic and copies ran while one was open for 3% -> 0% of each run, Pallas kernels for 14% -> 0%
where the time goes in v6:
time: 344 us; the launch traced here: 343 us
  Pallas kernels  286 us (83%)
  local copies, waits for them, and re-layouts  27.7 us (8%)
  matrix products  19.5 us (6%)
  other arithmetic  8.63 us (3%)
    pallas_call x1, Pallas kernels, back_pass(): pl.pallas_call(functools.partial(back_kernel, groups, experts, pairs), gr...  138 us
    pallas_call x1, Pallas kernels, expert_pass(): pl.pallas_call(functools.partial(expert_kernel, experts, capacity, tile),...  87.6 us
    pallas_call x1, Pallas kernels, attend(): pl.pallas_call(functools.partial(attend_kernel, experts), grid=(pairs,),...  51.7 us
    dot_general x6, matrix products, contract(): lax.dot_general(left, right, (((dims[0],), (dims[1],)), ((), ())), prefer...  18.6 us
    unnamed x56, local copies, waits for them, and re-layouts  16.7 us
    pallas_call x1, Pallas kernels, first_pass(): pl.pallas_call(functools.partial(first_kernel, capacity, experts), grid=(...  8.34 us

profile of v6, /device:TPU:1, one launch (start us, length us, event | category | flops | bytes accessed | tf_op | source)
XLA Modules:
  0.0 342.8 jit_solution(8843668382985244344)
XLA Ops:
  0.6 0.0 copy-start
  0.7 0.8 broadcast_in_dim.11.gain
  1.5 0.8 pad_add_fusion
  2.2 0.1 rev.3
  2.3 0.9 convolution_bitcast_fusion
  3.2 0.1 reshape.86.u_ref
  3.3 0.9 copy.37
  4.2 0.7 pad.8.rw
  4.9 0.7 fusion.7.hot
  5.6 1.4 copy-done.5
  7.0 0.7 copy-done.7
  7.7 1.4 copy-done.10
  9.1 1.3 copy-done.14
  10.4 1.3 copy-done.15
  11.7 1.3 copy-done.16
  12.9 8.3 %first.1 = (bf16[1024,768]{1,0:T(8,128)(2,1)S(1)}, bf16[1024,768]{1,0:T(8,128)(2,1)S(1)}, bf16[1024,768]{1,0:T(8,128)(2,1)S(1)}, bf16[1024,768]{1,0:T(8,128)(2,1...) custom-call(bf16[1024,768]{1,0:T(8,128)(2,1)S(1)} %copy-done.10, f32[1,768]{1,0:T(1,128)S(1)} %broadcast_in_dim.11.gain, ...), custom_call_target="tpu_custom_call" | custom-call | flops 5637144576 | bytes 15728640 | tf_op jit(solution)/shard_map/first/pallas_call | solution.py:212
  21.3 0.0 copy-done.9
  21.3 1.1 copy-done.4
  22.4 1.1 copy-done.17
  23.6 0.0 copy-start.11
  23.6 51.7 %attend.1 = (bf16[1024,768]{1,0:T(8,128)(2,1)S(1)}, f32[768,1024]{1,0:T(8,128)}, f32[6,8,1024]{2,1,0:T(8,128)}, bf16[12,1024,1024]{2,1,0:T(8,128)(2,1)}, bf16[1280,768]{1,0:T(8,128)(2,1)}) custom-call(bf16[1024,768]{1,0:T(8,128)(2,1)S(1)} %get-tuple-element.33.q_ref, bf16[1024,768]{1,0:T(8,128)(2,1)S(1)} %get-tuple-element.34.k_ref, ...), custom_call_target="tpu_custom_call" | custom-call | tf_op jit(solution)/shard_map/attend/pallas_call | solution.py:137
  75.3 0.0 copy-done.2
  75.3 0.0 copy-done.3
  75.3 0.0 copy-start.12
  75.3 0.0 copy-done
  75.4 0.0 copy-done.11
  75.4 0.0 copy-start.24
  75.4 0.0 copy-start.25
  75.4 1.6 multiply_reduce_fusion.2
  76.9 0.0 copy-done.12
  77.0 0.0 copy-start.18
  77.0 0.0 copy-start.8
  77.0 0.0 copy-done.24
  77.0 0.0 copy-done.25
  77.0 0.6 fusion.13
  77.7 0.0 copy-done.8
  77.7 0.9 copy-done.18
  78.6 1.0 copy.39.meta
  79.7 5.8 %fusion.2.xs = bf16[1280,768]{1,0:T(8,128)(2,1)} fusion(s32[1024]{0:T(1024)S(1)} %bitcast.44, f32[1024,768]{1,0:T(8,128)} %copy-done.18, f32[768]{0:T(1024)S(1)} %copy-done.25, f32[1024]{0:T(1024)S(1)} %get-tuple-element.103), kind=kOutput, calls=%fused_computation.3 | convolution fusion | flops 2017918976 | bytes 5123072 | tf_op jit(solution)/shard_map/dot_general | solution.py:1278
  85.4 87.6 %experts.1 = (bf16[1280,768]{1,0:T(8,128)(2,1)}, bf16[1280,768]{1,0:T(8,128)(2,1)}, bf16[768,3072]{1,0:T(8,128)(2,1)}, bf16[768,3072]{1,0:T(8,128)(2,1)}, f32[768,128]{1,0:T(8,128)}, /*index=5*/bf16[768,1536]{1,0:T(8,128)(2,1)}) custom-call(bf16[1280,768]{1,0:T(8,128)(2,1)} %fusion.2.xs, bf16[1280,768]{1,0:T(8,128)(2,1)} %get-tuple-element.39.gr_h, ...), custom_call_target="tpu_custom_call" | custom-call | flops 36238786560 | bytes 18874368 | tf_op jit(solution)/shard_map/experts/pallas_call | solution.py:580
  173.0 1.0 slice_bitcast_fusion.4
  174.0 0.1 copy.38
  174.2 5.6 %multiply_reduce_fusion = (f32[768]{0:T(1024)S(1)}, f32[1024]{0:T(1024)S(1)}, f32[1024,768]{1,0:T(8,128)S(1)}) fusion(f32[1024,768]{1,0:T(8,128)} %copy-done.18, f32[1024]{0:T(1024)S(1)} %get-tuple-element.103, f32[768]{0:T(1024)S(1)} %copy-done.25, bf16[1280,768]{1,0:T(8,128)(2,1)} %get-tuple-element.40, s32[1024]{0:T(1024)S(1)} %bitcast.45), kind=kOutput, calls=%fused_computation.4 | convolution fusion | flops 2019293440 | bytes 8275968 | tf_op jit(solution)/shard_map/dot_general | solution.py:1278
  179.8 0.0 copy-done.6
  179.8 0.0 copy-done.19
  179.9 0.0 copy-start.13
  179.9 1.0 subtract_add_fusion.ghid_h
  180.9 0.4 copy-done.13
  181.3 2.5 convolution_convert_fusion.1.dwo_h
  183.8 0.7 fusion.9.small_h
  184.4 2.6 convolution_convert_fusion.g_ref
  187.0 138.4 %attend_back.1 = (bf16[4,768,768]{2,1,0:T(8,128)(2,1)}, f32[1024,768]{1,0:T(8,128)}, f32[96,128]{1,0:T(8,128)}, bf16[2,192,3072]{2,1,0:T(8,128)(2,1)}, bf16[1024,768]{1,0:T(8,128)(2,1)}) custom-call(bf16[1024,768]{1,0:T(8,128)(2,1)} %copy-done.2, bf16[1024,768]{1,0:T(8,128)(2,1)} %copy-done.3, bf16[1024,768]{1,0:T(8,128)(2,1)} %copy-done.4, ...), custom_call_target="tpu_custom_call" | custom-call | flops 39460012032 | bytes 31457280 | tf_op jit(solution)/shard_map/attend_back/pallas_call | solution.py:1186
  325.4 1.3 slice_bitcast_fusion.5
  326.7 0.7 slice.38
  327.4 0.7 slice.41
  328.2 0.7 copy.40
  328.9 0.6 reshape.91
  329.5 4.5 %convert_bitcast_fusion = (f32[1,3072,192]{1,2,0:T(8,128)}, f32[1,192,3072]{2,1,0:T(8,128)}) fusion(bf16[2,192,3072]{2,1,0:T(8,128)(2,1)} %get-tuple-element.53), kind=kLoop, calls=%fused_computation.16 | loop fusion | flops 1179648 | bytes 7077888 | tf_op jit(solution)/shard_map/broadcast_in_dim | solution.py:1435
  334.0 0.0 copy-done.20
  334.0 0.8 convert_element_type.78
  334.8 3.8 %slice_bitcast_fusion = (f32[768,768]{1,0:T(8,128)}, f32[768,768]{1,0:T(8,128)}, f32[768,768]{1,0:T(8,128)}, f32[768,768]{1,0:T(8,128)}) fusion(f32[4,768,768]{2,1,0:T(8,128)S(1)} %convert_element_type.78), kind=kLoop, calls=%fused_computation.12 | loop fusion | bytes 18874368 | tf_op jit(solution)/shard_map/squeeze | solution.py:1434
  338.7 1.1 copy.44
  339.8 1.3 copy-done.21
  341.1 1.7 copy.45
  (30 shorter events, 0.1 us)
Async XLA Ops:
  0.6 74.7 %copy-start = (bf16[768,768]{1,0:T(8,128)(2,1)S(1)}, bf16[768,768]{1,0:T(8,128)(2,1)}, u32[]{:S(2)}) copy-start(bf16[768,768]{1,0:T(8,128)(2,1)} %param.19) | copy-start | bytes 3538948
  1.5 19.8 %copy-start.9 = (f32[1,768]{1,0:T(1,128)}, f32[1,768]{1,0:T(1,128)S(1)}, u32[]{:S(2)}) copy-start(f32[1,768]{1,0:T(1,128)S(1)} %broadcast_in_dim.11.gain) | copy-start | bytes 9220
  5.6 1.4 copy-start.5
  7.0 0.7 copy-start.7
  7.7 1.4 copy-start.10
  9.1 1.3 copy-start.14
  10.4 1.3 copy-start.15
  11.7 1.3 copy-start.16
  21.3 1.1 copy-start.4
  22.4 1.1 copy-start.17
  23.6 51.8 %copy-start.2 = (bf16[1024,768]{1,0:T(8,128)(2,1)}, bf16[1024,768]{1,0:T(8,128)(2,1)S(1)}, u32[]{:S(2)}) copy-start(bf16[1024,768]{1,0:T(8,128)(2,1)S(1)} %get-tuple-element.33.q_ref) | copy-start | bytes 4718596
  23.6 51.8 %copy-start.3 = (bf16[1024,768]{1,0:T(8,128)(2,1)}, bf16[1024,768]{1,0:T(8,128)(2,1)S(1)}, u32[]{:S(2)}) copy-start(bf16[1024,768]{1,0:T(8,128)(2,1)S(1)} %get-tuple-element.34.k_ref) | copy-start | bytes 4718596
  23.6 51.8 %copy-start.11 = (bf16[1024,768]{1,0:T(8,128)(2,1)S(1)}, bf16[1024,768]{1,0:T(8,128)(2,1)}, u32[]{:S(2)}) copy-start(bf16[1024,768]{1,0:T(8,128)(2,1)} %tok_h.1) | copy-start | bytes 4718596
  75.3 1.6 copy-start.12
  75.4 1.6 copy-start.24
  75.4 1.6 copy-start.25
  77.0 1.7 copy-start.18
  77.0 0.7 copy-start.8
  174.2 5.7 %copy-start.6 = (bf16[1024,768]{1,0:T(8,128)(2,1)S(1)}, bf16[1024,768]{1,0:T(8,128)(2,1)}, u32[]{:S(2)}) copy-start(bf16[1024,768]{1,0:T(8,128)(2,1)} %cot.1) | copy-start | bytes 4718596
  174.2 5.7 %copy-start.19 = (f32[1024,768]{1,0:T(8,128)S(1)}, f32[1024,768]{1,0:T(8,128)}, u32[]{:S(2)}) copy-start(f32[1024,768]{1,0:T(8,128)} %copy-done.18) | copy-start | bytes 9437188
  179.9 1.4 copy-start.13
  181.3 3.2 copy-start.22
  329.5 4.5 %copy-start.20 = (bf16[4,768,768]{2,1,0:T(8,128)(2,1)S(1)}, bf16[4,768,768]{2,1,0:T(8,128)(2,1)}, u32[]{:S(2)}) copy-start(bf16[4,768,768]{2,1,0:T(8,128)(2,1)} %get-tuple-element.51) | copy-start | bytes 14155780
  334.8 3.8 %copy-start.23 = (bf16[1024,768]{1,0:T(8,128)(2,1)S(1)}, bf16[1024,768]{1,0:T(8,128)(2,1)}, u32[]{:S(2)}) copy-start(bf16[1024,768]{1,0:T(8,128)(2,1)} %get-tuple-element.121) | copy-start | bytes 4718596
  338.7 2.5 copy-start.21
  338.7 4.1 %copy-start.1 = (bf16[768,768]{1,0:T(8,128)(2,1)S(1)}, bf16[768,768]{1,0:T(8,128)(2,1)}, u32[]{:S(2)}) copy-start(bf16[768,768]{1,0:T(8,128)(2,1)} %param.19) | copy-start | bytes 3538948

commit v7 on v6

--- a/solution.py
+++ b/solution.py
@@ -164,14 +164,14 @@
             dma((max(experts, 1),)), dma((max(experts, 1),)), dma(()),
         ],
         compiler_params=pltpu.CompilerParams(
-            vmem_limit_bytes=48 << 20, has_side_effects=experts > 0, collective_id=3 if experts else None
+            vmem_limit_bytes=62 << 20, has_side_effects=experts > 0, collective_id=3 if experts else None
         ),
         name="attend",
     )(q, k, v, u, gsend)
 
 
 def first_kernel(
-    capacity, experts, tok, gain, wq, wk, wv, route, cot, q_o, k_o, v_o, nl_o, gsend_o, slot_o, slot
+    capacity, experts, tok, gain, wq, wk, wv, route, cot, q_o, k_o, v_o, nl_o, gsend_o, slot_o, column_o, slot
 ):
     step = pl.program_id(0)
     slots = experts * capacity
@@ -190,6 +190,7 @@
         place = route[...].astype(f32) * capacity + position
         slot[...] = jnp.where(position < capacity, place, float(slots))
         slot_o[...] = slot[...]
+        column_o[...] = jnp.broadcast_to(slot[...], (128, seq)).T
 
     values = tok[...].astype(f32)
     scale = lax.rsqrt(jnp.mean(values * values, axis=-1, keepdims=True) + epsilon)
@@ -213,16 +214,128 @@
         functools.partial(first_kernel, capacity, experts),
         grid=(steps,),
         in_specs=[rows, fixed(gain.shape)] + [fixed(wq.shape)] * 3 + [fixed(route.shape), fixed(cotangent.shape)],
-        out_specs=[rows] * 4 + [pl.BlockSpec((slots // steps, width), lambda i: (i, 0)), fixed(route.shape)],
+        out_specs=[rows] * 4 + [pl.BlockSpec((slots // steps, width), lambda i: (i, 0)), fixed(route.shape), fixed((seq, 128))],
         out_shape=[jax.ShapeDtypeStruct((seq, width), bf16)] * 4
-        + [jax.ShapeDtypeStruct((slots, width), bf16), jax.ShapeDtypeStruct(route.shape, f32)],
+        + [jax.ShapeDtypeStruct((slots, width), bf16), jax.ShapeDtypeStruct(route.shape, f32),
+           jax.ShapeDtypeStruct((seq, 128), f32)],
         scratch_shapes=[pltpu.VMEM(route.shape, f32)],
-        compiler_params=pltpu.CompilerParams(vmem_limit_bytes=40 << 20),
+        compiler_params=pltpu.CompilerParams(vmem_limit_bytes=62 << 20),
         cost_estimate=pl.CostEstimate(
             flops=6 * seq * width * width + 2 * slots * seq * width, bytes_accessed=20 * seq * width, transcendentals=seq
         ),
         name="first",
     )(tokens, gain, wq, wk, wv, route, cotangent)
+
+
+def middle_kernel(experts, tok, ctx, wo, gain, rw, slot, column, hid_o, xs_o, meta_o, normed):
+    seq, width = tok.shape
+    span = 256
+
+    def token_block(idx, carry):
+        rows = pl.ds(pl.multiple_of(idx * span, span), span)
+        hidden = tok[rows, :].astype(f32) + dot_f32(ctx[rows, :], wo[...])
+        hid_o[rows, :] = hidden
+        scale = lax.rsqrt(jnp.mean(hidden * hidden, axis=-1, keepdims=True) + epsilon)
+        low = (hidden * scale * gain[...]).astype(bf16)
+        normed[rows, :] = low
+        lane = lax.broadcasted_iota(jnp.int32, (span, 128), 1)
+        logits = jnp.where(lane < experts, dot_f32(low, rw[...]), -1e30)
+        weights = jnp.exp(logits - jnp.max(logits, axis=-1, keepdims=True))
+        place = column[rows, :]
+        each = xs_o.shape[0] // experts
+        first = lane.astype(f32) * each
+        chosen = (place >= first) & (place < first + each) & (lane < experts)
+        gate = jnp.sum(jnp.where(chosen, weights, 0.0), axis=-1, keepdims=True) / jnp.sum(
+            weights, axis=-1, keepdims=True
+        )
+        meta_o[rows, :] = jnp.where(lane == 0, gate, place)
+        return carry
+
+    lax.fori_loop(0, seq // span, token_block, 0)
+
+    def slot_block(idx, carry):
+        rows = pl.ds(pl.multiple_of(idx * span, span), span)
+        number = lax.broadcasted_iota(jnp.int32, (span, seq), 0) + idx * span
+        pick = jnp.where(number.astype(f32) == slot[...], 1.0, 0.0).astype(bf16)
+        xs_o[rows, :] = dot_f32(pick, normed[...]).astype(bf16)
+        return carry
+
+    lax.fori_loop(0, xs_o.shape[0] // span, slot_block, 0)
+
+
+def middle_pass(tokens, ctx, wo, gain, rw, slot, column, slots, experts):
+    seq, width = tokens.shape
+    vmem = pl.BlockSpec(memory_space=pltpu.VMEM)
+    return pl.pallas_call(
+        functools.partial(middle_kernel, experts),
+        in_specs=[vmem] * 7,
+        out_specs=[vmem] * 3,
+        out_shape=[
+            jax.ShapeDtypeStruct((seq, width), f32),
+            jax.ShapeDtypeStruct((slots, width), bf16),
+            jax.ShapeDtypeStruct((seq, 128), f32),
+        ],
+        scratch_shapes=[pltpu.VMEM((seq, width), bf16)],
+        compiler_params=pltpu.CompilerParams(vmem_limit_bytes=62 << 20),
+        cost_estimate=pl.CostEstimate(
+            flops=2 * seq * width * width + 2 * slots * seq * width, bytes_accessed=10 * seq * width, transcendentals=seq
+        ),
+        name="middle",
+    )(tokens, ctx, wo, gain, rw, slot, column)
+
+
+def combine_kernel(gback, hid, cot, gain, ctx, wo, meta, ghid_o, dwo_o, gctx_o, gain_o, low):
+    seq, width = hid.shape
+    slots = gback.shape[0]
+    span = 256
+
+    def token_block(idx, carry):
+        rows = pl.ds(pl.multiple_of(idx * span, span), span)
+        where = lax.broadcasted_iota(jnp.int32, (span, slots), 1).astype(f32)
+        pick = jnp.where(meta[rows, 1:2] == where, 1.0, 0.0).astype(bf16)
+        grad = dot_f32(pick, gback[...])
+        values = hid[rows, :]
+        scale = lax.rsqrt(jnp.mean(values * values, axis=-1, keepdims=True) + epsilon)
+        weighted = grad * gain[...]
+        inner = jnp.mean(weighted * values, axis=-1, keepdims=True)
+        total = cot[rows, :].astype(f32) + scale * weighted - values * (scale * scale * scale * inner)
+        ghid_o[rows, :] = total
+        branch = total.astype(bf16)
+        low[rows, :] = branch
+        gctx_o[rows, :] = dot_nt(branch, wo[...]).astype(bf16)
+        return carry + jnp.sum(grad * values * scale, axis=0, keepdims=True)
+
+    gain_o[...] = lax.fori_loop(0, seq // span, token_block, jnp.zeros((1, width), f32))
+
+    def weight_block(idx, carry):
+        cols = pl.ds(pl.multiple_of(idx * span, span), span)
+        dwo_o[cols, :] = dot_f32(ctx[:, cols].T, low[...]).astype(bf16)
+        return carry
+
+    lax.fori_loop(0, width // span, weight_block, 0)
+
+
+def combine_pass(gback, hidden, cotangent, gain, ctx, wo, meta):
+    seq, width = hidden.shape
+    vmem = pl.BlockSpec(memory_space=pltpu.VMEM)
+    return pl.pallas_call(
+        combine_kernel,
+        in_specs=[vmem] * 7,
+        out_specs=[vmem] * 4,
+        out_shape=[
+            jax.ShapeDtypeStruct((seq, width), f32),
+            jax.ShapeDtypeStruct((width, width), bf16),
+            jax.ShapeDtypeStruct((seq, width), bf16),
+            jax.ShapeDtypeStruct((1, width), f32),
+        ],
+        scratch_shapes=[pltpu.VMEM((seq, width), bf16)],
+        compiler_params=pltpu.CompilerParams(vmem_limit_bytes=62 << 20),
+        cost_estimate=pl.CostEstimate(
+            flops=4 * seq * width * width + 2 * gback.shape[0] * seq * width,
+            bytes_accessed=16 * seq * width, transcendentals=seq,
+        ),
+        name="combine",
+    )(gback, hidden, cotangent, gain, ctx, wo, meta)
 
 
 def split_rows(row):
@@ -1348,11 +1461,9 @@
 
     tokens_f = tokens.astype(f32)
     if kernels:
-        queries, key_rows, value_rows, normed_low, grad_send, slot_row = first_pass(
+        queries, key_rows, value_rows, normed_low, grad_send, slot_row, slot_column = first_pass(
             tokens, gain_one[None], query_w, key_w, value_w, routes.reshape(1, seq_len), cotangent, capacity, experts
         )
-        slot_index = slot_row[0].astype(jnp.int32)
-        pick = (jnp.arange(slots, dtype=jnp.int32)[:, None] == slot_index[None, :]).astype(bf16)
     else:
         grad_send = scatter_rows(cotangent)
         normed_low = rms_forward(tokens_f, gain_one)[0].astype(bf16)
@@ -1366,34 +1477,35 @@
     context, context_t, logsum, weights, grad_recv = attend(
         queries, key_rows, value_rows, spread, grad_send, experts if kernels else 0
     )
-    if not kernels:
-        grad_recv = exchange(grad_send, experts)
-    hidden = tokens_f + contract(context, out_w, (1, 0))
-    normed_two, scale_two = rms_forward(hidden, gain_two)
-    normed_two_low = normed_two.astype(bf16)
-
-    send = scatter_rows(normed_two_low)
     if kernels:
         router_pad = jnp.pad(router_w, ((0, 0), (0, 128 - experts)))
+        hidden, send, meta = middle_pass(
+            tokens, context, out_w, gain_two[None], router_pad, slot_row, slot_column, slots, experts
+        )
         grad_rows, produced, in_grad, out_grad_t, router_grad, shared = expert_pass(
             send, grad_recv, weight_in, weight_out, router_pad, experts, capacity
         )
         router_grad = router_grad[:, :experts]
+        grad_hidden, out_w_grad, grad_context, gain_two_grad = combine_pass(
+            grad_rows, hidden, cotangent, gain_two[None], context, out_w, meta
+        )
     else:
+        grad_recv = exchange(grad_send, experts)
+        hidden = tokens_f + contract(context, out_w, (1, 0))
+        normed_two, scale_two = rms_forward(hidden, gain_two)
+        normed_two_low = normed_two.astype(bf16)
         grad_rows, produced, in_grad, out_grad_t, router_grad = expert_native(
-            send, grad_recv, weight_in, weight_out, router_w, experts
-        )
-
-    router_probs = jax.nn.softmax(contract(normed_two_low, router_w, (1, 0)), axis=-1)
-    gate_value = jnp.sum(router_probs * route_float, axis=-1, keepdims=True)
-
-    grad_out = cotangent.astype(f32)
-    grad_normed_two = gather_rows(grad_rows)
-    grad_hidden_norm, gain_two_grad = rms_backward(grad_normed_two, hidden, scale_two, gain_two)
-    grad_hidden = grad_out + grad_hidden_norm
-    branch_low = grad_hidden.astype(bf16)
-    out_w_grad = contract(context, branch_low, (0, 0)).astype(bf16)
-    grad_context = contract(branch_low, out_w, (1, 1)).astype(bf16)
+            scatter_rows(normed_two_low), grad_recv, weight_in, weight_out, router_w, experts
+        )
+        router_probs = jax.nn.softmax(contract(normed_two_low, router_w, (1, 0)), axis=-1)
+        gate_value = jnp.sum(router_probs * route_float, axis=-1, keepdims=True)
+        grad_normed_two = gather_rows(grad_rows)
+        grad_hidden_norm, gain_two_grad = rms_backward(grad_normed_two, hidden, scale_two, gain_two)
+        grad_hidden = cotangent.astype(f32) + grad_hidden_norm
+        branch_low = grad_hidden.astype(bf16)
+        out_w_grad = contract(context, branch_low, (0, 0)).astype(bf16)
+        grad_context = contract(branch_low, out_w, (1, 1)).astype(bf16)
+
     if kernels:
         small = jnp.concatenate(
             [
@@ -1406,7 +1518,7 @@
             queries, key_rows, value_rows, grad_context, context_t, query_w, key_w, value_w,
             bucket_hot, gain_one[None], normed_low, tokens, grad_hidden, out_w_grad, small,
             out_grad_t, shared, in_grad, weights, produced, hidden,
-            jnp.concatenate([gate_value, slot_index[:, None].astype(f32)], axis=1), groups, experts,
+            meta, groups, experts,
         )
         tiles = width // 128
         first = 8 + rel_table.shape[0]

time: 344 us -> 342 us (level)
  Pallas kernels: 286 us -> 314 us
  matrix products: 19.5 us -> 0.21 us
  local copies, waits for them, and re-layouts: 27.7 us -> 18.1 us
    pallas_call x0 -> x2, Pallas kernels: none -> 25.8 us  [the longest x1 14.2 us: combine_pass(): pl.pallas_call(combine_kernel, in_specs=[vmem] * 7, out_specs=[vmem] * 4,...]
    dot_general x6 -> x0, matrix products: 18.6 us -> none  [contract(): lax.dot_general(left, right, (((dims[0],), (dims[1],)), ((), ())), prefer...]
    unnamed x56 -> x14, local copies, waits for them, and re-layouts: 16.7 us -> 5.69 us
where the time goes in v7:
time: 342 us; the launch traced here: 341 us
  Pallas kernels  314 us (92%)
  local copies, waits for them, and re-layouts  18.1 us (5%)
  other arithmetic  8.23 us (2%)
    pallas_call x1, Pallas kernels, back_pass(): pl.pallas_call(functools.partial(back_kernel, groups, experts, pairs), gr...  138 us
    pallas_call x1, Pallas kernels, expert_pass(): pl.pallas_call(functools.partial(expert_kernel, experts, capacity, tile),...  88.6 us
    pallas_call x1, Pallas kernels, attend(): pl.pallas_call(functools.partial(attend_kernel, experts), grid=(pairs,),...  50.6 us
    pallas_call x1, Pallas kernels, combine_pass(): pl.pallas_call(combine_kernel, in_specs=[vmem] * 7, out_specs=[vmem] * 4,...  14.2 us
    pallas_call x1, Pallas kernels, middle_pass(): pl.pallas_call(functools.partial(middle_kernel, experts), in_specs=[vmem]...  11.7 us
    pallas_call x1, Pallas kernels, first_pass(): pl.pallas_call(functools.partial(first_kernel, capacity, experts), grid=(...  11 us

profile of v7, /device:TPU:1, one launch (start us, length us, event | category | flops | bytes accessed | tf_op | source)
XLA Modules:
  0.0 341.2 jit_solution(8175983525906629333)
XLA Ops:
  0.6 0.0 copy-start
  0.7 1.3 broadcast_in_dim.20.gain
  2.0 1.3 broadcast_in_dim.21.gain
  3.2 0.8 pad_add_fusion
  4.0 0.1 rev.3
  4.1 0.0 copy-done
  4.1 0.2 convolution_bitcast_fusion
  4.3 0.7 reshape.49.u_ref
  5.0 0.9 copy.26
  5.9 0.7 pad.8.rw
  6.6 0.7 fusion.hot
  7.3 11.0 %first.1 = (bf16[1024,768]{1,0:T(8,128)(2,1)}, bf16[1024,768]{1,0:T(8,128)(2,1)}, bf16[1024,768]{1,0:T(8,128)(2,1)}, bf16[1024,768]{1,0:T(8,128)(2,1)}, bf16[128...) custom-call(bf16[1024,768]{1,0:T(8,128)(2,1)} %tok_h.1, f32[1,768]{1,0:T(1,128)} %broadcast_in_dim.20.gain, ...), custom_call_target="tpu_custom_call" | custom-call | flops 5637144576 | bytes 15728640 | tf_op jit(solution)/shard_map/first/pallas_call | solution.py:213
  18.3 50.6 %attend.1 = (bf16[1024,768]{1,0:T(8,128)(2,1)}, f32[768,1024]{1,0:T(8,128)}, f32[6,8,1024]{2,1,0:T(8,128)}, bf16[12,1024,1024]{2,1,0:T(8,128)(2,1)}, bf16[1280,768]{1,0:T(8,128)(2,1)}) custom-call(bf16[1024,768]{1,0:T(8,128)(2,1)} %get-tuple-element.41.q_ref, bf16[1024,768]{1,0:T(8,128)(2,1)} %get-tuple-element.42.k_ref, ...), custom_call_target="tpu_custom_call" | custom-call | tf_op jit(solution)/shard_map/attend/pallas_call | solution.py:137
  68.9 11.7 %middle.1 = (f32[1024,768]{1,0:T(8,128)}, bf16[1280,768]{1,0:T(8,128)(2,1)}, f32[1024,128]{1,0:T(8,128)}) custom-call(bf16[1024,768]{1,0:T(8,128)(2,1)} %tok_h.1, bf16[1024,768]{1,0:T(8,128)(2,1)} %get-tuple-element.45.ctx, bf16[768,768]{1,0:T(8,128)(2,1)} %wo.3, f32[1,768]{1,0:T(1,128)} %broadcast_in_dim.21.gain, bf16[768,128]{1,0:T(8,128)(2,1)} %pad.8.rw, ...), custom_call_target="tpu_custom_call" | custom-call | flops 3221225472 | bytes 7864320 | tf_op jit(solution)/shard_map/middle/pallas_call | solution.py:269
  80.6 88.6 %experts.1 = (bf16[1280,768]{1,0:T(8,128)(2,1)}, bf16[1280,768]{1,0:T(8,128)(2,1)}, bf16[768,3072]{1,0:T(8,128)(2,1)}, bf16[768,3072]{1,0:T(8,128)(2,1)}, f32[768,128]{1,0:T(8,128)}, /*index=5*/bf16[768,1536]{1,0:T(8,128)(2,1)}) custom-call(bf16[1280,768]{1,0:T(8,128)(2,1)} %get-tuple-element.48.xs, bf16[1280,768]{1,0:T(8,128)(2,1)} %get-tuple-element.49.gr_h, ...), custom_call_target="tpu_custom_call" | custom-call | flops 36238786560 | bytes 18874368 | tf_op jit(solution)/shard_map/experts/pallas_call | solution.py:693
  169.2 1.0 slice_bitcast_fusion.4
  170.2 0.1 copy.27
  170.4 14.2 %combine.1 = (f32[1024,768]{1,0:T(8,128)}, bf16[768,768]{1,0:T(8,128)(2,1)}, bf16[1024,768]{1,0:T(8,128)(2,1)}, f32[1,768]{1,0:T(1,128)}) custom-call(bf16[1280,768]{1,0:T(8,128)(2,1)} %get-tuple-element.50.gback, f32[1024,768]{1,0:T(8,128)} %get-tuple-element.51.hid.hid_h, bf16[1024,768]{1,0:T(8,128)(2,1)} %cot.3, f32[1,768]{1,0:T(1,128)} %broadcast_in_dim.21.gain, ...), custom_call_target="tpu_custom_call" | custom-call | flops 4429185024 | bytes 12582912 | tf_op jit(solution)/shard_map/combine/pallas_call | solution.py:321
  184.5 0.7 reduce
  185.2 0.7 fusion.2.small_h
  185.9 137.9 %attend_back.1 = (bf16[4,768,768]{2,1,0:T(8,128)(2,1)}, f32[1024,768]{1,0:T(8,128)}, f32[96,128]{1,0:T(8,128)}, bf16[2,192,3072]{2,1,0:T(8,128)(2,1)}, bf16[1024,768]{1,0:T(8,128)(2,1)}) custom-call(bf16[1024,768]{1,0:T(8,128)(2,1)} %get-tuple-element.41.q_ref, bf16[1024,768]{1,0:T(8,128)(2,1)} %get-tuple-element.42.k_ref, ...), custom_call_target="tpu_custom_call" | custom-call | flops 39460012032 | bytes 31457280 | tf_op jit(solution)/shard_map/attend_back/pallas_call | solution.py:1299
  323.9 1.3 slice_bitcast_fusion.5
  325.1 0.7 slice.38
  325.9 0.7 slice.41
  326.6 0.7 copy.28
  327.3 0.6 reshape.54
  327.9 0.0 copy-start.2
  327.9 4.5 %convert_bitcast_fusion = (f32[1,3072,192]{1,2,0:T(8,128)}, f32[1,192,3072]{2,1,0:T(8,128)}) fusion(bf16[2,192,3072]{2,1,0:T(8,128)(2,1)} %get-tuple-element.69), kind=kLoop, calls=%fused_computation.4 | loop fusion | flops 1179648 | bytes 7077888 | tf_op jit(solution)/shard_map/broadcast_in_dim | solution.py:1547
  332.4 0.0 copy-done.2
  332.4 0.8 convert_element_type.19
  333.2 0.0 copy-start.4
  333.3 3.8 %slice_bitcast_fusion = (f32[768,768]{1,0:T(8,128)}, f32[768,768]{1,0:T(8,128)}, f32[768,768]{1,0:T(8,128)}, f32[768,768]{1,0:T(8,128)}) fusion(f32[4,768,768]{2,1,0:T(8,128)S(1)} %convert_element_type.19), kind=kLoop, calls=%fused_computation | loop fusion | bytes 18874368 | tf_op jit(solution)/shard_map/squeeze | solution.py:1546
  337.1 0.0 copy-start.3
  337.1 0.0 copy-done.4
  337.1 0.0 copy-start.1
  337.1 1.1 copy.31
  338.2 1.3 copy-done.3
  339.5 1.7 copy.32
  341.2 0.0 copy-done.1
  (3 shorter events, 0.0 us)
Async XLA Ops:
  0.6 3.4 %copy-start = (f32[32,12]{0,1:T(8,128)S(1)}, f32[32,12]{0,1:T(8,128)}, u32[]{:S(2)}) copy-start(f32[32,12]{0,1:T(8,128)} %param.20) | copy-start | bytes 4612
  327.9 4.5 %copy-start.2 = (bf16[4,768,768]{2,1,0:T(8,128)(2,1)S(1)}, bf16[4,768,768]{2,1,0:T(8,128)(2,1)}, u32[]{:S(2)}) copy-start(bf16[4,768,768]{2,1,0:T(8,128)(2,1)} %get-tuple-element.67) | copy-start | bytes 14155780
  333.2 3.8 %copy-start.4 = (bf16[1024,768]{1,0:T(8,128)(2,1)S(1)}, bf16[1024,768]{1,0:T(8,128)(2,1)}, u32[]{:S(2)}) copy-start(bf16[1024,768]{1,0:T(8,128)(2,1)} %get-tuple-element.102) | copy-start | bytes 4718596
  337.1 2.5 copy-start.3
  337.1 4.1 %copy-start.1 = (f32[32,12]{0,1:T(8,128)S(1)}, f32[32,12]{0,1:T(8,128)}, u32[]{:S(2)}) copy-start(f32[32,12]{0,1:T(8,128)} %param.20) | copy-start | bytes 4612

commit v8 on v7

--- a/solution.py
+++ b/solution.py
@@ -107,14 +107,14 @@
         both = jnp.concatenate(outs, axis=0)
         ctxt_ref[:, cols] = both
         ctx_ref[cols, :] = both.T.astype(bf16)
-        if experts:
-            @pl.when((pair == 0) & (idx == 0))
-            def _():
-                pl.semaphore_wait(barrier, experts - 1)
-                for peer in peers:
-                    give(peer, me).start()
-
         return carry
+
+    if experts:
+        @pl.when(pair == 0)
+        def _():
+            pl.semaphore_wait(barrier, experts - 1)
+            for peer in peers:
+                give(peer, me).start()
 
     lax.fori_loop(0, seq // span, step, 0)
 
@@ -194,7 +194,7 @@
 
     values = tok[...].astype(f32)
     scale = lax.rsqrt(jnp.mean(values * values, axis=-1, keepdims=True) + epsilon)
-    normed = (values * scale * gain[...]).astype(bf16)
+    normed = (values * scale * gain[0:1, :]).astype(bf16)
     nl_o[...] = normed
     for weight, out in ((wq, q_o), (wk, k_o), (wv, v_o)):
         out[...] = dot_f32(normed, weight[...]).astype(bf16)
@@ -227,49 +227,57 @@
     )(tokens, gain, wq, wk, wv, route, cotangent)
 
 
-def middle_kernel(experts, tok, ctx, wo, gain, rw, slot, column, hid_o, xs_o, meta_o, normed):
-    seq, width = tok.shape
-    span = 256
-
-    def token_block(idx, carry):
-        rows = pl.ds(pl.multiple_of(idx * span, span), span)
-        hidden = tok[rows, :].astype(f32) + dot_f32(ctx[rows, :], wo[...])
-        hid_o[rows, :] = hidden
+def middle_kernel(experts, steps, tok, ctx, wo, gain, rw, slot, column, hid_o, xs_o, meta_o, normed):
+    step = pl.program_id(0)
+    span, width = tok.shape
+    seq = normed.shape[0]
+
+    @pl.when(step < steps)
+    def _():
+        hidden = tok[...].astype(f32) + dot_f32(ctx[...], wo[...])
+        hid_o[...] = hidden
         scale = lax.rsqrt(jnp.mean(hidden * hidden, axis=-1, keepdims=True) + epsilon)
-        low = (hidden * scale * gain[...]).astype(bf16)
-        normed[rows, :] = low
+        low = (hidden * scale * gain[1:2, :]).astype(bf16)
+        normed[pl.ds(pl.multiple_of(step * span, span), span), :] = low
         lane = lax.broadcasted_iota(jnp.int32, (span, 128), 1)
         logits = jnp.where(lane < experts, dot_f32(low, rw[...]), -1e30)
         weights = jnp.exp(logits - jnp.max(logits, axis=-1, keepdims=True))
-        place = column[rows, :]
-        each = xs_o.shape[0] // experts
-        first = lane.astype(f32) * each
+        place = column[...]
+        each = xs_o.shape[0] * (pl.num_programs(0) - steps) // experts
+        first = (lane * each).astype(f32)
         chosen = (place >= first) & (place < first + each) & (lane < experts)
         gate = jnp.sum(jnp.where(chosen, weights, 0.0), axis=-1, keepdims=True) / jnp.sum(
             weights, axis=-1, keepdims=True
         )
-        meta_o[rows, :] = jnp.where(lane == 0, gate, place)
-        return carry
-
-    lax.fori_loop(0, seq // span, token_block, 0)
-
-    def slot_block(idx, carry):
-        rows = pl.ds(pl.multiple_of(idx * span, span), span)
-        number = lax.broadcasted_iota(jnp.int32, (span, seq), 0) + idx * span
+        meta_o[...] = jnp.where(lane == 0, gate, place)
+
+    @pl.when(step >= steps)
+    def _():
+        rows = xs_o.shape[0]
+        number = lax.broadcasted_iota(jnp.int32, (rows, seq), 0) + (step - steps) * rows
         pick = jnp.where(number.astype(f32) == slot[...], 1.0, 0.0).astype(bf16)
-        xs_o[rows, :] = dot_f32(pick, normed[...]).astype(bf16)
-        return carry
-
-    lax.fori_loop(0, xs_o.shape[0] // span, slot_block, 0)
+        xs_o[...] = dot_f32(pick, normed[...]).astype(bf16)
 
 
 def middle_pass(tokens, ctx, wo, gain, rw, slot, column, slots, experts):
     seq, width = tokens.shape
-    vmem = pl.BlockSpec(memory_space=pltpu.VMEM)
+    steps = 4
+    span = seq // steps
+    each = slots // steps
+    token_map = lambda i: (jnp.minimum(i, steps - 1), 0)
+    fixed = lambda shape: pl.BlockSpec(shape, lambda i: (0, 0))
     return pl.pallas_call(
-        functools.partial(middle_kernel, experts),
-        in_specs=[vmem] * 7,
-        out_specs=[vmem] * 3,
+        functools.partial(middle_kernel, experts, steps),
+        grid=(2 * steps,),
+        in_specs=[
+            pl.BlockSpec((span, width), token_map), pl.BlockSpec((span, width), token_map), fixed(wo.shape),
+            fixed(gain.shape), fixed(rw.shape), fixed(slot.shape), pl.BlockSpec((span, 128), token_map),
+        ],
+        out_specs=[
+            pl.BlockSpec((span, width), token_map),
+            pl.BlockSpec((each, width), lambda i: (jnp.maximum(i - steps, 0), 0)),
+            pl.BlockSpec((span, 128), token_map),
+        ],
         out_shape=[
             jax.ShapeDtypeStruct((seq, width), f32),
             jax.ShapeDtypeStruct((slots, width), bf16),
@@ -284,51 +292,59 @@
     )(tokens, ctx, wo, gain, rw, slot, column)
 
 
-def combine_kernel(gback, hid, cot, gain, ctx, wo, meta, ghid_o, dwo_o, gctx_o, gain_o, low):
-    seq, width = hid.shape
+def combine_kernel(gback, hid, cot, gain, ctx, wo, meta, ghid_o, dwo_o, gctx_o, gain_o, total_w):
+    step = pl.program_id(0)
+    span = hid.shape[0]
     slots = gback.shape[0]
-    span = 256
-
-    def token_block(idx, carry):
-        rows = pl.ds(pl.multiple_of(idx * span, span), span)
-        where = lax.broadcasted_iota(jnp.int32, (span, slots), 1).astype(f32)
-        pick = jnp.where(meta[rows, 1:2] == where, 1.0, 0.0).astype(bf16)
-        grad = dot_f32(pick, gback[...])
-        values = hid[rows, :]
-        scale = lax.rsqrt(jnp.mean(values * values, axis=-1, keepdims=True) + epsilon)
-        weighted = grad * gain[...]
-        inner = jnp.mean(weighted * values, axis=-1, keepdims=True)
-        total = cot[rows, :].astype(f32) + scale * weighted - values * (scale * scale * scale * inner)
-        ghid_o[rows, :] = total
-        branch = total.astype(bf16)
-        low[rows, :] = branch
-        gctx_o[rows, :] = dot_nt(branch, wo[...]).astype(bf16)
-        return carry + jnp.sum(grad * values * scale, axis=0, keepdims=True)
-
-    gain_o[...] = lax.fori_loop(0, seq // span, token_block, jnp.zeros((1, width), f32))
-
-    def weight_block(idx, carry):
-        cols = pl.ds(pl.multiple_of(idx * span, span), span)
-        dwo_o[cols, :] = dot_f32(ctx[:, cols].T, low[...]).astype(bf16)
-        return carry
-
-    lax.fori_loop(0, width // span, weight_block, 0)
+    where = lax.broadcasted_iota(jnp.int32, (span, slots), 1).astype(f32)
+    pick = jnp.where(meta[:, 1:2] == where, 1.0, 0.0).astype(bf16)
+    grad = dot_f32(pick, gback[...])
+    values = hid[...]
+    scale = lax.rsqrt(jnp.mean(values * values, axis=-1, keepdims=True) + epsilon)
+    weighted = grad * gain[1:2, :]
+    inner = jnp.mean(weighted * values, axis=-1, keepdims=True)
+    total = cot[...].astype(f32) + scale * weighted - values * (scale * scale * scale * inner)
+    ghid_o[...] = total
+    branch = total.astype(bf16)
+    gctx_o[...] = dot_nt(branch, wo[...]).astype(bf16)
+    gains = jnp.sum(grad * values * scale, axis=0, keepdims=True)
+    now = dot_f32(ctx[...].T, branch)
+
+    @pl.when(step == 0)
+    def _():
+        total_w[...] = now
+        gain_o[...] = gains
+
+    @pl.when(step > 0)
+    def _():
+        total_w[...] += now
+        gain_o[...] += gains
+
+    @pl.when(step == pl.num_programs(0) - 1)
+    def _():
+        dwo_o[...] = total_w[...].astype(bf16)
 
 
 def combine_pass(gback, hidden, cotangent, gain, ctx, wo, meta):
     seq, width = hidden.shape
-    vmem = pl.BlockSpec(memory_space=pltpu.VMEM)
+    steps = 4
+    rows = pl.BlockSpec((seq // steps, width), lambda i: (i, 0))
+    fixed = lambda shape: pl.BlockSpec(shape, lambda i: (0, 0))
     return pl.pallas_call(
         combine_kernel,
-        in_specs=[vmem] * 7,
-        out_specs=[vmem] * 4,
+        grid=(steps,),
+        in_specs=[
+            fixed(gback.shape), rows, rows, fixed(gain.shape), rows, fixed(wo.shape),
+            pl.BlockSpec((seq // steps, 128), lambda i: (i, 0)),
+        ],
+        out_specs=[rows, fixed((width, width)), rows, fixed((1, width))],
         out_shape=[
             jax.ShapeDtypeStruct((seq, width), f32),
             jax.ShapeDtypeStruct((width, width), bf16),
             jax.ShapeDtypeStruct((seq, width), bf16),
             jax.ShapeDtypeStruct((1, width), f32),
         ],
-        scratch_shapes=[pltpu.VMEM((seq, width), bf16)],
+        scratch_shapes=[pltpu.VMEM((width, width), f32)],
         compiler_params=pltpu.CompilerParams(vmem_limit_bytes=62 << 20),
         cost_estimate=pl.CostEstimate(
             flops=4 * seq * width * width + 2 * gback.shape[0] * seq * width,
@@ -1203,7 +1219,7 @@
             )
             values = tok[rows, :].astype(f32)
             scale = lax.rsqrt(jnp.mean(values * values, axis=-1, keepdims=True) + epsilon)
-            weighted = grad * gain[...]
+            weighted = grad * gain[0:1, :]
             inner = jnp.mean(weighted * values, axis=-1, keepdims=True)
             ing_o[rows, :] += scale * weighted - values * (scale * scale * scale * inner)
             return carry + jnp.sum(grad * values * scale, axis=0, keepdims=True)
@@ -1460,9 +1476,10 @@
         return contract(pick, rows, (0, 0))
 
     tokens_f = tokens.astype(f32)
+    gains = jnp.stack([gain_one, gain_two])
     if kernels:
         queries, key_rows, value_rows, normed_low, grad_send, slot_row, slot_column = first_pass(
-            tokens, gain_one[None], query_w, key_w, value_w, routes.reshape(1, seq_len), cotangent, capacity, experts
+            tokens, gains, query_w, key_w, value_w, routes.reshape(1, seq_len), cotangent, capacity, experts
         )
     else:
         grad_send = scatter_rows(cotangent)
@@ -1480,14 +1497,14 @@
     if kernels:
         router_pad = jnp.pad(router_w, ((0, 0), (0, 128 - experts)))
         hidden, send, meta = middle_pass(
-            tokens, context, out_w, gain_two[None], router_pad, slot_row, slot_column, slots, experts
+            tokens, context, out_w, gains, router_pad, slot_row, slot_column, slots, experts
         )
         grad_rows, produced, in_grad, out_grad_t, router_grad, shared = expert_pass(
             send, grad_recv, weight_in, weight_out, router_pad, experts, capacity
         )
         router_grad = router_grad[:, :experts]
         grad_hidden, out_w_grad, grad_context, gain_two_grad = combine_pass(
-            grad_rows, hidden, cotangent, gain_two[None], context, out_w, meta
+            grad_rows, hidden, cotangent, gains, context, out_w, meta
         )
     else:
         grad_recv = exchange(grad_send, experts)
@@ -1516,7 +1533,7 @@
         )
         grads, input_grad, small, shares, output = back_pass(
             queries, key_rows, value_rows, grad_context, context_t, query_w, key_w, value_w,
-            bucket_hot, gain_one[None], normed_low, tokens, grad_hidden, out_w_grad, small,
+            bucket_hot, gains, normed_low, tokens, grad_hidden, out_w_grad, small,
             out_grad_t, shared, in_grad, weights, produced, hidden,
             meta, groups, experts,
         )

time: 342 us -> 340 us (level)
  no operation moved by 1% of the time
where the time goes in v8:
time: 340 us
  Pallas kernels  313 us (92%)
  local copies, waits for them, and re-layouts  16.9 us (5%)
  other arithmetic  8.84 us (3%)
    pallas_call x1, Pallas kernels, back_pass(): pl.pallas_call(functools.partial(back_kernel, groups, experts, pairs), gr...  139 us
    pallas_call x1, Pallas kernels, expert_pass(): pl.pallas_call(functools.partial(expert_kernel, experts, capacity, tile),...  87.2 us
    pallas_call x1, Pallas kernels, attend(): pl.pallas_call(functools.partial(attend_kernel, experts), grid=(pairs,),...  52 us
    pallas_call x1, Pallas kernels, combine_pass(): pl.pallas_call(combine_kernel, grid=(steps,), in_specs=[fixed(gback.shape...  13 us
    pallas_call x1, Pallas kernels, first_pass(): pl.pallas_call(functools.partial(first_kernel, capacity, experts), grid=(...  11 us
    pallas_call x1, Pallas kernels, middle_pass(): pl.pallas_call(functools.partial(middle_kernel, experts, steps), grid=(2...  10.8 us

profile of v8, /device:TPU:1, one launch (start us, length us, event | category | flops | bytes accessed | tf_op | source)
XLA Modules:
  0.0 339.6 jit_solution(4402216553694228093)
XLA Ops:
  0.6 0.0 copy-start
  0.7 0.7 stack.9
  1.4 0.7 stack.10
  2.1 0.6 pad_maximum_fusion.gain
  2.7 0.8 pad_add_fusion
  3.4 0.1 rev.3
  3.5 0.0 copy-done
  3.5 0.2 convolution_bitcast_fusion
  3.7 0.7 reshape.49.u_ref
  4.4 0.9 copy.26
  5.3 0.7 pad.8.rw
  6.0 0.7 fusion.hot
  6.8 11.0 %first.1 = (bf16[1024,768]{1,0:T(8,128)(2,1)}, bf16[1024,768]{1,0:T(8,128)(2,1)}, bf16[1024,768]{1,0:T(8,128)(2,1)}, bf16[1024,768]{1,0:T(8,128)(2,1)}, bf16[128...) custom-call(bf16[1024,768]{1,0:T(8,128)(2,1)} %tok_h.1, f32[2,768]{1,0:T(2,128)} %pad_maximum_fusion.gain, ...), custom_call_target="tpu_custom_call" | custom-call | flops 5637144576 | bytes 15728640 | tf_op jit(solution)/shard_map/first/pallas_call | solution.py:213
  17.8 52.0 %attend.1 = (bf16[1024,768]{1,0:T(8,128)(2,1)}, f32[768,1024]{1,0:T(8,128)}, f32[6,8,1024]{2,1,0:T(8,128)}, bf16[12,1024,1024]{2,1,0:T(8,128)(2,1)}, bf16[1280,768]{1,0:T(8,128)(2,1)}) custom-call(bf16[1024,768]{1,0:T(8,128)(2,1)} %get-tuple-element.41.q_ref, bf16[1024,768]{1,0:T(8,128)(2,1)} %get-tuple-element.42.k_ref, ...), custom_call_target="tpu_custom_call" | custom-call | tf_op jit(solution)/shard_map/attend/pallas_call | solution.py:137
  69.8 10.8 %middle.1 = (f32[1024,768]{1,0:T(8,128)}, bf16[1280,768]{1,0:T(8,128)(2,1)}, f32[1024,128]{1,0:T(8,128)}) custom-call(bf16[1024,768]{1,0:T(8,128)(2,1)} %tok_h.1, bf16[1024,768]{1,0:T(8,128)(2,1)} %get-tuple-element.45.ctx, bf16[768,768]{1,0:T(8,128)(2,1)} %wo.3, f32[2,768]{1,0:T(2,128)} %pad_maximum_fusion.gain, bf16[768,128]{1,0:T(8,128)(2,1)} %pad.8.rw, ...), custom_call_target="tpu_custom_call" | custom-call | flops 3221225472 | bytes 7864320 | tf_op jit(solution)/shard_map/middle/pallas_call | solution.py:269
  80.7 87.2 %experts.1 = (bf16[1280,768]{1,0:T(8,128)(2,1)}, bf16[1280,768]{1,0:T(8,128)(2,1)}, bf16[768,3072]{1,0:T(8,128)(2,1)}, bf16[768,3072]{1,0:T(8,128)(2,1)}, f32[768,128]{1,0:T(8,128)}, /*index=5*/bf16[768,1536]{1,0:T(8,128)(2,1)}) custom-call(bf16[1280,768]{1,0:T(8,128)(2,1)} %get-tuple-element.48.xs, bf16[1280,768]{1,0:T(8,128)(2,1)} %get-tuple-element.49.gr_h, ...), custom_call_target="tpu_custom_call" | custom-call | flops 36238786560 | bytes 18874368 | tf_op jit(solution)/shard_map/experts/pallas_call | solution.py:709
  167.9 1.0 slice_bitcast_fusion.4
  168.9 0.1 copy.27
  169.0 13.0 %combine.1 = (f32[1024,768]{1,0:T(8,128)}, bf16[768,768]{1,0:T(8,128)(2,1)}, bf16[1024,768]{1,0:T(8,128)(2,1)}, f32[1,768]{1,0:T(1,128)}) custom-call(bf16[1280,768]{1,0:T(8,128)(2,1)} %get-tuple-element.50.gback, f32[1024,768]{1,0:T(8,128)} %get-tuple-element.51.hid.hid_h, bf16[1024,768]{1,0:T(8,128)(2,1)} %cot.3, f32[2,768]{1,0:T(2,128)} %pad_maximum_fusion.gain, ...), custom_call_target="tpu_custom_call" | custom-call | flops 4429185024 | bytes 12582912 | tf_op jit(solution)/shard_map/combine/pallas_call | solution.py:333
  182.0 0.7 reduce
  182.7 0.7 fusion.2.small_h
  183.4 138.9 %attend_back.1 = (bf16[4,768,768]{2,1,0:T(8,128)(2,1)}, f32[1024,768]{1,0:T(8,128)}, f32[96,128]{1,0:T(8,128)}, bf16[2,192,3072]{2,1,0:T(8,128)(2,1)}, bf16[1024,768]{1,0:T(8,128)(2,1)}) custom-call(bf16[1024,768]{1,0:T(8,128)(2,1)} %get-tuple-element.41.q_ref, bf16[1024,768]{1,0:T(8,128)(2,1)} %get-tuple-element.42.k_ref, ...), custom_call_target="tpu_custom_call" | custom-call | flops 39460012032 | bytes 31457280 | tf_op jit(solution)/shard_map/attend_back/pallas_call | solution.py:1315
  322.3 1.3 slice_bitcast_fusion.5
  323.5 0.7 slice.38
  324.3 0.7 slice.41
  325.0 0.7 copy.28
  325.7 0.6 reshape.54
  326.3 0.0 copy-start.2
  326.3 4.5 %convert_bitcast_fusion = (f32[1,3072,192]{1,2,0:T(8,128)}, f32[1,192,3072]{2,1,0:T(8,128)}) fusion(bf16[2,192,3072]{2,1,0:T(8,128)(2,1)} %get-tuple-element.69), kind=kLoop, calls=%fused_computation.4 | loop fusion | flops 1179648 | bytes 7077888 | tf_op jit(solution)/shard_map/broadcast_in_dim | solution.py:1564
  330.8 0.0 copy-done.2
  330.8 0.8 convert_element_type.19
  331.6 0.0 copy-start.4
  331.7 3.8 %slice_bitcast_fusion = (f32[768,768]{1,0:T(8,128)}, f32[768,768]{1,0:T(8,128)}, f32[768,768]{1,0:T(8,128)}, f32[768,768]{1,0:T(8,128)}) fusion(f32[4,768,768]{2,1,0:T(8,128)S(1)} %convert_element_type.19), kind=kLoop, calls=%fused_computation | loop fusion | bytes 18874368 | tf_op jit(solution)/shard_map/squeeze | solution.py:1563
  335.5 0.0 copy-start.3
  335.5 0.0 copy-done.4
  335.5 0.0 copy-start.1
  335.5 1.1 copy.31
  336.6 1.3 copy-done.3
  337.9 1.7 copy.32
  339.6 0.0 copy-done.1
  (3 shorter events, 0.0 us)
Async XLA Ops:
  0.6 2.9 copy-start
  326.3 4.5 %copy-start.2 = (bf16[4,768,768]{2,1,0:T(8,128)(2,1)S(1)}, bf16[4,768,768]{2,1,0:T(8,128)(2,1)}, u32[]{:S(2)}) copy-start(bf16[4,768,768]{2,1,0:T(8,128)(2,1)} %get-tuple-element.67) | copy-start | bytes 14155780
  331.6 3.8 %copy-start.4 = (bf16[1024,768]{1,0:T(8,128)(2,1)S(1)}, bf16[1024,768]{1,0:T(8,128)(2,1)}, u32[]{:S(2)}) copy-start(bf16[1024,768]{1,0:T(8,128)(2,1)} %get-tuple-element.102) | copy-start | bytes 4718596
  335.5 2.5 copy-start.3
  335.5 4.1 %copy-start.1 = (f32[32,12]{0,1:T(8,128)S(1)}, f32[32,12]{0,1:T(8,128)}, u32[]{:S(2)}) copy-start(f32[32,12]{0,1:T(8,128)} %param.20) | copy-start | bytes 4612

commit v9 on v8

--- a/solution.py
+++ b/solution.py
@@ -780,11 +780,11 @@
 
 def back_kernel(
     groups, experts, pairs,
-    q_ref, k_ref, v_ref, g_ref, ctxt_ref, wq, wk, wv, hot, gain, nl_h, tok_h, ghid_h, dwo_h, small_h,
+    q_ref, k_ref, v_ref, g_ref, ctxt_ref, wq, wk, wv, hot, gain, nl_h, tok_h, ghid_h, dwo_h, gain_two, router,
     eout_h, shared_h, ein_h, p_h, prod_h, hid_h, meta,
-    wsum_o, ing_o, small_o, esum_o, out_o,
+    wsum_o, ing_o, small_o, esum_o, out_o, eflip_o,
     acc, vaug, gaug, qz, gz, kt, dqt, pbuf, pret, hbuf, obuf, dall, nt, tok,
-    part, r1, r2, r3, full, sbuf, srecv, sone, stwo, keep, other, final,
+    part, r1, r2, r3, full, sbuf, srecv, sone, stwo, keep, other, final, flip,
     send1, recv1, send2, recv2, send3, recv3, send4, recv4, send5, recv5, send6, recv6, send7, recv7, local,
     send_a, recv_a, send_b, recv_b, out_sem, copy_sem, p_sem, send_p, recv_p, o_sem,
 ):
@@ -935,7 +935,9 @@
         return pltpu.make_async_copy(shared_h, other.at[0], copy_sem.at[4])
 
     def save(which):
-        return pltpu.make_async_copy(final.at[which], esum_o.at[which], copy_sem.at[5])
+        if which == 0:
+            return pltpu.make_async_copy(flip, eflip_o, copy_sem.at[5])
+        return pltpu.make_async_copy(final.at[1], esum_o, copy_sem.at[5])
 
     def experts_begin():
         for copy in own_loads(eout_h) + [shared_load()]:
@@ -977,6 +979,10 @@
 
         lax.fori_loop(0, share // 64, block, 0)
         if which == 0:
+            for side in range(2):
+                cols = slice(middle * side, middle * side + middle)
+                tall = jnp.concatenate([final[0, :, cols], jnp.zeros((256 - share, middle), bf16)], axis=0)
+                flip[cols, :] = tall.T[:, :share]
             for copy in own_loads(ein_h):
                 copy.start()
         else:
@@ -1082,7 +1088,6 @@
         pltpu.make_async_copy(ghid_h, ing_o, local.at[2]),
         pltpu.make_async_copy(dwo_h.at[:, 0:thick], part.at[0], local.at[3]),
         pltpu.make_async_copy(dwo_h.at[:, thick : 2 * thick], part.at[1], local.at[4]),
-        pltpu.make_async_copy(small_h, sbuf, local.at[5]),
     ]
 
     @pl.when(pair == 0)
@@ -1097,6 +1102,15 @@
         load_p(0, 0).start()
         own_back().start()
         load_hidden(0).start()
+        sbuf[...] = jnp.zeros_like(sbuf)
+        first_row = 8 + hot.shape[0]
+        by_expert = router[...].T
+        for tile in range(gain_rows):
+            lanes = slice(128 * tile, 128 * tile + 128)
+            sbuf[first_row + tile : first_row + tile + 1, :] = gain_two[:, lanes]
+            for which in range(experts):
+                row = first_row + 8 + gain_rows * which + tile
+                sbuf[row : row + 1, :] = by_expert[which : which + 1, lanes]
         for copy in loads:
             copy.wait()
         nt[...] = tok[...].T
@@ -1297,12 +1311,13 @@
 
 
 def back_pass(
-    q, k, v, g, ctxt, wq, wk, wv, hot, gain, normed_low, tokens, grad_hidden, dwo, small,
+    q, k, v, g, ctxt, wq, wk, wv, hot, gain, normed_low, tokens, grad_hidden, dwo, gain_two, router,
     expert_out_grad, shared, expert_in_grad, weights, produced, hidden_rows, meta, groups, experts
 ):
     seq, width = q.shape
     pairs = width // 128
     chunks = pairs + 2
+    small_shape = (8 + hot.shape[0] + 8 + width // 128 * experts, 128)
     hidden = expert_in_grad.shape[1]
     thick = width // 2
     half = width // 2
@@ -1320,16 +1335,17 @@
             pl.BlockSpec((128, seq), lambda p: (p, 0)),
             fixed((width, width)), fixed((width, width)), fixed((width, width)),
             fixed(hot.shape), fixed(gain.shape),
-            hbm, hbm, hbm, hbm, hbm, hbm, hbm, hbm,
+            hbm, hbm, hbm, hbm, fixed(gain_two.shape), fixed(router.shape), hbm, hbm, hbm,
             hbm, hbm, hbm, fixed(meta.shape),
         ],
-        out_specs=[hbm, fixed((seq, width)), fixed(small.shape), hbm, hbm],
+        out_specs=[hbm, fixed((seq, width)), fixed(small_shape), hbm, hbm, hbm],
         out_shape=[
             jax.ShapeDtypeStruct((4, width, width), bf16),
             jax.ShapeDtypeStruct((seq, width), f32),
-            jax.ShapeDtypeStruct(small.shape, f32),
-            jax.ShapeDtypeStruct((2, width // 4, hidden), bf16),
+            jax.ShapeDtypeStruct(small_shape, f32),
+            jax.ShapeDtypeStruct((width // 4, hidden), bf16),
             jax.ShapeDtypeStruct((seq, width), bf16),
+            jax.ShapeDtypeStruct((hidden, width // 4), bf16),
         ],
         scratch_shapes=[
             pltpu.VMEM((2, 128, 2 * seq), f32),
@@ -1351,13 +1367,14 @@
             pltpu.VMEM((chunks, groups, piece, thick), bf16),
             pltpu.VMEM((chunks, chips, piece, thick), bf16),
             pltpu.VMEM((chunks, width, thick), bf16),
-            pltpu.VMEM(small.shape, f32),
-            pltpu.VMEM((experts,) + small.shape, f32),
-            pltpu.VMEM(small.shape, f32),
-            pltpu.VMEM((groups,) + small.shape, f32),
+            pltpu.VMEM(small_shape, f32),
+            pltpu.VMEM((experts,) + small_shape, f32),
+            pltpu.VMEM(small_shape, f32),
+            pltpu.VMEM((groups,) + small_shape, f32),
             pltpu.VMEM((width, hidden // 2), bf16),
             pltpu.VMEM((2, width, hidden // 2), bf16),
             pltpu.VMEM((2, width // 4, hidden), bf16),
+            pltpu.VMEM((hidden, width // 4), bf16),
             dma((chunks,)), dma((chunks,)),
             dma((chunks, groups)), dma((chunks, groups)),
             dma((chunks, chips)), dma((chunks, chips)),
@@ -1380,7 +1397,7 @@
         ),
         name="attend_back",
     )(
-        q, k, v, g, ctxt, wq, wk, wv, hot, gain, normed_low, tokens, grad_hidden, dwo, small,
+        q, k, v, g, ctxt, wq, wk, wv, hot, gain, normed_low, tokens, grad_hidden, dwo, gain_two, router,
         expert_out_grad, shared, expert_in_grad, weights, produced, hidden_rows, meta,
     )
 
@@ -1502,7 +1519,6 @@
         grad_rows, produced, in_grad, out_grad_t, router_grad, shared = expert_pass(
             send, grad_recv, weight_in, weight_out, router_pad, experts, capacity
         )
-        router_grad = router_grad[:, :experts]
         grad_hidden, out_w_grad, grad_context, gain_two_grad = combine_pass(
             grad_rows, hidden, cotangent, gains, context, out_w, meta
         )
@@ -1524,16 +1540,10 @@
         grad_context = contract(branch_low, out_w, (1, 1)).astype(bf16)
 
     if kernels:
-        small = jnp.concatenate(
-            [
-                jnp.zeros((8 + rel_table.shape[0], 128), f32),
-                jnp.pad(gain_two_grad.reshape(-1, 128), ((0, 2), (0, 0))),
-                router_grad.T.reshape(-1, 128),
-            ]
-        )
-        grads, input_grad, small, shares, output = back_pass(
+        grads, input_grad, small, in_share, output, out_share = back_pass(
             queries, key_rows, value_rows, grad_context, context_t, query_w, key_w, value_w,
-            bucket_hot, gains, normed_low, tokens, grad_hidden, out_w_grad, small,
+            bucket_hot, gains, normed_low, tokens, grad_hidden, out_w_grad,
+            gain_two_grad, router_grad,
             out_grad_t, shared, in_grad, weights, produced, hidden,
             meta, groups, experts,
         )
@@ -1543,11 +1553,10 @@
         rel_grad = small[8:first, :heads]
         gain_two_grad = small[first : first + tiles].reshape(-1)
         router_grad = small[first + 8 :].reshape(experts, width).T
-        out_share, in_share = shares[0], shares[1]
     else:
         output = (hidden + gate_value * gather_rows(exchange(produced, experts))).astype(bf16)
         in_share = lax.psum_scatter(in_grad, "dp", scatter_dimension=0, tiled=True)
-        out_share = lax.psum_scatter(out_grad_t, "dp", scatter_dimension=0, tiled=True)
+        out_share = lax.psum_scatter(out_grad_t, "dp", scatter_dimension=0, tiled=True).T
         query_grad, key_grad, value_grad, diagonals = attend_back(
             queries, key_rows, value_rows, grad_context, spread, context_t, logsum
         )
@@ -1561,7 +1570,7 @@
     grads = grads.astype(f32)
     return (
         output, input_grad, grads[1], grads[2], grads[3], grads[0], rel_grad,
-        gain_one_grad, gain_two_grad, router_grad, in_share.astype(f32)[None], out_share.astype(f32).T[None],
+        gain_one_grad, gain_two_grad, router_grad, in_share.astype(f32)[None], out_share.astype(f32)[None],
     )
 
 

time: 340 us -> 341 us (level)
    unnamed x14 -> x15, local copies, waits for them, and re-layouts: 5.69 us -> 7.86 us
where the time goes in v9:
time: 341 us
  Pallas kernels  313 us (92%)
  local copies, waits for them, and re-layouts  17.9 us (5%)
  other arithmetic  8.55 us (3%)
    pallas_call x1, Pallas kernels, back_pass(): pl.pallas_call(functools.partial(back_kernel, groups, experts, pairs), gr...  139 us
    pallas_call x1, Pallas kernels, expert_pass(): pl.pallas_call(functools.partial(expert_kernel, experts, capacity, tile),...  87.2 us
    pallas_call x1, Pallas kernels, attend(): pl.pallas_call(functools.partial(attend_kernel, experts), grid=(pairs,),...  52.1 us
    pallas_call x1, Pallas kernels, combine_pass(): pl.pallas_call(combine_kernel, grid=(steps,), in_specs=[fixed(gback.shape...  12.9 us
    pallas_call x1, Pallas kernels, first_pass(): pl.pallas_call(functools.partial(first_kernel, capacity, experts), grid=(...  11 us
    pallas_call x1, Pallas kernels, middle_pass(): pl.pallas_call(functools.partial(middle_kernel, experts, steps), grid=(2...  10.9 us
    unnamed x15, local copies, waits for them, and re-layouts  7.86 us

profile of v9, /device:TPU:1, one launch (start us, length us, event | category | flops | bytes accessed | tf_op | source)
XLA Modules:
  0.0 340.7 jit_solution(9691303107628735148)
XLA Ops:
  0.6 0.0 copy-start
  0.7 0.7 stack.9
  1.4 0.7 stack.10
  2.0 0.6 pad_maximum_fusion.gain
  2.6 0.8 pad_add_fusion
  3.4 0.1 rev.3
  3.5 0.0 copy-done
  3.5 0.2 convolution_bitcast_fusion
  3.7 0.7 reshape.41.u_ref
  4.4 0.9 copy.26
  5.3 0.7 pad.4.rw
  6.0 0.7 fusion.hot
  6.8 11.0 %first.1 = (bf16[1024,768]{1,0:T(8,128)(2,1)}, bf16[1024,768]{1,0:T(8,128)(2,1)}, bf16[1024,768]{1,0:T(8,128)(2,1)}, bf16[1024,768]{1,0:T(8,128)(2,1)}, bf16[128...) custom-call(bf16[1024,768]{1,0:T(8,128)(2,1)} %tok_h.1, f32[2,768]{1,0:T(2,128)} %pad_maximum_fusion.gain, ...), custom_call_target="tpu_custom_call" | custom-call | flops 5637144576 | bytes 15728640 | tf_op jit(solution)/shard_map/first/pallas_call | solution.py:213
  17.8 52.1 %attend.1 = (bf16[1024,768]{1,0:T(8,128)(2,1)}, f32[768,1024]{1,0:T(8,128)}, f32[6,8,1024]{2,1,0:T(8,128)}, bf16[12,1024,1024]{2,1,0:T(8,128)(2,1)}, bf16[1280,768]{1,0:T(8,128)(2,1)}) custom-call(bf16[1024,768]{1,0:T(8,128)(2,1)} %get-tuple-element.42.q_ref, bf16[1024,768]{1,0:T(8,128)(2,1)} %get-tuple-element.43.k_ref, ...), custom_call_target="tpu_custom_call" | custom-call | tf_op jit(solution)/shard_map/attend/pallas_call | solution.py:137
  69.8 10.9 %middle.1 = (f32[1024,768]{1,0:T(8,128)}, bf16[1280,768]{1,0:T(8,128)(2,1)}, f32[1024,128]{1,0:T(8,128)}) custom-call(bf16[1024,768]{1,0:T(8,128)(2,1)} %tok_h.1, bf16[1024,768]{1,0:T(8,128)(2,1)} %get-tuple-element.46.ctx, bf16[768,768]{1,0:T(8,128)(2,1)} %wo.3, f32[2,768]{1,0:T(2,128)} %pad_maximum_fusion.gain, bf16[768,128]{1,0:T(8,128)(2,1)} %pad.4.rw, ...), custom_call_target="tpu_custom_call" | custom-call | flops 3221225472 | bytes 7864320 | tf_op jit(solution)/shard_map/middle/pallas_call | solution.py:269
  80.7 87.2 %experts.1 = (bf16[1280,768]{1,0:T(8,128)(2,1)}, bf16[1280,768]{1,0:T(8,128)(2,1)}, bf16[768,3072]{1,0:T(8,128)(2,1)}, bf16[768,3072]{1,0:T(8,128)(2,1)}, f32[768,128]{1,0:T(8,128)}, /*index=5*/bf16[768,1536]{1,0:T(8,128)(2,1)}) custom-call(bf16[1280,768]{1,0:T(8,128)(2,1)} %get-tuple-element.49.xs, bf16[1280,768]{1,0:T(8,128)(2,1)} %get-tuple-element.50.gr_h, ...), custom_call_target="tpu_custom_call" | custom-call | flops 36238786560 | bytes 18874368 | tf_op jit(solution)/shard_map/experts/pallas_call | solution.py:709
  167.9 12.9 %combine.1 = (f32[1024,768]{1,0:T(8,128)}, bf16[768,768]{1,0:T(8,128)(2,1)}, bf16[1024,768]{1,0:T(8,128)(2,1)}, f32[1,768]{1,0:T(1,128)}) custom-call(bf16[1280,768]{1,0:T(8,128)(2,1)} %get-tuple-element.51.gback, f32[1024,768]{1,0:T(8,128)} %get-tuple-element.52.hid.hid_h, bf16[1024,768]{1,0:T(8,128)(2,1)} %cot.3, f32[2,768]{1,0:T(2,128)} %pad_maximum_fusion.gain, ...), custom_call_target="tpu_custom_call" | custom-call | flops 4429185024 | bytes 12582912 | tf_op jit(solution)/shard_map/combine/pallas_call | solution.py:333
  180.8 139.2 %attend_back.1 = (bf16[4,768,768]{2,1,0:T(8,128)(2,1)}, f32[1024,768]{1,0:T(8,128)}, f32[96,128]{1,0:T(8,128)}, bf16[192,3072]{1,0:T(8,128)(2,1)}, bf16[1024,768]{1,0:T(8,128)(2,1)}, /*index=5*/bf16[3072,192]{1,0:T(8,128)(2,1)}) custom-call(bf16[1024,768]{1,0:T(8,128)(2,1)} %get-tuple-element.42.q_ref, bf16[1024,768]{1,0:T(8,128)(2,1)} %get-tuple-element.43.k_ref, ...), custom_call_target="tpu_custom_call" | custom-call | flops 39460012032 | bytes 31457280 | tf_op jit(solution)/shard_map/attend_back/pallas_call | solution.py:1330
  320.1 1.3 slice_bitcast_fusion.4
  321.4 0.7 slice.28
  322.1 0.7 slice.31
  322.8 0.7 copy.27
  323.5 0.6 reshape.44
  324.1 0.0 copy-start.4
  324.1 3.1 bitcast_convert_fusion.1
  327.2 0.0 copy-done.4
  327.2 0.2 bitcast_convert_fusion
  327.4 2.2 copy.28
  329.6 3.2 convert_element_type.11
  332.7 0.0 copy-start.3
  332.7 3.8 %slice_bitcast_fusion = (f32[768,768]{1,0:T(8,128)}, f32[768,768]{1,0:T(8,128)}, f32[768,768]{1,0:T(8,128)}, f32[768,768]{1,0:T(8,128)}) fusion(f32[4,768,768]{2,1,0:T(8,128)S(1)} %convert_element_type.11), kind=kLoop, calls=%fused_computation | loop fusion | bytes 18874368 | tf_op jit(solution)/shard_map/squeeze | solution.py:1572
  336.6 0.0 copy-start.2
  336.6 0.0 copy-done.3
  336.6 0.0 copy-start.1
  336.6 1.1 copy.31
  337.7 1.3 copy-done.2
  339.0 1.7 copy.32
  340.7 0.0 copy-done.1
Async XLA Ops:
  0.6 2.9 copy-start
  324.1 3.1 copy-start.4
  332.7 3.8 %copy-start.3 = (bf16[1024,768]{1,0:T(8,128)(2,1)S(1)}, bf16[1024,768]{1,0:T(8,128)(2,1)}, u32[]{:S(2)}) copy-start(bf16[1024,768]{1,0:T(8,128)(2,1)} %get-tuple-element.102) | copy-start | bytes 4718596
  336.6 2.5 copy-start.2
  336.6 4.1 %copy-start.1 = (f32[32,12]{0,1:T(8,128)S(1)}, f32[32,12]{0,1:T(8,128)}, u32[]{:S(2)}) copy-start(f32[32,12]{0,1:T(8,128)} %param.20) | copy-start | bytes 4612

commit v10 on v9

--- a/solution.py
+++ b/solution.py
@@ -782,9 +782,9 @@
     groups, experts, pairs,
     q_ref, k_ref, v_ref, g_ref, ctxt_ref, wq, wk, wv, hot, gain, nl_h, tok_h, ghid_h, dwo_h, gain_two, router,
     eout_h, shared_h, ein_h, p_h, prod_h, hid_h, meta,
-    wsum_o, ing_o, small_o, esum_o, out_o, eflip_o,
+    wsum_o, ing_o, small_o, esum_o, out_o,
     acc, vaug, gaug, qz, gz, kt, dqt, pbuf, pret, hbuf, obuf, dall, nt, tok,
-    part, r1, r2, r3, full, sbuf, srecv, sone, stwo, keep, other, final, flip,
+    part, r1, r2, r3, full, sbuf, srecv, sone, stwo, keep, other, final,
     send1, recv1, send2, recv2, send3, recv3, send4, recv4, send5, recv5, send6, recv6, send7, recv7, local,
     send_a, recv_a, send_b, recv_b, out_sem, copy_sem, p_sem, send_p, recv_p, o_sem,
 ):
@@ -935,9 +935,7 @@
         return pltpu.make_async_copy(shared_h, other.at[0], copy_sem.at[4])
 
     def save(which):
-        if which == 0:
-            return pltpu.make_async_copy(flip, eflip_o, copy_sem.at[5])
-        return pltpu.make_async_copy(final.at[1], esum_o, copy_sem.at[5])
+        return pltpu.make_async_copy(final.at[which], esum_o.at[which], copy_sem.at[5])
 
     def experts_begin():
         for copy in own_loads(eout_h) + [shared_load()]:
@@ -979,10 +977,6 @@
 
         lax.fori_loop(0, share // 64, block, 0)
         if which == 0:
-            for side in range(2):
-                cols = slice(middle * side, middle * side + middle)
-                tall = jnp.concatenate([final[0, :, cols], jnp.zeros((256 - share, middle), bf16)], axis=0)
-                flip[cols, :] = tall.T[:, :share]
             for copy in own_loads(ein_h):
                 copy.start()
         else:
@@ -1338,14 +1332,13 @@
             hbm, hbm, hbm, hbm, fixed(gain_two.shape), fixed(router.shape), hbm, hbm, hbm,
             hbm, hbm, hbm, fixed(meta.shape),
         ],
-        out_specs=[hbm, fixed((seq, width)), fixed(small_shape), hbm, hbm, hbm],
+        out_specs=[hbm, fixed((seq, width)), fixed(small_shape), hbm, hbm],
         out_shape=[
             jax.ShapeDtypeStruct((4, width, width), bf16),
             jax.ShapeDtypeStruct((seq, width), f32),
             jax.ShapeDtypeStruct(small_shape, f32),
-            jax.ShapeDtypeStruct((width // 4, hidden), bf16),
+            jax.ShapeDtypeStruct((2, width // 4, hidden), bf16),
             jax.ShapeDtypeStruct((seq, width), bf16),
-            jax.ShapeDtypeStruct((hidden, width // 4), bf16),
         ],
         scratch_shapes=[
             pltpu.VMEM((2, 128, 2 * seq), f32),
@@ -1374,7 +1367,6 @@
             pltpu.VMEM((width, hidden // 2), bf16),
             pltpu.VMEM((2, width, hidden // 2), bf16),
             pltpu.VMEM((2, width // 4, hidden), bf16),
-            pltpu.VMEM((hidden, width // 4), bf16),
             dma((chunks,)), dma((chunks,)),
             dma((chunks, groups)), dma((chunks, groups)),
             dma((chunks, chips)), dma((chunks, chips)),
@@ -1540,7 +1532,7 @@
         grad_context = contract(branch_low, out_w, (1, 1)).astype(bf16)
 
     if kernels:
-        grads, input_grad, small, in_share, output, out_share = back_pass(
+        grads, input_grad, small, shares, output = back_pass(
             queries, key_rows, value_rows, grad_context, context_t, query_w, key_w, value_w,
             bucket_hot, gains, normed_low, tokens, grad_hidden, out_w_grad,
             gain_two_grad, router_grad,
@@ -1553,10 +1545,11 @@
         rel_grad = small[8:first, :heads]
         gain_two_grad = small[first : first + tiles].reshape(-1)
         router_grad = small[first + 8 :].reshape(experts, width).T
+        out_share, in_share = shares[0], shares[1]
     else:
         output = (hidden + gate_value * gather_rows(exchange(produced, experts))).astype(bf16)
         in_share = lax.psum_scatter(in_grad, "dp", scatter_dimension=0, tiled=True)
-        out_share = lax.psum_scatter(out_grad_t, "dp", scatter_dimension=0, tiled=True).T
+        out_share = lax.psum_scatter(out_grad_t, "dp", scatter_dimension=0, tiled=True)
         query_grad, key_grad, value_grad, diagonals = attend_back(
             queries, key_rows, value_rows, grad_context, spread, context_t, logsum
         )
@@ -1570,7 +1563,7 @@
     grads = grads.astype(f32)
     return (
         output, input_grad, grads[1], grads[2], grads[3], grads[0], rel_grad,
-        gain_one_grad, gain_two_grad, router_grad, in_share.astype(f32)[None], out_share.astype(f32)[None],
+        gain_one_grad, gain_two_grad, router_grad, in_share.astype(f32)[None], out_share.astype(f32).T[None],
     )
 
 

time: 341 us -> 338 us (level)
    unnamed x15 -> x14, local copies, waits for them, and re-layouts: 7.86 us -> 5.69 us
where the time goes in v10:
time: 338 us; the launch traced here: 337 us
  Pallas kernels  313 us (93%)
  local copies, waits for them, and re-layouts  15.8 us (5%)
  other arithmetic  7.42 us (2%)
    pallas_call x1, Pallas kernels, back_pass(): pl.pallas_call(functools.partial(back_kernel, groups, experts, pairs), gr...  139 us
    pallas_call x1, Pallas kernels, expert_pass(): pl.pallas_call(functools.partial(expert_kernel, experts, capacity, tile),...  87.2 us
    pallas_call x1, Pallas kernels, attend(): pl.pallas_call(functools.partial(attend_kernel, experts), grid=(pairs,),...  52.1 us
    pallas_call x1, Pallas kernels, combine_pass(): pl.pallas_call(combine_kernel, grid=(steps,), in_specs=[fixed(gback.shape...  13 us
    pallas_call x1, Pallas kernels, first_pass(): pl.pallas_call(functools.partial(first_kernel, capacity, experts), grid=(...  11 us
    pallas_call x1, Pallas kernels, middle_pass(): pl.pallas_call(functools.partial(middle_kernel, experts, steps), grid=(2...  10.8 us

profile of v10, /device:TPU:1, one launch (start us, length us, event | category | flops | bytes accessed | tf_op | source)
XLA Modules:
  0.0 337.4 jit_solution(18043401023192557203)
XLA Ops:
  0.6 0.0 copy-start
  0.7 0.7 stack.9
  1.4 0.7 stack.10
  2.0 0.6 pad_maximum_fusion.gain
  2.6 0.8 pad_add_fusion
  3.4 0.1 rev.3
  3.5 0.0 copy-done
  3.5 0.2 convolution_bitcast_fusion
  3.7 0.7 reshape.43.u_ref
  4.4 0.9 copy.26
  5.3 0.7 pad.4.rw
  6.0 0.7 fusion.hot
  6.7 11.0 %first.1 = (bf16[1024,768]{1,0:T(8,128)(2,1)}, bf16[1024,768]{1,0:T(8,128)(2,1)}, bf16[1024,768]{1,0:T(8,128)(2,1)}, bf16[1024,768]{1,0:T(8,128)(2,1)}, bf16[128...) custom-call(bf16[1024,768]{1,0:T(8,128)(2,1)} %tok_h.1, f32[2,768]{1,0:T(2,128)} %pad_maximum_fusion.gain, ...), custom_call_target="tpu_custom_call" | custom-call | flops 5637144576 | bytes 15728640 | tf_op jit(solution)/shard_map/first/pallas_call | solution.py:213
  17.7 52.1 %attend.1 = (bf16[1024,768]{1,0:T(8,128)(2,1)}, f32[768,1024]{1,0:T(8,128)}, f32[6,8,1024]{2,1,0:T(8,128)}, bf16[12,1024,1024]{2,1,0:T(8,128)(2,1)}, bf16[1280,768]{1,0:T(8,128)(2,1)}) custom-call(bf16[1024,768]{1,0:T(8,128)(2,1)} %get-tuple-element.41.q_ref, bf16[1024,768]{1,0:T(8,128)(2,1)} %get-tuple-element.42.k_ref, ...), custom_call_target="tpu_custom_call" | custom-call | tf_op jit(solution)/shard_map/attend/pallas_call | solution.py:137
  69.8 10.8 %middle.1 = (f32[1024,768]{1,0:T(8,128)}, bf16[1280,768]{1,0:T(8,128)(2,1)}, f32[1024,128]{1,0:T(8,128)}) custom-call(bf16[1024,768]{1,0:T(8,128)(2,1)} %tok_h.1, bf16[1024,768]{1,0:T(8,128)(2,1)} %get-tuple-element.45.ctx, bf16[768,768]{1,0:T(8,128)(2,1)} %wo.3, f32[2,768]{1,0:T(2,128)} %pad_maximum_fusion.gain, bf16[768,128]{1,0:T(8,128)(2,1)} %pad.4.rw, ...), custom_call_target="tpu_custom_call" | custom-call | flops 3221225472 | bytes 7864320 | tf_op jit(solution)/shard_map/middle/pallas_call | solution.py:269
  80.7 87.2 %experts.1 = (bf16[1280,768]{1,0:T(8,128)(2,1)}, bf16[1280,768]{1,0:T(8,128)(2,1)}, bf16[768,3072]{1,0:T(8,128)(2,1)}, bf16[768,3072]{1,0:T(8,128)(2,1)}, f32[768,128]{1,0:T(8,128)}, /*index=5*/bf16[768,1536]{1,0:T(8,128)(2,1)}) custom-call(bf16[1280,768]{1,0:T(8,128)(2,1)} %get-tuple-element.48.xs, bf16[1280,768]{1,0:T(8,128)(2,1)} %get-tuple-element.49.gr_h, ...), custom_call_target="tpu_custom_call" | custom-call | flops 36238786560 | bytes 18874368 | tf_op jit(solution)/shard_map/experts/pallas_call | solution.py:709
  167.9 13.0 %combine.1 = (f32[1024,768]{1,0:T(8,128)}, bf16[768,768]{1,0:T(8,128)(2,1)}, bf16[1024,768]{1,0:T(8,128)(2,1)}, f32[1,768]{1,0:T(1,128)}) custom-call(bf16[1280,768]{1,0:T(8,128)(2,1)} %get-tuple-element.50.gback, f32[1024,768]{1,0:T(8,128)} %get-tuple-element.51.hid.hid_h, bf16[1024,768]{1,0:T(8,128)(2,1)} %cot.3, f32[2,768]{1,0:T(2,128)} %pad_maximum_fusion.gain, ...), custom_call_target="tpu_custom_call" | custom-call | flops 4429185024 | bytes 12582912 | tf_op jit(solution)/shard_map/combine/pallas_call | solution.py:333
  180.8 139.2 %attend_back.1 = (bf16[4,768,768]{2,1,0:T(8,128)(2,1)}, f32[1024,768]{1,0:T(8,128)}, f32[96,128]{1,0:T(8,128)}, bf16[2,192,3072]{2,1,0:T(8,128)(2,1)}, bf16[1024,768]{1,0:T(8,128)(2,1)}) custom-call(bf16[1024,768]{1,0:T(8,128)(2,1)} %get-tuple-element.41.q_ref, bf16[1024,768]{1,0:T(8,128)(2,1)} %get-tuple-element.42.k_ref, ...), custom_call_target="tpu_custom_call" | custom-call | flops 39460012032 | bytes 31457280 | tf_op jit(solution)/shard_map/attend_back/pallas_call | solution.py:1324
  320.0 1.3 slice_bitcast_fusion.4
  321.3 0.7 slice.34
  322.0 0.7 slice.37
  322.8 0.7 copy.27
  323.5 0.6 reshape.46
  324.1 0.0 copy-start.2
  324.1 4.5 %convert_bitcast_fusion = (f32[1,3072,192]{1,2,0:T(8,128)}, f32[1,192,3072]{2,1,0:T(8,128)}) fusion(bf16[2,192,3072]{2,1,0:T(8,128)(2,1)} %get-tuple-element.69), kind=kLoop, calls=%fused_computation.4 | loop fusion | flops 1179648 | bytes 7077888 | tf_op jit(solution)/shard_map/broadcast_in_dim | solution.py:1566
  328.6 0.0 copy-done.2
  328.6 0.8 convert_element_type.17
  329.4 0.0 copy-start.4
  329.4 3.8 %slice_bitcast_fusion = (f32[768,768]{1,0:T(8,128)}, f32[768,768]{1,0:T(8,128)}, f32[768,768]{1,0:T(8,128)}, f32[768,768]{1,0:T(8,128)}) fusion(f32[4,768,768]{2,1,0:T(8,128)S(1)} %convert_element_type.17), kind=kLoop, calls=%fused_computation | loop fusion | bytes 18874368 | tf_op jit(solution)/shard_map/squeeze | solution.py:1565
  333.3 0.0 copy-start.3
  333.3 0.0 copy-done.4
  333.3 0.0 copy-start.1
  333.3 1.1 copy.30
  334.4 1.3 copy-done.3
  335.7 1.7 copy.31
  337.4 0.0 copy-done.1
Async XLA Ops:
  0.6 2.9 copy-start
  324.1 4.5 %copy-start.2 = (bf16[4,768,768]{2,1,0:T(8,128)(2,1)S(1)}, bf16[4,768,768]{2,1,0:T(8,128)(2,1)}, u32[]{:S(2)}) copy-start(bf16[4,768,768]{2,1,0:T(8,128)(2,1)} %get-tuple-element.67) | copy-start | bytes 14155780
  329.4 3.8 %copy-start.4 = (bf16[1024,768]{1,0:T(8,128)(2,1)S(1)}, bf16[1024,768]{1,0:T(8,128)(2,1)}, u32[]{:S(2)}) copy-start(bf16[1024,768]{1,0:T(8,128)(2,1)} %get-tuple-element.102) | copy-start | bytes 4718596
  333.3 2.5 copy-start.3
  333.3 4.1 %copy-start.1 = (f32[32,12]{0,1:T(8,128)S(1)}, f32[32,12]{0,1:T(8,128)}, u32[]{:S(2)}) copy-start(f32[32,12]{0,1:T(8,128)} %param.20) | copy-start | bytes 4612

commit v11 on v10

--- a/solution.py
+++ b/solution.py
@@ -619,9 +619,7 @@
     ]
     for copy in outs:
         copy.start()
-    xt[...] = xall[...].T
     gpt[...] = gp[...].T
-    drw_o[...] = dot_f32(xt[...], logit[...])
 
     share = width // 4
     tiles = hidden // tile
@@ -664,6 +662,8 @@
     lax.fori_loop(0, tiles, out_block, 0)
     whole = pltpu.make_async_copy(dwt, dwout_o, local.at[2])
     whole.start()
+    xt[...] = xall[...].T
+    drw_o[...] = dot_f32(xt[...], logit[...])
 
     def put(slot, cols):
         return pltpu.make_async_copy(stage.at[slot], dwin_o.at[:, cols], out_sem.at[slot])

time: 338 us -> 338 us (level)
  no operation moved by 1% of the time
where the time goes in v11:
time: 338 us; the launch traced here: 337 us
  Pallas kernels  313 us (93%)
  local copies, waits for them, and re-layouts  15.8 us (5%)
  other arithmetic  7.42 us (2%)
    pallas_call x1, Pallas kernels, back_pass(): pl.pallas_call(functools.partial(back_kernel, groups, experts, pairs), gr...  140 us
    pallas_call x1, Pallas kernels, expert_pass(): pl.pallas_call(functools.partial(expert_kernel, experts, capacity, tile),...  86.7 us
    pallas_call x1, Pallas kernels, attend(): pl.pallas_call(functools.partial(attend_kernel, experts), grid=(pairs,),...  52.1 us
    pallas_call x1, Pallas kernels, combine_pass(): pl.pallas_call(combine_kernel, grid=(steps,), in_specs=[fixed(gback.shape...  13 us
    pallas_call x1, Pallas kernels, first_pass(): pl.pallas_call(functools.partial(first_kernel, capacity, experts), grid=(...  11 us
    pallas_call x1, Pallas kernels, middle_pass(): pl.pallas_call(functools.partial(middle_kernel, experts, steps), grid=(2...  10.8 us

profile of v11, /device:TPU:1, one launch (start us, length us, event | category | flops | bytes accessed | tf_op | source)
XLA Modules:
  0.0 337.4 jit_solution(17608819859534922226)
XLA Ops:
  0.6 0.0 copy-start
  0.7 0.7 stack.9
  1.4 0.7 stack.10
  2.0 0.6 pad_maximum_fusion.gain
  2.6 0.8 pad_add_fusion
  3.4 0.1 rev.3
  3.5 0.0 copy-done
  3.5 0.2 convolution_bitcast_fusion
  3.7 0.7 reshape.43.u_ref
  4.4 0.9 copy.26
  5.3 0.7 pad.4.rw
  6.0 0.7 fusion.hot
  6.7 11.0 %first.1 = (bf16[1024,768]{1,0:T(8,128)(2,1)}, bf16[1024,768]{1,0:T(8,128)(2,1)}, bf16[1024,768]{1,0:T(8,128)(2,1)}, bf16[1024,768]{1,0:T(8,128)(2,1)}, bf16[128...) custom-call(bf16[1024,768]{1,0:T(8,128)(2,1)} %tok_h.1, f32[2,768]{1,0:T(2,128)} %pad_maximum_fusion.gain, ...), custom_call_target="tpu_custom_call" | custom-call | flops 5637144576 | bytes 15728640 | tf_op jit(solution)/shard_map/first/pallas_call | solution.py:213
  17.7 52.1 %attend.1 = (bf16[1024,768]{1,0:T(8,128)(2,1)}, f32[768,1024]{1,0:T(8,128)}, f32[6,8,1024]{2,1,0:T(8,128)}, bf16[12,1024,1024]{2,1,0:T(8,128)(2,1)}, bf16[1280,768]{1,0:T(8,128)(2,1)}) custom-call(bf16[1024,768]{1,0:T(8,128)(2,1)} %get-tuple-element.41.q_ref, bf16[1024,768]{1,0:T(8,128)(2,1)} %get-tuple-element.42.k_ref, ...), custom_call_target="tpu_custom_call" | custom-call | tf_op jit(solution)/shard_map/attend/pallas_call | solution.py:137
  69.8 10.8 %middle.1 = (f32[1024,768]{1,0:T(8,128)}, bf16[1280,768]{1,0:T(8,128)(2,1)}, f32[1024,128]{1,0:T(8,128)}) custom-call(bf16[1024,768]{1,0:T(8,128)(2,1)} %tok_h.1, bf16[1024,768]{1,0:T(8,128)(2,1)} %get-tuple-element.45.ctx, bf16[768,768]{1,0:T(8,128)(2,1)} %wo.3, f32[2,768]{1,0:T(2,128)} %pad_maximum_fusion.gain, bf16[768,128]{1,0:T(8,128)(2,1)} %pad.4.rw, ...), custom_call_target="tpu_custom_call" | custom-call | flops 3221225472 | bytes 7864320 | tf_op jit(solution)/shard_map/middle/pallas_call | solution.py:269
  80.7 86.7 %experts.1 = (bf16[1280,768]{1,0:T(8,128)(2,1)}, bf16[1280,768]{1,0:T(8,128)(2,1)}, bf16[768,3072]{1,0:T(8,128)(2,1)}, bf16[768,3072]{1,0:T(8,128)(2,1)}, f32[768,128]{1,0:T(8,128)}, /*index=5*/bf16[768,1536]{1,0:T(8,128)(2,1)}) custom-call(bf16[1280,768]{1,0:T(8,128)(2,1)} %get-tuple-element.48.xs, bf16[1280,768]{1,0:T(8,128)(2,1)} %get-tuple-element.49.gr_h, ...), custom_call_target="tpu_custom_call" | custom-call | flops 36238786560 | bytes 18874368 | tf_op jit(solution)/shard_map/experts/pallas_call | solution.py:709
  167.3 13.0 %combine.1 = (f32[1024,768]{1,0:T(8,128)}, bf16[768,768]{1,0:T(8,128)(2,1)}, bf16[1024,768]{1,0:T(8,128)(2,1)}, f32[1,768]{1,0:T(1,128)}) custom-call(bf16[1280,768]{1,0:T(8,128)(2,1)} %get-tuple-element.50.gback, f32[1024,768]{1,0:T(8,128)} %get-tuple-element.51.hid.hid_h, bf16[1024,768]{1,0:T(8,128)(2,1)} %cot.3, f32[2,768]{1,0:T(2,128)} %pad_maximum_fusion.gain, ...), custom_call_target="tpu_custom_call" | custom-call | flops 4429185024 | bytes 12582912 | tf_op jit(solution)/shard_map/combine/pallas_call | solution.py:333
  180.3 139.7 %attend_back.1 = (bf16[4,768,768]{2,1,0:T(8,128)(2,1)}, f32[1024,768]{1,0:T(8,128)}, f32[96,128]{1,0:T(8,128)}, bf16[2,192,3072]{2,1,0:T(8,128)(2,1)}, bf16[1024,768]{1,0:T(8,128)(2,1)}) custom-call(bf16[1024,768]{1,0:T(8,128)(2,1)} %get-tuple-element.41.q_ref, bf16[1024,768]{1,0:T(8,128)(2,1)} %get-tuple-element.42.k_ref, ...), custom_call_target="tpu_custom_call" | custom-call | flops 39460012032 | bytes 31457280 | tf_op jit(solution)/shard_map/attend_back/pallas_call | solution.py:1324
  320.0 1.3 slice_bitcast_fusion.4
  321.3 0.7 slice.34
  322.0 0.7 slice.37
  322.8 0.7 copy.27
  323.5 0.6 reshape.46
  324.1 0.0 copy-start.2
  324.1 4.5 %convert_bitcast_fusion = (f32[1,3072,192]{1,2,0:T(8,128)}, f32[1,192,3072]{2,1,0:T(8,128)}) fusion(bf16[2,192,3072]{2,1,0:T(8,128)(2,1)} %get-tuple-element.69), kind=kLoop, calls=%fused_computation.4 | loop fusion | flops 1179648 | bytes 7077888 | tf_op jit(solution)/shard_map/broadcast_in_dim | solution.py:1566
  328.6 0.0 copy-done.2
  328.6 0.8 convert_element_type.17
  329.4 0.0 copy-start.4
  329.4 3.8 %slice_bitcast_fusion = (f32[768,768]{1,0:T(8,128)}, f32[768,768]{1,0:T(8,128)}, f32[768,768]{1,0:T(8,128)}, f32[768,768]{1,0:T(8,128)}) fusion(f32[4,768,768]{2,1,0:T(8,128)S(1)} %convert_element_type.17), kind=kLoop, calls=%fused_computation | loop fusion | bytes 18874368 | tf_op jit(solution)/shard_map/squeeze | solution.py:1565
  333.3 0.0 copy-start.3
  333.3 0.0 copy-done.4
  333.3 0.0 copy-start.1
  333.3 1.1 copy.30
  334.4 1.3 copy-done.3
  335.7 1.7 copy.31
  337.4 0.0 copy-done.1
Async XLA Ops:
  0.6 2.9 copy-start
  324.1 4.5 %copy-start.2 = (bf16[4,768,768]{2,1,0:T(8,128)(2,1)S(1)}, bf16[4,768,768]{2,1,0:T(8,128)(2,1)}, u32[]{:S(2)}) copy-start(bf16[4,768,768]{2,1,0:T(8,128)(2,1)} %get-tuple-element.67) | copy-start | bytes 14155780
  329.4 3.8 %copy-start.4 = (bf16[1024,768]{1,0:T(8,128)(2,1)S(1)}, bf16[1024,768]{1,0:T(8,128)(2,1)}, u32[]{:S(2)}) copy-start(bf16[1024,768]{1,0:T(8,128)(2,1)} %get-tuple-element.102) | copy-start | bytes 4718596
  333.3 2.5 copy-start.3
  333.3 4.1 %copy-start.1 = (f32[32,12]{0,1:T(8,128)S(1)}, f32[32,12]{0,1:T(8,128)}, u32[]{:S(2)}) copy-start(f32[32,12]{0,1:T(8,128)} %param.20) | copy-start | bytes 4612
